TPU v7x, 128 devices: a whole 4x4x4 slice. The times are simulated.
128 devices in a mesh: group: 4 (over x), img: 32 (over z, y, core).
Axes of the slice: x: 4, y: 4, z: 4, core: 2. Of those that a mesh axis runs over, the one named last changes fastest.
Arguments:
- enc_tokens: bfloat16 [128, 768, 1024], P(('group', 'img')), may hold values from -6 to 6
- embed_weight: bfloat16 [1024, 768], replicated, may hold values from -0.1875 to 0.1875
- embed_bias: float32 [768], replicated, may hold values from -3 to 3
- query_gain: float32 [768], replicated, may hold values from 0.25 to 1.75
- memory_gain: float32 [768], replicated, may hold values from 0.25 to 1.75
- query_weight: bfloat16 [768, 768], replicated, may hold values from -0.43164062 to 0.43164062
- key_weight: bfloat16 [768, 768], replicated, may hold values from -0.21875 to 0.21875
- value_weight: bfloat16 [768, 768], replicated, may hold values from -0.21875 to 0.21875
- out_weight: bfloat16 [768, 768], replicated, may hold values from -0.43164062 to 0.43164062
- head_weight: bfloat16 [768, 512], replicated, may hold values from -0.21875 to 0.21875
- pair_dst: int32 [512], P(('group', 'img')), may hold values from 0 to 127, as said below
- pair_count: int32 [128], P(('group', 'img')), may hold values from 3 to 4, as said below
- depth: float32 [128, 768, 256], P(('group', 'img')), may hold values from -3 to 3
- scale: float32 [128], replicated, may hold values from -3 to 3
- focal: float32 [128], replicated, may hold values from -3 to 3
Outputs:
- pair_tokens: bfloat16 [512, 768, 768], P(('group', 'img'))
- depth_out: float32 [128, 768, 256], P(('group', 'img'))
- scale_out: float32 [128], replicated
- focal_out: float32 [128], replicated
Inputs may be any that keep to these rules, and one draw needn't show every extreme that they name: `pair_dst`: each slot of the device at (group g, img j) names an image owned by the device at (g, j - 1), (g, j + 1), or (g - 1 wrapped over the group axis, j). The live slots of a device are its first pair_count slots.
All inputs are finite; a program needn't handle non-finite values.
Results may differ from a plain program's by a relative error of at most 0.008.
Values may be sent and summed in bfloat16 or wider, within the bound.
No kernel may reach another device: no remote copies, remote signals or barrier semaphores. Data moves between devices by JAX's collectives and lax.ppermute only.
A program may use at most 192 MiB of HBM per device.

v0:
```python
import jax
import jax.numpy as jnp
from jax import lax
from jax.sharding import PartitionSpec as P

HEADS = 12
IMG_DEV = 1
ITERS = 2


STEP_DEPTH = 0.1
STEP_SCALE = 0.1
STEP_FOCAL = 0.1


def padded(cells, sides, width):
    for axis, dim in sides:
        count = lax.axis_size(axis)
        ends = count - 1
        head = lax.slice_in_dim(cells, 0, width, axis=dim)
        tail = lax.slice_in_dim(cells, cells.shape[dim] - width, cells.shape[dim], axis=dim)
        cells = jnp.concatenate(
            [
                lax.ppermute(tail, axis, [(i, (i + 1) % count) for i in range(ends)]),
                cells,
                lax.ppermute(head, axis, [((i + 1) % count, i) for i in range(ends)]),
            ],
            axis=dim,
        )
    return cells


def passed_along(value, axis, steps):
    count = lax.axis_size(axis)
    pairs = [(source, (source + steps) % count) for source in range(count)]
    return lax.ppermute(value, axis, pairs)


def shortened(array):

    def short(part):
        return part.astype(jnp.bfloat16) if part.dtype == jnp.float32 else part

    return jax.tree.map(short, array)


def shifted(array, axis, by):
    length = lax.axis_size(axis)
    pairs = [(i, i + by) for i in range(length) if 0 <= i + by < length]
    return lax.ppermute(array, axis, pairs)


def layer_norm(rows, gain):
    values = rows.astype(jnp.float32)
    center = values - jnp.mean(values, axis=-1, keepdims=True)
    spread = jnp.mean(center * center, axis=-1, keepdims=True)
    return (center * lax.rsqrt(spread + 1e-05) * gain).astype(jnp.bfloat16)


def project_rows(rows, weight):
    return jnp.einsum("nlx,xy->nly", rows, weight, preferred_element_type=jnp.float32)


def embed_rows(tokens, embed_weight, embed_bias):
    return (project_rows(tokens, embed_weight) + embed_bias).astype(jnp.bfloat16)


def memory_rows(embedded, memory_gain, key_weight, value_weight):
    normed = layer_norm(embedded, memory_gain)
    key_rows = project_rows(normed, key_weight).astype(jnp.bfloat16)
    value_rows = project_rows(normed, value_weight).astype(jnp.bfloat16)
    return jnp.stack([key_rows, value_rows], axis=1)


def attend(query, key_rows, value_rows):
    token_count, feat_width = query.shape
    head_size = feat_width // HEADS
    query_heads = query.reshape(token_count, HEADS, head_size)
    key_heads = key_rows.reshape(key_rows.shape[0], HEADS, head_size)
    value_heads = value_rows.reshape(value_rows.shape[0], HEADS, head_size)
    scores = jnp.einsum(
        "qhd,khd->hqk", query_heads, key_heads, preferred_element_type=jnp.float32
    ) * head_size ** (-0.5)
    probs = jax.nn.softmax(scores, axis=-1).astype(jnp.bfloat16)
    mixed = jnp.einsum("hqk,khd->qhd", probs, value_heads, preferred_element_type=jnp.float32)
    return mixed.astype(jnp.bfloat16).reshape(token_count, feat_width)


def local(
    enc_tokens,
    embed_weight,
    embed_bias,
    query_gain,
    memory_gain,
    query_weight,
    key_weight,
    value_weight,
    out_weight,
    head_weight,
    pair_dst,
    pair_count,
    depth,
    scale,
    focal,
):
    img_count = lax.axis_size("img")
    group_index = lax.axis_index("group")
    base = (group_index * img_count + lax.axis_index("img")) * IMG_DEV
    own_embed = embed_rows(enc_tokens, embed_weight, embed_bias)
    near = padded(enc_tokens, (("img", 0),), IMG_DEV)
    far = passed_along(enc_tokens, "group", 1)
    side_tokens = jnp.concatenate([near[:IMG_DEV], near[2 * IMG_DEV :], far], axis=0)
    side_embed = embed_rows(side_tokens, embed_weight, embed_bias)
    pool_embed = jnp.concatenate([side_embed[:IMG_DEV], own_embed, side_embed[IMG_DEV:]], axis=0)
    pool_memory = memory_rows(pool_embed, memory_gain, key_weight, value_weight)
    queries = project_rows(layer_norm(own_embed, query_gain), query_weight).astype(jnp.bfloat16)
    slot_count = pair_dst.shape[0]
    slot_ids = jnp.arange(slot_count, dtype=jnp.int32)
    local_src = slot_ids % IMG_DEV
    global_src = base + local_src
    same_group = pair_dst // IMG_DEV // img_count == group_index
    pool_index = jnp.where(same_group, pair_dst - base + IMG_DEV, 3 * IMG_DEV + pair_dst % IMG_DEV)
    live = slot_ids < pair_count[0]

    def one_pair(index_pair):
        source, target = index_pair
        memory = pool_memory[target]
        mixed = attend(queries[source], memory[0], memory[1])
        attended = jnp.dot(mixed, out_weight, preferred_element_type=jnp.float32)
        tokens_out = (own_embed[source].astype(jnp.float32) + attended).astype(jnp.bfloat16)
        head = jnp.dot(tokens_out, head_weight, preferred_element_type=jnp.float32)
        return (tokens_out, head)

    outs, heads = lax.map(one_pair, (local_src, pool_index))
    patch = heads.shape[-1] // 2
    pair_tokens = jnp.where(live[:, None, None], outs, jnp.zeros_like(outs))
    offset = heads[..., :patch]
    confidence = jnp.where(live[:, None, None], 0.1 + jax.nn.softplus(heads[..., patch:]), 0.0)
    token_count = depth.shape[1]
    pixel_total = token_count * patch
    ramp = (2.0 * (jnp.arange(pixel_total, dtype=jnp.float32) + 0.5) / pixel_total - 1.0).reshape(
        token_count, patch
    )
    src_onehot = (local_src[:, None] == jnp.arange(IMG_DEV, dtype=jnp.int32)[None, :]).astype(
        jnp.float32
    )
    dst_onehot = (pool_index[:, None] == jnp.arange(4 * IMG_DEV, dtype=jnp.int32)[None, :]).astype(
        jnp.float32
    )
    global_ids = jnp.arange(scale.shape[0], dtype=jnp.int32)
    pose_map = (global_src[:, None] == global_ids[None, :]).astype(jnp.float32) - (
        pair_dst[:, None] == global_ids[None, :]
    ).astype(jnp.float32)
    for turn in range(ITERS):
        near_depth = padded(shortened(depth), (("img", 0),), IMG_DEV).astype(depth.dtype)
        far_depth = passed_along(shortened(depth), "group", 1).astype(depth.dtype)
        pool_depth = jnp.concatenate([near_depth, far_depth], axis=0)
        shift_terms = scale[global_src] - scale[pair_dst]
        focal_terms = focal[global_src] - focal[pair_dst]
        resid = (
            depth[local_src]
            - pool_depth[pool_index]
            + shift_terms[:, None, None]
            + focal_terms[:, None, None] * ramp
            - offset
        )
        weighted = confidence * resid
        src_grad = jnp.einsum("ci,clq->ilq", src_onehot, weighted, precision=lax.Precision.HIGHEST)
        dst_grad = jnp.einsum("cp,clq->plq", dst_onehot, weighted, precision=lax.Precision.HIGHEST)
        from_above = shifted(shortened(dst_grad[:IMG_DEV]), "img", -1)
        from_below = shifted(shortened(dst_grad[2 * IMG_DEV : 3 * IMG_DEV]), "img", 1)
        from_cross = passed_along(shortened(dst_grad[3 * IMG_DEV :]), "group", -1)
        depth_grad = (
            src_grad - dst_grad[IMG_DEV : 2 * IMG_DEV] - from_above - from_below - from_cross
        )
        plain = jnp.sum(weighted, axis=(1, 2)) / pixel_total
        slope = jnp.sum(weighted * ramp, axis=(1, 2)) / pixel_total
        terms = jnp.stack([plain, slope], axis=0)
        dense = jnp.dot(terms, pose_map, precision=lax.Precision.HIGHEST)
        totals = lax.psum(dense, ("group", "img"))
        scale = scale - STEP_SCALE * totals[0]
        focal = focal - STEP_FOCAL * totals[1]
        depth = depth - STEP_DEPTH * depth_grad
    return (pair_tokens, depth, scale, focal)


def solution(mesh):
    placed = (
        P(("group", "img"), None, None),
        P(),
        P(),
        P(),
        P(),
        P(),
        P(),
        P(),
        P(),
        P(),
        P(("group", "img")),
        P(("group", "img")),
        P(("group", "img"), None, None),
        P(),
        P(),
    )
    return jax.shard_map(
        local,
        mesh=mesh,
        in_specs=placed,
        out_specs=(P(("group", "img"), None, None), P(("group", "img"), None, None), P(), P()),
        check_vma=False,
    )
```

profile of v0, /device:TPU:6, one launch (start us, length us, event | category | flops | bytes accessed | tf_op | source)
XLA Modules:
  0.0 458.8 jit_solution(5455576251224926062)
XLA Ops:
  33.3 17.5 %collective-permute-done.5 = bf16[1,768,256]{2,1,0:T(8,128)(2,1)} collective-permute-done((bf16[1,768,256]{2,1,0:T(8,128)(2,1)S(1)}, bf16[1,768,256]{2,1,0:T(8,128)(2,1)}, u32[]{:S(2)}, u32[]{:S(2)}) %collective-permute-start.5) | collective-permute-done | bytes 393248 | tf_op jit(solution)/shard_map/ppermute | solution.py:36
  58.2 6.2 %add_convert_fusion = bf16[3,768,768]{1,2,0:T(8,128)(2,1)S(1)} fusion(f32[768]{0:T(1024)S(1)} %copy-done.28, bf16[1,768,1024]{2,1,0:T(8,128)(2,1)} %collective-permute-done.2, bf16[1,768,1024]{2,1,0:T(8,128)(2,1)} %collective-permute-done.1, bf16[1,768,1024]{2,1,0:T(8,128)(2,1)} %collective-permute-done, bf16[1024,768]{1,0:T(8,128)(2,1)S(1)} %copy-done), kind=kOutput, calls=%fused_computation.37 | convolution fusion | flops 3632136192 | bytes 9833472 | tf_op jit(solution)/shard_map/nlx,xy->nly/dot_general | solution.py:61
  66.8 6.0 %convert_bitcast_fusion.1 = bf16[4,1,768,768]{3,2,0,1:T(8,128)(2,1)} fusion(bf16[768,768]{1,0:T(8,128)(2,1)S(1)} %copy-done.24, f32[768]{0:T(1024)S(1)} %copy-done.29, f32[4,768]{1,0:T(4,128)S(1)} %add_rsqrt_fusion, f32[4,768]{1,0:T(4,128)S(1)} %broadcast_multiply_fusion, bf16[2,768,768]{1,2,0:T(8,128)(2,1)S(1)} %slice.101, ...), kind=kOutput, calls=%fused_computation.46 | convolution fusion | flops 3642753024 | bytes 10644480 | tf_op jit(solution)/shard_map/nlx,xy->nly/dot_general | solution.py:61
  72.8 6.2 %convert_bitcast_fusion = bf16[4,1,768,768]{3,2,0,1:T(8,128)(2,1)} fusion(bf16[768,768]{1,0:T(8,128)(2,1)S(1)} %copy-done.25, f32[768]{0:T(1024)S(1)} %copy-done.29, f32[4,768]{1,0:T(4,128)S(1)} %add_rsqrt_fusion, f32[4,768]{1,0:T(4,128)S(1)} %broadcast_multiply_fusion, bf16[2,768,768]{1,2,0:T(8,128)(2,1)S(1)} %slice.101, ...), kind=kOutput, calls=%fused_computation.45 | convolution fusion | flops 3642753024 | bytes 10644480 | tf_op jit(solution)/shard_map/nlx,xy->nly/dot_general | solution.py:61
  79.0 8.3 %pad_maximum_fusion = bf16[4,2,768,768]{3,2,0,1:T(8,128)(2,1)} fusion(bf16[4,1,768,768]{3,2,0,1:T(8,128)(2,1)} %convert_bitcast_fusion, bf16[4,1,768,768]{3,2,0,1:T(8,128)(2,1)} %convert_bitcast_fusion.1), kind=kLoop, calls=%fused_computation.35 | loop fusion | flops 4718592 | bytes 18874368 | tf_op jit(solution)/shard_map/stack | solution.py:72
  89.8 144.6 %while.13 = (s32[]{:T(128)}, bf16[4,768,768]{2,1,0:T(8,128)(2,1)}, f32[4,768,512]{2,1,0:T(8,128)}, bf16[1,768,768]{2,1,0:T(8,128)(2,1)}, s32[4]{0:T(128)S(1)}, /...) while((s32[]{:T(128)}, bf16[4,768,768]{2,1,0:T(8,128)(2,1)}, ...), condition=%wide.region_7.8_spmd, body=%wide.region_4.7_spmd.sunk | while | flops 3359638272 | bytes 92874008 | solution.py:134
  95.6 14.8 %fusion.125 = (f32[12,768]{1,0:T(8,128)S(1)}, f32[12,768,768]{1,2,0:T(8,128)}) fusion(bf16[768,12,64]{0,2,1:T(8,128)(2,1)} %bitcast.119, bf16[768,12,64]{0,2,1:T(8,128)(2,1)} %bitcast.130), kind=kOutput, calls=%fused_computation.147.clone.1 | convolution fusion | flops 927204096 | bytes 30707712 | tf_op jit(solution)/shard_map/while/body/eval_jaxpr/sub | solution.py:84
  111.1 10.8 %fusion.126 = bf16[12,64,768]{2,1,0:T(8,128)(2,1)S(1)} fusion(bf16[768,12,64]{0,2,1:T(8,128)(2,1)S(1)} %bitcast.120, f32[12,768,768]{1,2,0:T(8,128)} %get-tuple-element.240, f32[12,768]{1,0:T(8,128)S(1)} %get-tuple-element.241), kind=kOutput, calls=%fused_computation.23.clone.1 | convolution fusion | flops 920715264 | bytes 30707712 | tf_op jit(solution)/shard_map/while/body/eval_jaxpr/hqk,khd->qhd/dot_general | solution.py:85
  131.7 14.8 %fusion.125 = (f32[12,768]{1,0:T(8,128)S(1)}, f32[12,768,768]{1,2,0:T(8,128)}) fusion(bf16[768,12,64]{0,2,1:T(8,128)(2,1)} %bitcast.119, bf16[768,12,64]{0,2,1:T(8,128)(2,1)} %bitcast.130), kind=kOutput, calls=%fused_computation.147.clone.1 | convolution fusion | flops 927204096 | bytes 30707712 | tf_op jit(solution)/shard_map/while/body/eval_jaxpr/sub | solution.py:84
  147.2 10.8 %fusion.126 = bf16[12,64,768]{2,1,0:T(8,128)(2,1)S(1)} fusion(bf16[768,12,64]{0,2,1:T(8,128)(2,1)S(1)} %bitcast.120, f32[12,768,768]{1,2,0:T(8,128)} %get-tuple-element.240, f32[12,768]{1,0:T(8,128)S(1)} %get-tuple-element.241), kind=kOutput, calls=%fused_computation.23.clone.1 | convolution fusion | flops 920715264 | bytes 30707712 | tf_op jit(solution)/shard_map/while/body/eval_jaxpr/hqk,khd->qhd/dot_general | solution.py:85
  167.9 14.8 %fusion.125 = (f32[12,768]{1,0:T(8,128)S(1)}, f32[12,768,768]{1,2,0:T(8,128)}) fusion(bf16[768,12,64]{0,2,1:T(8,128)(2,1)} %bitcast.119, bf16[768,12,64]{0,2,1:T(8,128)(2,1)} %bitcast.130), kind=kOutput, calls=%fused_computation.147.clone.1 | convolution fusion | flops 927204096 | bytes 30707712 | tf_op jit(solution)/shard_map/while/body/eval_jaxpr/sub | solution.py:84
  183.3 10.8 %fusion.126 = bf16[12,64,768]{2,1,0:T(8,128)(2,1)S(1)} fusion(bf16[768,12,64]{0,2,1:T(8,128)(2,1)S(1)} %bitcast.120, f32[12,768,768]{1,2,0:T(8,128)} %get-tuple-element.240, f32[12,768]{1,0:T(8,128)S(1)} %get-tuple-element.241), kind=kOutput, calls=%fused_computation.23.clone.1 | convolution fusion | flops 920715264 | bytes 30707712 | tf_op jit(solution)/shard_map/while/body/eval_jaxpr/hqk,khd->qhd/dot_general | solution.py:85
  204.0 14.8 %fusion.125 = (f32[12,768]{1,0:T(8,128)S(1)}, f32[12,768,768]{1,2,0:T(8,128)}) fusion(bf16[768,12,64]{0,2,1:T(8,128)(2,1)} %bitcast.119, bf16[768,12,64]{0,2,1:T(8,128)(2,1)} %bitcast.130), kind=kOutput, calls=%fused_computation.147.clone.1 | convolution fusion | flops 927204096 | bytes 30707712 | tf_op jit(solution)/shard_map/while/body/eval_jaxpr/sub | solution.py:84
  219.5 10.8 %fusion.126 = bf16[12,64,768]{2,1,0:T(8,128)(2,1)S(1)} fusion(bf16[768,12,64]{0,2,1:T(8,128)(2,1)S(1)} %bitcast.120, f32[12,768,768]{1,2,0:T(8,128)} %get-tuple-element.240, f32[12,768]{1,0:T(8,128)S(1)} %get-tuple-element.241), kind=kOutput, calls=%fused_computation.23.clone.1 | convolution fusion | flops 920715264 | bytes 30707712 | tf_op jit(solution)/shard_map/while/body/eval_jaxpr/hqk,khd->qhd/dot_general | solution.py:85
  234.5 5.9 %fusion.90 = (f32[4]{0:T(128)S(1)}, f32[4]{0:T(128)S(1)}, f32[4,768,256]{2,1,0:T(8,128)S(1)}) fusion(f32[768,256]{1,0:T(8,128)} %multiply_add_fusion, f32[4,768,512]{2,1,0:T(8,128)} %get-tuple-element.75, f32[4]{0:T(128)S(1)} %copy-done.19, f32[4]{0:T(128)S(1)} %copy-done.18, f32[4,768,256]{2,1,0:T(8,128)} %gather_fusion, f32[768,256]{1,0:T(8,128)S(1)} %bitcast.128, ...), kind=kLoop, calls=%fused_computation.145 | loop fusion | flops 13369336 | bytes 14155844 | tf_op jit(solution)/shard_map/reduce_sum | solution.py:176
  240.4 5.7 %fusion.96 = (bf16[4,768,256]{2,0,1:T(4,128)(2,1)S(1)}, f32[4,768,256]{2,0,1:T(4,128)}) fusion(f32[4,768,256]{2,1,0:T(8,128)S(1)} %get-tuple-element.147, s32[4]{0:T(128)S(1)} %get-tuple-element.303), kind=kOutput, calls=%fused_computation.150 | convolution fusion | flops 38535184 | bytes 7864336 | tf_op jit(solution)/shard_map/cp,clq->plq/dot_general | solution.py:169
  254.2 71.1 %psum.14 = f32[2,128]{1,0:T(2,128)S(1)} all-reduce(f32[2,128]{1,0:T(2,128)S(1)} %fusion.66), channel_id=1, replica_groups=mesh['group'=4,'img'=32] {'group','img'}, use_global_device_ids=true, to_apply=%region_10.11 | all-reduce | flops 256 | bytes 2048 | tf_op jit(solution)/shard_map/psum | solution.py:180
  331.2 6.7 %fusion.32 = f32[1,768,256]{2,0,1:T(1,128)S(1)} fusion(f32[4,768,256]{2,1,0:T(8,128)} %copy-done.6), kind=kOutput, calls=%fused_computation.62 | convolution fusion | flops 9437184 | bytes 3932160 | tf_op jit(solution)/shard_map/ci,clq->ilq/dot_general | solution.py:168
  348.5 4.9 %collective-permute-done.11 = bf16[1,768,256]{2,1,0:T(8,128)(2,1)S(1)} collective-permute-done((bf16[1,768,256]{2,1,0:T(8,128)(2,1)S(1)}, bf16[1,768,256]{2,1,0:T(8,128)(2,1)S(1)}, u32[]{:S(2)}, u32[]{:S(2)}) %collective-permute-start.11) | collective-permute-done | bytes 393248 | tf_op jit(solution)/shard_map/ppermute | solution.py:36
  355.2 4.5 gather_fusion.5
  359.7 7.1 %fusion.89 = (f32[4]{0:T(128)S(1)}, f32[4]{0:T(128)S(1)}, f32[4,768,256]{2,1,0:T(8,128)}) fusion(f32[768,256]{1,0:T(8,128)S(1)} %copy-done.9, f32[4,768,512]{2,1,0:T(8,128)} %get-tuple-element.75, f32[4]{0:T(128)S(1)} %sub.158, f32[4]{0:T(128)S(1)} %sub.156, f32[4,768,256]{2,1,0:T(8,128)} %gather_fusion.5, f32[768,256]{1,0:T(8,128)S(1)} %bitcast.129, ...), kind=kLoop, calls=%fused_computation.144 | loop fusion | flops 13369336 | bytes 14155844 | tf_op jit(solution)/shard_map/reduce_sum | solution.py:176
  367.0 63.7 %psum.15 = f32[2,128]{1,0:T(2,128)S(1)} all-reduce(f32[2,128]{1,0:T(2,128)S(1)} %fusion.65), channel_id=1, replica_groups=mesh['group'=4,'img'=32] {'group','img'}, use_global_device_ids=true, to_apply=%region_13.14 | all-reduce | flops 256 | bytes 2048 | tf_op jit(solution)/shard_map/psum | solution.py:180
  430.7 6.9 %fusion.97 = (bf16[4,768,256]{2,0,1:T(4,128)(2,1)S(1)}, f32[4,768,256]{2,0,1:T(4,128)S(1)}) fusion(f32[4,768,256]{2,1,0:T(8,128)} %get-tuple-element.146, s32[4]{0:T(128)S(1)} %get-tuple-element.303), kind=kOutput, calls=%fused_computation.151 | convolution fusion | flops 38535184 | bytes 7864336 | tf_op jit(solution)/shard_map/cp,clq->plq/dot_general | solution.py:169
  451.6 5.9 %collective-permute-done.14 = bf16[1,768,256]{2,1,0:T(8,128)(2,1)S(1)} collective-permute-done((bf16[1,768,256]{2,1,0:T(8,128)(2,1)S(1)}, bf16[1,768,256]{2,1,0:T(8,128)(2,1)S(1)}, u32[]{:S(2)}, u32[]{:S(2)}) %collective-permute-start.14) | collective-permute-done | bytes 393248 | tf_op jit(solution)/shard_map/ppermute | solution.py:36
  (193 shorter events, 119.9 us)
Async XLA Ops:
  0.6 57.5 %collective-permute-start = (bf16[1,768,1024]{2,1,0:T(8,128)(2,1)}, bf16[1,768,1024]{2,1,0:T(8,128)(2,1)}, u32[]{:S(2)}, u32[]{:S(2)}) collective-permute-start(bf16[1,768,1024]{2,1,0:T(8,128)(2,1)} %param.17), channel_id=1, source_target_pairs={{0,1},{1,2},{2,3},{3,4},{4,5},{5,6},{6,7},{7,8},{8,9},{9,10},{10,1... | collective-permute-start | bytes 4718600 | tf_op jit(solution)/shard_map/ppermute | solution.py:24
  3.7 54.5 %collective-permute-start.1 = (bf16[1,768,1024]{2,1,0:T(8,128)(2,1)}, bf16[1,768,1024]{2,1,0:T(8,128)(2,1)}, u32[]{:S(2)}, u32[]{:S(2)}) collective-permute-start(bf16[1,768,1024]{2,1,0:T(8,128)(2,1)} %param.17), channel_id=1, source_target_pairs={{1,0},{2,1},{3,2},{4,3},{5,4},{6,5},{7,6},{8,7},{9,8},{10,9},{11,1... | collective-permute-start | bytes 4718600 | tf_op jit(solution)/shard_map/ppermute | solution.py:26
  5.0 53.2 %collective-permute-start.2 = (bf16[1,768,1024]{2,1,0:T(8,128)(2,1)}, bf16[1,768,1024]{2,1,0:T(8,128)(2,1)}, u32[]{:S(2)}, u32[]{:S(2)}) collective-permute-start(bf16[1,768,1024]{2,1,0:T(8,128)(2,1)} %param.17), channel_id=1, source_target_pairs={{0,32},{32,64},{64,96},{96,0},{1,33},{33,65},{65,97},{97,1},{2,34}... | collective-permute-start | bytes 4718600 | tf_op jit(solution)/shard_map/ppermute | solution.py:36
  6.3 12.2 %collective-permute-start.3 = (bf16[1,768,256]{2,1,0:T(8,128)(2,1)S(1)}, bf16[1,768,256]{2,1,0:T(8,128)(2,1)S(1)}, u32[]{:S(2)}, u32[]{:S(2)}) collective-permute-start(bf16[1,768,256]{2,1,0:T(8,128)(2,1)S(1)} %convert_element_type.112), channel_id=1, source_target_pairs={{0,1},{1,2},{2,3},{3,4},{4,5},{5,6},{6,7},{7,8},{8,9},{9,10},{10,1... | collective-permute-start | bytes 1179656 | tf_op jit(solution)/shard_map/ppermute | solution.py:24
  9.7 23.5 %collective-permute-start.4 = (bf16[1,768,256]{2,1,0:T(8,128)(2,1)S(1)}, bf16[1,768,256]{2,1,0:T(8,128)(2,1)}, u32[]{:S(2)}, u32[]{:S(2)}) collective-permute-start(bf16[1,768,256]{2,1,0:T(8,128)(2,1)S(1)} %convert_element_type.112), channel_id=1, source_target_pairs={{1,0},{2,1},{3,2},{4,3},{5,4},{6,5},{7,6},{8,7},{9,8},{10,9},{11,1... | collective-permute-start | bytes 1179656 | tf_op jit(solution)/shard_map/ppermute | solution.py:26
  18.5 32.2 %collective-permute-start.5 = (bf16[1,768,256]{2,1,0:T(8,128)(2,1)S(1)}, bf16[1,768,256]{2,1,0:T(8,128)(2,1)}, u32[]{:S(2)}, u32[]{:S(2)}) collective-permute-start(bf16[1,768,256]{2,1,0:T(8,128)(2,1)S(1)} %convert_element_type.112), channel_id=1, source_target_pairs={{0,32},{32,64},{64,96},{96,0},{1,33},{33,65},{65,97},{97,1},{2,34}... | collective-permute-start | bytes 1179656 | tf_op jit(solution)/shard_map/ppermute | solution.py:36
  32.1 26.0 %copy-start.14 = (s32[1024]{0:T(1024)}, s32[1024]{0:T(1024)S(1)}, u32[]{:S(2)}) copy-start(s32[1024]{0:T(1024)S(1)} %pad_clamp_fusion.2) | copy-start | bytes 12292
  89.8 144.6 %copy-start.8 = (f32[1,768,256]{2,1,0:T(8,128)S(1)}, f32[1,768,256]{2,1,0:T(8,128)}, u32[]{:S(2)}) copy-start(f32[1,768,256]{2,1,0:T(8,128)} %param.29) | copy-start | bytes 2359300
  89.8 144.6 %copy-start.15 = (pred[4]{0:T(512)(128)(4,1)S(1)}, pred[4]{0:T(512)(128)(4,1)}, u32[]{:S(2)}) copy-start(pred[4]{0:T(512)(128)(4,1)} %iota_compare_fusion.7) | copy-start | bytes 16
  89.8 144.6 %copy-start.18 = (f32[4]{0:T(128)S(1)}, f32[4]{0:T(128)}, u32[]{:S(2)}) copy-start(f32[4]{0:T(128)} %sub.144) | copy-start | bytes 52
  89.8 144.6 %copy-start.19 = (f32[4]{0:T(128)S(1)}, f32[4]{0:T(128)}, u32[]{:S(2)}) copy-start(f32[4]{0:T(128)} %sub.145) | copy-start | bytes 52
  246.1 79.2 %copy-start.3 = (f32[128]{0:T(128)S(1)}, f32[128]{0:T(128)}, u32[]{:S(2)}) copy-start(f32[128]{0:T(128)} %param.31) | copy-start | bytes 1540
  246.1 79.2 %copy-start.5 = (f32[128]{0:T(128)S(1)}, f32[128]{0:T(128)}, u32[]{:S(2)}) copy-start(f32[128]{0:T(128)} %param.30) | copy-start | bytes 1540
  247.9 90.0 %collective-permute-start.6 = (bf16[1,768,256]{2,1,0:T(8,128)(2,1)S(1)}, bf16[1,768,256]{2,1,0:T(8,128)(2,1)S(1)}, u32[]{:S(2)}, u32[]{:S(2)}) collective-permute-start(bf16[1,768,256]{2,1,0:T(8,128)(2,1)S(1)} %copy.81), channel_id=1, source_target_pairs={{1,0},{2,1},{3,2},{4,3},{5,4},{6,5},{7,6},{8,7},{9,8},{10,9},{11,1... | collective-permute-start | bytes 1179656 | tf_op jit(solution)/shard_map/ppermute | solution.py:50
  249.3 88.7 %collective-permute-start.7 = (bf16[1,768,256]{2,1,0:T(8,128)(2,1)S(1)}, bf16[1,768,256]{2,1,0:T(8,128)(2,1)S(1)}, u32[]{:S(2)}, u32[]{:S(2)}) collective-permute-start(bf16[1,768,256]{2,1,0:T(8,128)(2,1)S(1)} %copy.82), channel_id=1, source_target_pairs={{0,1},{1,2},{2,3},{3,4},{4,5},{5,6},{6,7},{7,8},{8,9},{9,10},{10,1... | collective-permute-start | bytes 1179656 | tf_op jit(solution)/shard_map/ppermute | solution.py:50
  253.1 85.6 %collective-permute-start.8 = (bf16[1,768,256]{2,1,0:T(8,128)(2,1)}, bf16[1,768,256]{2,1,0:T(8,128)(2,1)}, u32[]{:S(2)}, u32[]{:S(2)}) collective-permute-start(bf16[1,768,256]{2,1,0:T(8,128)(2,1)} %copy.83), channel_id=1, source_target_pairs={{0,96},{32,0},{64,32},{96,64},{1,97},{33,1},{65,33},{97,65},{2,98}... | collective-permute-start | bytes 1179656 | tf_op jit(solution)/shard_map/ppermute | solution.py:36
  328.3 17.6 %slice-start = ((s8[4718592]{0:T(1024)(128)(4,1)}), s8[4194304]{0:T(1024)(128)(4,1)S(1)}, s32[]{:S(2)}) async-start(s8[4718592]{0:T(1024)(128)(4,1)} %bitcast.121), calls=%async_computation | async-start | bytes 8388608
  331.2 14.7 %slice-start.1 = ((s8[4718592]{0:T(1024)(128)(4,1)}), s8[524288]{0:T(1024)(128)(4,1)S(1)}, s32[]{:S(2)}) async-start(s8[4718592]{0:T(1024)(128)(4,1)} %bitcast.121), calls=%async_computation.1 | async-start | bytes 1048576
  340.1 8.3 %collective-permute-start.10 = (bf16[1,768,256]{2,1,0:T(8,128)(2,1)S(1)}, bf16[1,768,256]{2,1,0:T(8,128)(2,1)S(1)}, u32[]{:S(2)}, u32[]{:S(2)}) collective-permute-start(bf16[1,768,256]{2,1,0:T(8,128)(2,1)S(1)} %get-tuple-element.148), channel_id=1, source_target_pairs={{1,0},{2,1},{3,2},{4,3},{5,4},{6,5},{7,6},{8,7},{9,8},{10,9},{11,1... | collective-permute-start | bytes 1179656 | tf_op jit(solution)/shard_map/ppermute | solution.py:26
  341.4 11.9 %collective-permute-start.11 = (bf16[1,768,256]{2,1,0:T(8,128)(2,1)S(1)}, bf16[1,768,256]{2,1,0:T(8,128)(2,1)S(1)}, u32[]{:S(2)}, u32[]{:S(2)}) collective-permute-start(bf16[1,768,256]{2,1,0:T(8,128)(2,1)S(1)} %get-tuple-element.148), channel_id=1, source_target_pairs={{0,32},{32,64},{64,96},{96,0},{1,33},{33,65},{65,97},{97,1},{2,34}... | collective-permute-start | bytes 1179656 | tf_op jit(solution)/shard_map/ppermute | solution.py:36
  342.7 10.6 %collective-permute-start.9 = (bf16[1,768,256]{2,1,0:T(8,128)(2,1)S(1)}, bf16[1,768,256]{2,1,0:T(8,128)(2,1)S(1)}, u32[]{:S(2)}, u32[]{:S(2)}) collective-permute-start(bf16[1,768,256]{2,1,0:T(8,128)(2,1)S(1)} %get-tuple-element.148), channel_id=1, source_target_pairs={{0,1},{1,2},{2,3},{3,4},{4,5},{5,6},{6,7},{7,8},{8,9},{9,10},{10,1... | collective-permute-start | bytes 1179656 | tf_op jit(solution)/shard_map/ppermute | solution.py:24
  439.4 12.1 %collective-permute-start.12 = (bf16[1,768,256]{2,1,0:T(8,128)(2,1)S(1)}, bf16[1,768,256]{2,1,0:T(8,128)(2,1)S(1)}, u32[]{:S(2)}, u32[]{:S(2)}) collective-permute-start(bf16[1,768,256]{2,1,0:T(8,128)(2,1)S(1)} %copy.86), channel_id=1, source_target_pairs={{1,0},{2,1},{3,2},{4,3},{5,4},{6,5},{7,6},{8,7},{9,8},{10,9},{11,1... | collective-permute-start | bytes 1179656 | tf_op jit(solution)/shard_map/ppermute | solution.py:50
  441.1 10.5 %collective-permute-start.13 = (bf16[1,768,256]{2,1,0:T(8,128)(2,1)S(1)}, bf16[1,768,256]{2,1,0:T(8,128)(2,1)S(1)}, u32[]{:S(2)}, u32[]{:S(2)}) collective-permute-start(bf16[1,768,256]{2,1,0:T(8,128)(2,1)S(1)} %copy.87), channel_id=1, source_target_pairs={{0,1},{1,2},{2,3},{3,4},{4,5},{5,6},{6,7},{7,8},{8,9},{9,10},{10,1... | collective-permute-start | bytes 1179656 | tf_op jit(solution)/shard_map/ppermute | solution.py:50
  444.2 13.2 %collective-permute-start.14 = (bf16[1,768,256]{2,1,0:T(8,128)(2,1)S(1)}, bf16[1,768,256]{2,1,0:T(8,128)(2,1)S(1)}, u32[]{:S(2)}, u32[]{:S(2)}) collective-permute-start(bf16[1,768,256]{2,1,0:T(8,128)(2,1)S(1)} %copy.88), channel_id=1, source_target_pairs={{0,96},{32,0},{64,32},{96,64},{1,97},{33,1},{65,33},{97,65},{2,98}... | collective-permute-start | bytes 1179656 | tf_op jit(solution)/shard_map/ppermute | solution.py:36
  (32 other events, 219.8 us)
where the time goes:
time: 466 us; the launch traced here: 459 us
  matrix products  167 us (36%)
  blocking collectives  135 us (29%)
  local copies, waits for them, and re-layouts  50.3 us (11%)
  other arithmetic  39.6 us (8%)
  starting transfers between devices  28.6 us (6%)
  waiting for transfers between devices  28.2 us (6%)
  loops' own time  8.03 us (2%)
    psum x2, blocking collectives, local(): totals = lax.psum(dense, ('group', 'img'))  135 us
    sub x4, matrix products, attend(): probs = jax.nn.softmax(scores, axis=-1).astype(jnp.bfloat16)  59.2 us
    dot_general x4, matrix products, attend(): jnp.einsum('hqk,khd->qhd', probs, value_heads, preferred_element_type=jnp...  43.2 us
    ppermute x5, waiting for transfers between devices, passed_along(): return lax.ppermute(value, axis, pairs)  28.2 us
    dot_general x5, matrix products, project_rows(): jnp.einsum('nlx,xy->nly', rows, weight, preferred_element_type=jnp.float32)  24.9 us
    reduce_sum x2, other arithmetic, local(): plain = jnp.sum(weighted, axis=(1, 2)) / pixel_total  13 us
    dot_general x2, matrix products, local(): jnp.einsum('cp,clq->plq', dst_onehot, weighted, precision=lax.Precision.H...  12.6 us
    dot_general x2, matrix products, local(): jnp.einsum('ci,clq->ilq', src_onehot, weighted, precision=lax.Precision.H...  10.8 us
  transfers between devices with their start and end apart: 15, of which 3 were waited for; matrix products, arithmetic and copies ran while one was open for 11% of the time, Pallas kernels for 0%

commit v1 on v0

v1 whole, which is shorter than its diff:
```python
import jax
import jax.numpy as jnp
from jax import lax
from jax.experimental import pallas as pl
from jax.experimental.pallas import tpu as pltpu
from jax.sharding import PartitionSpec as P

HEADS = 12
HEAD = 64
STEP = 0.1
LOG2E = 1.4426950408889634
F32 = jnp.float32
BF16 = jnp.bfloat16


def matmul(a, b, left=1, right=0):
    return lax.dot_general(a, b, (((left,), (right,)), ((), ())), preferred_element_type=F32)


def ramp_of(start, rows, width, total):
    row = lax.broadcasted_iota(jnp.int32, (rows, width), 0) + start
    col = lax.broadcasted_iota(jnp.int32, (rows, width), 1)
    return 2.0 * ((row * width + col).astype(F32) + 0.5) / total - 1.0


def params():
    return pltpu.CompilerParams(vmem_limit_bytes=56 << 20)


def embed_kernel(enc, weight, bias, query_gain, memory_gain, depth, embed, normed_q, packed):
    rows = 256
    width = embed.shape[1]
    for start in range(0, enc.shape[0], rows):
        part = pl.ds(start, rows)
        value = (matmul(enc[part, :], weight[...]) + bias[...]).astype(BF16)
        embed[part, :] = value
        value = value.astype(F32)
        center = value - jnp.mean(value, axis=-1, keepdims=True)
        spread = jnp.mean(center * center, axis=-1, keepdims=True)
        scaled = center * lax.rsqrt(spread + 1e-05)
        normed_q[part, :] = (scaled * query_gain[...]).astype(BF16)
        packed[part, :width] = (scaled * memory_gain[...]).astype(BF16)
        packed[part, width:] = depth[part, :].astype(BF16)


def embed_stage(enc, weight, bias, query_gain, memory_gain, depth):
    tokens, width = enc.shape[0], weight.shape[1]
    return pl.pallas_call(
        embed_kernel,
        out_shape=(
            jax.ShapeDtypeStruct((tokens, width), BF16),
            jax.ShapeDtypeStruct((tokens, width), BF16),
            jax.ShapeDtypeStruct((tokens, width + depth.shape[1]), BF16),
        ),
        compiler_params=params(),
        name="embed_stage",
    )(enc, weight, bias, query_gain, memory_gain, depth)


def attention(query_t, keys, values_t, mixed_t, group):
    tokens = query_t.shape[1]

    def scores(base, half):
        offset = pl.multiple_of(base + half * HEAD, HEAD)
        query = query_t[pl.ds(offset, HEAD), :]
        blank = jnp.zeros_like(query)
        both = jnp.concatenate([query, blank] if half == 0 else [blank, query], axis=0)
        return matmul(keys[:, pl.ds(base, 2 * HEAD)], both), offset

    def finish(score, offset):
        probs = jnp.exp2(score - jnp.max(score, axis=0, keepdims=True)).astype(BF16)
        ones = jnp.ones((16, keys.shape[0]), BF16)
        stacked = jnp.concatenate([values_t[pl.ds(offset, HEAD), :], ones], axis=0)
        mixed = matmul(stacked, probs)
        mixed_t[pl.ds(offset, HEAD), :] = (mixed[:HEAD] * (1.0 / mixed[HEAD : HEAD + 1])).astype(BF16)

    def step(index, carry):
        pending = None
        for pair in range(group):
            base = pl.multiple_of((index * group + pair) * 2 * HEAD, 2 * HEAD)
            for half in range(2):
                current = scores(base, half)
                if pending is not None:
                    finish(*pending)
                pending = current
        finish(*pending)
        return carry

    lax.fori_loop(0, HEADS // 2 // group, step, 0)


def pair_kernel(first, *refs):
    refs = list(refs)
    take = lambda count: [refs.pop(0) for _ in range(count)]
    flags, terms, packed, query_t, embed, key_w, value_wt, out_w, head_w, depth = take(10)
    total_in = None if first else take(1)[0]
    _ = None if first else take(1)[0]
    pair_tokens, sent, total_out = take(3)
    keys, values_t, mixed_t, rows_out, sems = take(5)
    zeros = take(1)[0] if first else None
    tokens, width = embed.shape
    patch = depth.shape[1]
    slots = pair_tokens.shape[0]

    if first:
        zeros[...] = jnp.zeros_like(zeros)
        for slot in range(slots):
            @pl.when(flags[slots + slot] > 0)
            def _():
                pltpu.make_async_copy(zeros, pair_tokens.at[slot], sems.at[slots + slot]).start()

    memory = packed[:, :width]
    keys[...] = matmul(memory, key_w[...]).astype(BF16)
    values_t[...] = matmul(value_wt[...], memory, 1, 1).astype(BF16)
    attention(query_t, keys, values_t, mixed_t, 3)
    rows = 256
    weight = terms[0]
    for start in range(0, tokens, rows):
        part = pl.ds(start, rows)
        attended = matmul(mixed_t[:, part], out_w[...], 0, 0)
        value = (embed[part, :].astype(F32) + attended).astype(BF16)
        rows_out[part, :] = value
        head = matmul(value, head_w[...])
        logit = head[:, patch:]
        soft = jnp.maximum(logit, 0.0) + jnp.log1p(jnp.exp(-jnp.abs(logit)))
        confidence = weight * (0.1 + soft)
        ramp = ramp_of(start, rows, patch, tokens * patch)
        other = packed[part, width:].astype(F32)
        resid = depth[part, :] - other + terms[1] + terms[2] * ramp - head[:, :patch]
        moved = confidence * resid
        sent[0, part, :] = moved.astype(BF16)
        sent[1, part, :] = confidence.astype(BF16)
        total_out[part, :] = moved if first else total_in[part, :] + moved
    for slot in range(slots):
        @pl.when(flags[slot] > 0)
        def _():
            pltpu.make_async_copy(rows_out, pair_tokens.at[slot], sems.at[slot]).start()
    for slot in range(slots):
        @pl.when(flags[slot] > 0)
        def _():
            pltpu.make_async_copy(rows_out, pair_tokens.at[slot], sems.at[slot]).wait()
    if first:
        for slot in range(slots):
            @pl.when(flags[slots + slot] > 0)
            def _():
                pltpu.make_async_copy(zeros, pair_tokens.at[slot], sems.at[slots + slot]).wait()


def pair_stage(flags, terms, packed, query_t, embed, weights, depth, slots, chain):
    first = chain is None
    tokens, width = embed.shape
    patch = depth.shape[1]
    vmem = pl.BlockSpec(memory_space=pltpu.VMEM)
    smem = pl.BlockSpec(memory_space=pltpu.SMEM)
    hbm = pl.BlockSpec(memory_space=pl.ANY)
    operands = [flags, terms, packed, query_t, embed, *weights, depth]
    specs = [smem, smem] + [vmem] * 8
    if not first:
        operands += [chain[1], chain[0]]
        specs += [vmem, hbm]
    scratch = [
        pltpu.VMEM((tokens, width), BF16),
        pltpu.VMEM((width, tokens), BF16),
        pltpu.VMEM((width, tokens), BF16),
        pltpu.VMEM((tokens, width), BF16),
        pltpu.SemaphoreType.DMA((2 * slots,)),
    ]
    if first:
        scratch.append(pltpu.VMEM((tokens, width), BF16))

    def body(*refs):
        pair_kernel(first, *refs)

    return pl.pallas_call(
        body,
        in_specs=specs,
        out_specs=(hbm, vmem, vmem),
        out_shape=(
            jax.ShapeDtypeStruct((slots, tokens, width), BF16),
            jax.ShapeDtypeStruct((2, tokens, patch), BF16),
            jax.ShapeDtypeStruct((tokens, patch), F32),
        ),
        scratch_shapes=scratch,
        input_output_aliases={} if first else {len(operands) - 1: 0},
        compiler_params=params(),
        name="pair_stage",
    )(*operands)


def align_kernel(lanes, pose, depth, total, out_p, out_o, out_x, in_p, in_o, in_x, base, change, poses):
    tokens, patch = depth.shape
    pixels = tokens * patch
    grad = total[...] - in_p[0].astype(F32) - in_o[0].astype(F32) - in_x[0].astype(F32)
    ramp = ramp_of(0, tokens, patch, pixels)
    plain = jnp.sum(grad) / pixels
    slope = jnp.sum(grad * ramp) / pixels
    delta = -STEP * (grad + plain + slope * ramp)
    change[...] = delta.astype(BF16)
    link_p = out_p[1].astype(F32) + in_p[1].astype(F32)
    link_o = out_o[1].astype(F32) + in_o[1].astype(F32)
    back = out_x[1].astype(F32)
    ahead = in_x[1].astype(F32)
    links = (link_p, link_o, back, ahead)
    base[...] = depth[...] - STEP * (2.0 * grad + delta * (link_p + link_o + back + ahead))
    tilted = delta * ramp
    shares = [jnp.sum(link * delta) / pixels for link in links]
    leans = [jnp.sum(link * tilted) / pixels for link in links]
    lane = lax.broadcasted_iota(jnp.int32, (1, poses.shape[1]), 1)

    def spread(start, first, parts):
        own = start - STEP * (2.0 * first + (parts[0] + parts[1] + parts[2] + parts[3]))
        row = jnp.where(lane == lanes[0], own, 0.0)
        for index in range(4):
            row = row + jnp.where(lane == lanes[index + 1], STEP * parts[index], 0.0)
        return row

    poses[0:1, :] = spread(pose[0], plain, shares)
    poses[1:2, :] = spread(pose[1], slope, leans)


def align_stage(lanes, pose, depth, total, outs, ins, images):
    tokens, patch = depth.shape
    vmem = pl.BlockSpec(memory_space=pltpu.VMEM)
    smem = pl.BlockSpec(memory_space=pltpu.SMEM)
    return pl.pallas_call(
        align_kernel,
        in_specs=[smem, smem] + [vmem] * 8,
        out_specs=(vmem, vmem, vmem),
        out_shape=(
            jax.ShapeDtypeStruct((tokens, patch), F32),
            jax.ShapeDtypeStruct((tokens, patch), BF16),
            jax.ShapeDtypeStruct((2, images), F32),
        ),
        compiler_params=params(),
        name="align_stage",
    )(lanes, pose, depth, total, *outs, *ins)


def swap_inner(value, count):
    return lax.ppermute(value, "img", [(i, i ^ 1) for i in range(count)])


def swap_outer(value, count):
    pairs = [(i, i + 1) for i in range(1, count - 1, 2)]
    return lax.ppermute(value, "img", pairs + [(b, a) for a, b in pairs])


def along(value, count, by):
    return lax.ppermute(value, "group", [(i, (i + by) % count) for i in range(count)])


def local(
    enc_tokens,
    embed_weight,
    embed_bias,
    query_gain,
    memory_gain,
    query_weight,
    key_weight,
    value_weight,
    out_weight,
    head_weight,
    pair_dst,
    pair_count,
    depth,
    scale,
    focal,
):
    group_count, img_count = lax.axis_size("group"), lax.axis_size("img")
    group, img = lax.axis_index("group"), lax.axis_index("img")
    slots = pair_dst.shape[0]
    images = scale.shape[0]
    own_id = group * img_count + img
    inner_id = group * img_count + (img ^ 1)
    outer_img = jnp.where(img % 2 == 0, img - 1, img + 1)
    outer_ok = (outer_img >= 0) & (outer_img < img_count)
    outer_id = group * img_count + jnp.clip(outer_img, 0, img_count - 1)
    back_id = (group + group_count - 1) % group_count * img_count + img
    next_id = (group + 1) % group_count * img_count + img
    live = jnp.arange(slots, dtype=jnp.int32) < pair_count[0]
    depth_now = depth[0]

    embed, normed_q, packed = embed_stage(
        enc_tokens[0],
        embed_weight,
        embed_bias[None, :],
        query_gain[None, :],
        memory_gain[None, :],
        depth_now,
    )
    packed_p = swap_inner(packed, img_count)
    packed_x = along(packed, group_count, 1)
    packed_o = swap_outer(packed, img_count)
    query_t = (matmul(query_weight, normed_q, 0, 1) * (HEAD**-0.5 * LOG2E)).astype(BF16)
    weights = (key_weight, value_weight.T, out_weight, head_weight)

    def stage(packed_in, target, chosen, chain):
        hits = live & chosen
        flags = jnp.concatenate([hits, ~live]).astype(jnp.int32)
        shift = scale[own_id] - scale[target]
        tilt = focal[own_id] - focal[target]
        terms = jnp.stack([jnp.sum(hits.astype(F32)), shift, tilt])
        return pair_stage(flags, terms, packed_in, query_t, embed, weights, depth_now, slots, chain)

    to_inner = pair_dst == inner_id
    to_back = pair_dst == back_id
    to_outer = ~to_inner & ~to_back
    tokens_p, sent_p, total_p = stage(packed_p, inner_id, to_inner, None)
    in_p = swap_inner(sent_p, img_count)
    tokens_o, sent_o, total_o = stage(packed_o, outer_id, to_outer, (tokens_p, total_p))
    in_o = swap_outer(sent_o, img_count)
    tokens_x, sent_x, total_x = stage(packed_x, back_id, to_back, (tokens_o, total_o))
    in_x = along(sent_x, group_count, -1)

    lanes = jnp.stack([own_id, inner_id, outer_id, back_id, next_id]).astype(jnp.int32)
    pose = jnp.stack([scale[own_id], focal[own_id]])
    base, change, poses = align_stage(
        lanes, pose, depth_now, total_x, (sent_p, sent_o, sent_x), (in_p, in_o, in_x), images
    )
    change_p = swap_inner(change, img_count)
    change_o = swap_outer(change, img_count)
    change_b = along(change, group_count, 1)
    change_n = along(change, group_count, -1)
    bit = 1
    while bit < img_count:
        poses = poses + lax.ppermute(poses, "img", [(i, i ^ bit) for i in range(img_count)])
        bit *= 2
    bit = 1
    while bit < group_count:
        poses = poses + lax.ppermute(poses, "group", [(i, i ^ bit) for i in range(group_count)])
        bit *= 2
    wide = lambda array: array.astype(F32)
    depth_out = base + STEP * (
        (wide(sent_p[1]) + wide(in_p[1])) * wide(change_p)
        + (wide(sent_o[1]) + wide(in_o[1])) * wide(change_o)
        + wide(sent_x[1]) * wide(change_b)
        + wide(in_x[1]) * wide(change_n)
    )
    return (tokens_x, depth_out[None], poses[0], poses[1])


def solution(mesh):
    placed = (
        P(("group", "img"), None, None),
        P(),
        P(),
        P(),
        P(),
        P(),
        P(),
        P(),
        P(),
        P(),
        P(("group", "img")),
        P(("group", "img")),
        P(("group", "img"), None, None),
        P(),
        P(),
    )
    return jax.shard_map(
        local,
        mesh=mesh,
        in_specs=placed,
        out_specs=(P(("group", "img"), None, None), P(("group", "img"), None, None), P(), P()),
        check_vma=False,
    )
```

time: 466 us -> 159 us (0.34); the launches traced: 459 us -> 159 us
  matrix products: 167 us -> 3.48 us
  blocking collectives: 135 us -> 0 us
  Pallas kernels: 0 us -> 67.7 us
  local copies, waits for them, and re-layouts: 50.3 us -> 10.3 us
  other arithmetic: 39.6 us -> 10.4 us
  loops' own time: 8.03 us -> 0 us
  between operations: 2.01 us -> 8.97 us
    psum x2 -> x0, blocking collectives: 135 us -> none  [local(): totals = lax.psum(dense, ('group', 'img'))]
    dot_general x23 -> x1, matrix products: 108 us -> 3.48 us  [matmul(): lax.dot_general(a, b, (((left,), (right,)), ((), ())), preferred_element_...]
    pallas_call x0 -> x5, Pallas kernels: none -> 67.7 us  [the longest x3 55.6 us: pair_stage(): pl.pallas_call(body, in_specs=specs, out_specs=(hbm, vmem, vmem), out_sha...]
    sub x4 -> x0, matrix products: 59.2 us -> none  [attend(): probs = jax.nn.softmax(scores, axis=-1).astype(jnp.bfloat16)]
    gather x10 -> x0, local copies, waits for them, and re-layouts: 16.7 us -> none  [the longest x2 8.92 us: local(): pool_depth[pool_index]]
    slice x16 -> x0, local copies, waits for them, and re-layouts: 15.6 us -> none  [the longest x4 7.14 us: one_pair(): mixed = attend(queries[source], memory[0], memory[1])]
    reduce_sum x5 -> x1, other arithmetic: 15.3 us -> 0.63 us  [stage(): terms = jnp.stack([jnp.sum(hits.astype(F32)), shift, tilt])]
    while x34 -> x0, local copies, waits for them, and re-layouts: 12.2 us -> none
  transfers between devices with their start and end apart: 15 -> 17, of which waited for: 3 -> 8; matrix products, arithmetic and copies ran while one was open for 11% -> 10% of each run, Pallas kernels for 0% -> 23%
where the time goes in v1:
time: 159 us
  Pallas kernels  67.7 us (43%)
  waiting for transfers between devices  30.2 us (19%)
  starting transfers between devices  27.8 us (17%)
  other arithmetic  10.4 us (7%)
  local copies, waits for them, and re-layouts  10.3 us (6%)
  between operations  8.97 us (6%)
  matrix products  3.48 us (2%)
    pallas_call x3, Pallas kernels, pair_stage(): pl.pallas_call(body, in_specs=specs, out_specs=(hbm, vmem, vmem), out_sha...  55.6 us
    ppermute x4, waiting for transfers between devices, along(): lax.ppermute(value, 'group', [(i, (i + by) % count) for i in range(count)])  12.4 us
    ppermute x5, starting transfers between devices, local(): lax.ppermute(poses, 'img', [(i, i ^ bit) for i in range(img_count)])  10.5 us
    ppermute x5, waiting for transfers between devices, local(): lax.ppermute(poses, 'img', [(i, i ^ bit) for i in range(img_count)])  9.12 us
    ppermute x2, waiting for transfers between devices, local(): lax.ppermute(poses, 'group', [(i, i ^ bit) for i in range(group_count)])  8.65 us
    ppermute x3, starting transfers between devices, swap_inner(): return lax.ppermute(value, 'img', [(i, i ^ 1) for i in range(count)])  7.93 us
    pallas_call x1, Pallas kernels, align_stage(): pl.pallas_call(align_kernel, in_specs=[smem, smem] + [vmem] * 8, out_spec...  6.51 us
    pallas_call x1, Pallas kernels, embed_stage(): pl.pallas_call(embed_kernel, out_shape=(jax.ShapeDtypeStruct((tokens, wid...  5.6 us
  transfers between devices with their start and end apart: 17, of which 8 were waited for; matrix products, arithmetic and copies ran while one was open for 10% of the time, Pallas kernels for 23%

profile of v1, /device:TPU:6, one launch (start us, length us, event | category | flops | bytes accessed | tf_op | source)
XLA Modules:
  0.0 158.8 jit_solution(2979892146575405409)
XLA Ops:
  4.6 5.6 %embed_stage.1 = (bf16[768,768]{1,0:T(8,128)(2,1)}, bf16[768,768]{1,0:T(8,128)(2,1)}, bf16[768,1024]{1,0:T(8,128)(2,1)}) custom-call(bf16[768,1024]{1,0:T(8,128)(2,1)} %bitcast.50, bf16[1024,768]{1,0:T(8,128)(2,1)} %weight.1, f32[1,768]{1,0:T(1,128)} %broadcast_in_dim.12.bias, f32[1,768]{1,0:T(1,128)} %broadcast_in_dim.13.query_gain, ...), custom_call_target="tpu_custom_call" | custom-call | tf_op jit(solution)/shard_map/embed_stage/pallas_call | solution.py:48
  10.2 1.8 %collective-permute-start.1 = (bf16[768,1024]{1,0:T(8,128)(2,1)}, bf16[768,1024]{1,0:T(8,128)(2,1)}, u32[]{:S(2)}, u32[]{:S(2)}) collective-permute-start(bf16[768,1024]{1,0:T(8,128)(2,1)} %get-tuple-element.19), channel_id=1, source_target_pairs={{1,2},{3,4},{5,6},{7,8},{9,10},{11,12},{13,14},{15,16},{17,18},{19... | collective-permute-start | bytes 4718600 | tf_op jit(solution)/shard_map/ppermute | solution.py:245
  21.2 2.4 %copy.22 = bf16[768,768]{0,1:T(8,128)(2,1)} copy(bf16[768,768]{1,0:T(8,128)(2,1)} %param.22) | data formatting | bytes 2359296 | tf_op args[7]
  28.6 3.5 %fusion.refs_3_ = bf16[768,768]{1,0:T(8,128)(2,1)} fusion(bf16[768,768]{1,0:T(8,128)(2,1)} %get-tuple-element.20, bf16[768,768]{1,0:T(8,128)(2,1)S(1)} %copy-done), kind=kOutput, calls=%fused_computation.1 | convolution fusion | flops 907149312 | bytes 3538944 | tf_op jit(solution)/shard_map/dot_general | solution.py:17
  32.0 18.9 %pair_stage.3 = (bf16[4,768,768]{2,1,0:T(8,128)(2,1)}, bf16[2,768,256]{2,1,0:T(8,128)(2,1)}, f32[768,256]{1,0:T(8,128)}) custom-call(s32[8]{0:T(128)} %get-tuple-element.50.refs_0_, f32[3]{0:T(128)} %pad_maximum_fusion.2.refs_1_, bf16[768,1024]{1,0:T(8,128)(2,1)} %collective-permute-done.2.refs_2_, bf16[768,768]{1,0:T(8,128)(2,1)} %fusion.refs_3_, ...), custom_call_target="tpu_custom_call" | custom-call | tf_op jit(solution)/shard_map/pair_stage/pallas_call | solution.py:174
  51.0 18.0 %pair_stage.4 = (bf16[4,768,768]{2,1,0:T(8,128)(2,1)}, bf16[2,768,256]{2,1,0:T(8,128)(2,1)}, f32[768,256]{1,0:T(8,128)}) custom-call(s32[8]{0:T(128)} %get-tuple-element.51.refs_0_, f32[3]{0:T(128)} %pad_maximum_fusion.1.refs_1_, bf16[768,1024]{1,0:T(8,128)(2,1)} %collective-permute-done.1.refs_2_, ...), custom_call_target="tpu_custom_call", output_to_operand_aliasing={{0}: (11, {})} | custom-call | tf_op jit(solution)/shard_map/pair_stage/pallas_call | solution.py:174
  70.2 18.7 %pair_stage.5 = (bf16[4,768,768]{2,1,0:T(8,128)(2,1)}, bf16[2,768,256]{2,1,0:T(8,128)(2,1)}, f32[768,256]{1,0:T(8,128)}) custom-call(s32[8]{0:T(128)} %get-tuple-element.52.refs_0_, f32[3]{0:T(128)} %pad_maximum_fusion.refs_1_, bf16[768,1024]{1,0:T(8,128)(2,1)} %copy-done.7, bf16[768,768]{1,0:T(8,128)(2,1)} %fusion.refs_3_, ...), custom_call_target="tpu_custom_call", output_to_operand_aliasing={{0}: (11, {})} | custom-call | tf_op jit(solution)/shard_map/pair_stage/pallas_call | solution.py:174
  88.9 1.7 %collective-permute-start.5 = (bf16[2,768,256]{2,1,0:T(8,128)(2,1)}, bf16[2,768,256]{2,1,0:T(8,128)(2,1)S(1)}, u32[]{:S(2)}, u32[]{:S(2)}) collective-permute-start(bf16[2,768,256]{2,1,0:T(8,128)(2,1)} %get-tuple-element.30.out_x), channel_id=1, source_target_pairs={{0,96},{32,0},{64,32},{96,64},{1,97},{33,1},{65,33},{97,65},{2,98}... | collective-permute-start | bytes 2359304 | tf_op jit(solution)/shard_map/ppermute | solution.py:249
  90.6 1.6 collective-permute-start.4
  92.2 2.9 %collective-permute-start.3 = (bf16[2,768,256]{2,1,0:T(8,128)(2,1)S(1)}, bf16[2,768,256]{2,1,0:T(8,128)(2,1)}, u32[]{:S(2)}, u32[]{:S(2)}) collective-permute-start(bf16[2,768,256]{2,1,0:T(8,128)(2,1)S(1)} %copy-done.1), channel_id=1, source_target_pairs={{0,1},{1,0},{2,3},{3,2},{4,5},{5,4},{6,7},{7,6},{8,9},{9,8},{10,11... | collective-permute-start | bytes 2359304 | tf_op jit(solution)/shard_map/ppermute | solution.py:240
  95.8 1.8 %pad_maximum_fusion.3.pose = f32[2]{0:T(128)} fusion(f32[1]{0:T(128)} %get-tuple-element.58, f32[1]{0:T(128)} %get-tuple-element.44), kind=kLoop, calls=%fused_computation.22 | loop fusion | flops 2 | bytes 16 | tf_op jit(solution)/shard_map/stack | solution.py:316
  97.6 12.4 %collective-permute-done.5.in_x = bf16[2,768,256]{2,1,0:T(8,128)(2,1)S(1)} collective-permute-done((bf16[2,768,256]{2,1,0:T(8,128)(2,1)}, bf16[2,768,256]{2,1,0:T(8,128)(2,1)S(1)}, u32[]{:S(2)}, u32[]{:S(2)}) %collective-permute-start.5) | collective-permute-done | bytes 786464 | tf_op jit(solution)/shard_map/ppermute | solution.py:249
  110.9 6.5 %align_stage.1 = (f32[768,256]{1,0:T(8,128)}, bf16[768,256]{1,0:T(8,128)(2,1)}, f32[2,128]{1,0:T(2,128)}) custom-call(s32[5]{0:T(128)} %stack.56.lanes, f32[2]{0:T(128)} %pad_maximum_fusion.3.pose, f32[768,256]{1,0:T(8,128)} %bitcast.46, f32[768,256]{1,0:T(8,128)} %get-tuple-element.27.total, bf16[2,768,256]{2,1,0:T(8,128)(2,1)} %get-tuple-element.28.out_p, ...), custom_call_target="tpu_custom_call" | custom-call | tf_op jit(solution)/shard_map/align_stage/pallas_call | solution.py:225
  117.6 3.1 %collective-permute-start.8 = (bf16[768,256]{1,0:T(8,128)(2,1)}, bf16[768,256]{1,0:T(8,128)(2,1)S(1)}, u32[]{:S(2)}, u32[]{:S(2)}) collective-permute-start(bf16[768,256]{1,0:T(8,128)(2,1)} %get-tuple-element.32), channel_id=1, source_target_pairs={{0,32},{32,64},{64,96},{96,0},{1,33},{33,65},{65,97},{97,1},{2,34}... | collective-permute-start | bytes 1179656 | tf_op jit(solution)/shard_map/ppermute | solution.py:249
  121.4 5.0 %collective-permute-start.6 = (bf16[768,256]{1,0:T(8,128)(2,1)}, bf16[768,256]{1,0:T(8,128)(2,1)S(1)}, u32[]{:S(2)}, u32[]{:S(2)}) collective-permute-start(bf16[768,256]{1,0:T(8,128)(2,1)} %get-tuple-element.32), channel_id=1, source_target_pairs={{0,1},{1,0},{2,3},{3,2},{4,5},{5,4},{6,7},{7,6},{8,9},{9,8},{10,11... | collective-permute-start | bytes 1179656 | tf_op jit(solution)/shard_map/ppermute | solution.py:240
  129.9 2.3 %collective-permute-done.11 = f32[2,128]{1,0:T(2,128)S(1)} collective-permute-done((f32[2,128]{1,0:T(2,128)S(1)}, f32[2,128]{1,0:T(2,128)S(1)}, u32[]{:S(2)}, u32[]{:S(2)}) %collective-permute-start.11) | collective-permute-done | bytes 1056 | tf_op jit(solution)/shard_map/ppermute | solution.py:326
  132.2 2.9 %collective-permute-start.12 = (f32[2,128]{1,0:T(2,128)S(1)}, f32[2,128]{1,0:T(2,128)S(1)}, u32[]{:S(2)}, u32[]{:S(2)}) collective-permute-start(f32[2,128]{1,0:T(2,128)S(1)} %add.126), channel_id=1, source_target_pairs={{0,4},{1,5},{2,6},{3,7},{4,0},{5,1},{6,2},{7,3},{8,12},{9,13},{10,... | collective-permute-start | bytes 3080 | tf_op jit(solution)/shard_map/ppermute | solution.py:326
  135.1 2.2 %collective-permute-done.12 = f32[2,128]{1,0:T(2,128)S(1)} collective-permute-done((f32[2,128]{1,0:T(2,128)S(1)}, f32[2,128]{1,0:T(2,128)S(1)}, u32[]{:S(2)}, u32[]{:S(2)}) %collective-permute-start.12) | collective-permute-done | bytes 1056 | tf_op jit(solution)/shard_map/ppermute | solution.py:326
  137.2 1.9 %collective-permute-start.13 = (f32[2,128]{1,0:T(2,128)S(1)}, f32[2,128]{1,0:T(2,128)S(1)}, u32[]{:S(2)}, u32[]{:S(2)}) collective-permute-start(f32[2,128]{1,0:T(2,128)S(1)} %add.127), channel_id=1, source_target_pairs={{0,8},{1,9},{2,10},{3,11},{4,12},{5,13},{6,14},{7,15},{8,0},{9,1},... | collective-permute-start | bytes 3080 | tf_op jit(solution)/shard_map/ppermute | solution.py:326
  139.2 1.7 %collective-permute-done.13 = f32[2,128]{1,0:T(2,128)S(1)} collective-permute-done((f32[2,128]{1,0:T(2,128)S(1)}, f32[2,128]{1,0:T(2,128)S(1)}, u32[]{:S(2)}, u32[]{:S(2)}) %collective-permute-start.13) | collective-permute-done | bytes 1056 | tf_op jit(solution)/shard_map/ppermute | solution.py:326
  140.8 4.3 %collective-permute-start.14 = (f32[2,128]{1,0:T(2,128)S(1)}, f32[2,128]{1,0:T(2,128)S(1)}, u32[]{:S(2)}, u32[]{:S(2)}) collective-permute-start(f32[2,128]{1,0:T(2,128)S(1)} %add.128), channel_id=1, source_target_pairs={{0,16},{1,17},{2,18},{3,19},{4,20},{5,21},{6,22},{7,23},{8,24},{9,... | collective-permute-start | bytes 3080 | tf_op jit(solution)/shard_map/ppermute | solution.py:326
  146.6 3.6 %collective-permute-done.15 = f32[2,128]{1,0:T(2,128)S(1)} collective-permute-done((f32[2,128]{1,0:T(2,128)S(1)}, f32[2,128]{1,0:T(2,128)S(1)}, u32[]{:S(2)}, u32[]{:S(2)}) %collective-permute-start.15) | collective-permute-done | bytes 1056 | tf_op jit(solution)/shard_map/ppermute | solution.py:330
  150.2 5.1 %collective-permute-done.16 = f32[2,128]{1,0:T(2,128)S(1)} collective-permute-done((f32[2,128]{1,0:T(2,128)S(1)}, f32[2,128]{1,0:T(2,128)S(1)}, u32[]{:S(2)}, u32[]{:S(2)}) %collective-permute-start.16) | collective-permute-done | bytes 1056 | tf_op jit(solution)/shard_map/ppermute | solution.py:330
  155.9 2.9 %fusion.4 = f32[1,768,256]{2,1,0:T(8,128)} fusion(f32[768,256]{1,0:T(8,128)} %get-tuple-element.31, bf16[768,256]{1,0:T(8,128)(2,1)S(1)} %collective-permute-done.9, bf16[768,256]{1,0:T(8,128)(2,1)S(1)} %collective-permute-done.8, bf16[768,256]{1,0:T(8,128)(2,1)S(1)} %collective-permute-done.7, bf16[768,256]{1,0:T(8,128)(2,1)S(1)} %collective-permute-done.6, ...), kind=kLoop, calls=%fused_computation.6 | loop fusion | flops 4128768 | bytes 5505024 | tf_op jit(solution)/shard_map/broadcast_in_dim | solution.py:339
  (60 shorter events, 19.2 us)
Async XLA Ops:
  0.6 27.9 %copy-start = (bf16[768,768]{1,0:T(8,128)(2,1)S(1)}, bf16[768,768]{1,0:T(8,128)(2,1)}, u32[]{:S(2)}) copy-start(bf16[768,768]{1,0:T(8,128)(2,1)} %param.20) | copy-start | bytes 3538948
  4.6 8.4 %copy-start.9 = (f32[128]{0:T(128)S(1)}, f32[128]{0:T(128)}, u32[]{:S(2)}) copy-start(f32[128]{0:T(128)} %param.29) | copy-start | bytes 1540
  10.2 21.9 %collective-permute-start.2 = (bf16[768,1024]{1,0:T(8,128)(2,1)}, bf16[768,1024]{1,0:T(8,128)(2,1)}, u32[]{:S(2)}, u32[]{:S(2)}) collective-permute-start(bf16[768,1024]{1,0:T(8,128)(2,1)} %get-tuple-element.19), channel_id=1, source_target_pairs={{0,1},{1,0},{2,3},{3,2},{4,5},{5,4},{6,7},{7,6},{8,9},{9,8},{10,11... | collective-permute-start | bytes 4718600 | tf_op jit(solution)/shard_map/ppermute | solution.py:240
  10.2 40.8 %collective-permute-start.1 = (bf16[768,1024]{1,0:T(8,128)(2,1)}, bf16[768,1024]{1,0:T(8,128)(2,1)}, u32[]{:S(2)}, u32[]{:S(2)}) collective-permute-start(bf16[768,1024]{1,0:T(8,128)(2,1)} %get-tuple-element.19), channel_id=1, source_target_pairs={{1,2},{3,4},{5,6},{7,8},{9,10},{11,12},{13,14},{15,16},{17,18},{19... | collective-permute-start | bytes 4718600 | tf_op jit(solution)/shard_map/ppermute | solution.py:245
  12.0 57.0 %collective-permute-start = (bf16[768,1024]{1,0:T(8,128)(2,1)}, bf16[768,1024]{1,0:T(8,128)(2,1)S(1)}, u32[]{:S(2)}, u32[]{:S(2)}) collective-permute-start(bf16[768,1024]{1,0:T(8,128)(2,1)} %get-tuple-element.19), channel_id=1, source_target_pairs={{0,32},{32,64},{64,96},{96,0},{1,33},{33,65},{65,97},{97,1},{2,34}... | collective-permute-start | bytes 4718600 | tf_op jit(solution)/shard_map/ppermute | solution.py:249
  70.2 20.5 %copy-start.3 = (bf16[2,768,256]{2,1,0:T(8,128)(2,1)S(1)}, bf16[2,768,256]{2,1,0:T(8,128)(2,1)}, u32[]{:S(2)}) copy-start(bf16[2,768,256]{2,1,0:T(8,128)(2,1)} %get-tuple-element.29.out_o) | copy-start | bytes 2359300
  70.2 22.0 %copy-start.1 = (bf16[2,768,256]{2,1,0:T(8,128)(2,1)S(1)}, bf16[2,768,256]{2,1,0:T(8,128)(2,1)}, u32[]{:S(2)}) copy-start(bf16[2,768,256]{2,1,0:T(8,128)(2,1)} %get-tuple-element.28.out_p) | copy-start | bytes 2359300
  88.9 21.1 %collective-permute-start.5 = (bf16[2,768,256]{2,1,0:T(8,128)(2,1)}, bf16[2,768,256]{2,1,0:T(8,128)(2,1)S(1)}, u32[]{:S(2)}, u32[]{:S(2)}) collective-permute-start(bf16[2,768,256]{2,1,0:T(8,128)(2,1)} %get-tuple-element.30.out_x), channel_id=1, source_target_pairs={{0,96},{32,0},{64,32},{96,64},{1,97},{33,1},{65,33},{97,65},{2,98}... | collective-permute-start | bytes 2359304 | tf_op jit(solution)/shard_map/ppermute | solution.py:249
  90.6 19.4 %collective-permute-start.4 = (bf16[2,768,256]{2,1,0:T(8,128)(2,1)S(1)}, bf16[2,768,256]{2,1,0:T(8,128)(2,1)}, u32[]{:S(2)}, u32[]{:S(2)}) collective-permute-start(bf16[2,768,256]{2,1,0:T(8,128)(2,1)S(1)} %copy-done.3), channel_id=1, source_target_pairs={{1,2},{3,4},{5,6},{7,8},{9,10},{11,12},{13,14},{15,16},{17,18},{19... | collective-permute-start | bytes 2359304 | tf_op jit(solution)/shard_map/ppermute | solution.py:245
  92.2 17.8 %collective-permute-start.3 = (bf16[2,768,256]{2,1,0:T(8,128)(2,1)S(1)}, bf16[2,768,256]{2,1,0:T(8,128)(2,1)}, u32[]{:S(2)}, u32[]{:S(2)}) collective-permute-start(bf16[2,768,256]{2,1,0:T(8,128)(2,1)S(1)} %copy-done.1), channel_id=1, source_target_pairs={{0,1},{1,0},{2,3},{3,2},{4,5},{5,4},{6,7},{7,6},{8,9},{9,8},{10,11... | collective-permute-start | bytes 2359304 | tf_op jit(solution)/shard_map/ppermute | solution.py:240
  110.9 44.9 %copy-start.2 = (bf16[2,768,256]{2,1,0:T(8,128)(2,1)S(1)}, bf16[2,768,256]{2,1,0:T(8,128)(2,1)}, u32[]{:S(2)}) copy-start(bf16[2,768,256]{2,1,0:T(8,128)(2,1)} %get-tuple-element.28.out_p) | copy-start | bytes 2359300
  110.9 44.9 %copy-start.4 = (bf16[2,768,256]{2,1,0:T(8,128)(2,1)S(1)}, bf16[2,768,256]{2,1,0:T(8,128)(2,1)}, u32[]{:S(2)}) copy-start(bf16[2,768,256]{2,1,0:T(8,128)(2,1)} %get-tuple-element.29.out_o) | copy-start | bytes 2359300
  110.9 44.9 %copy-start.5 = (bf16[2,768,256]{2,1,0:T(8,128)(2,1)S(1)}, bf16[2,768,256]{2,1,0:T(8,128)(2,1)}, u32[]{:S(2)}) copy-start(bf16[2,768,256]{2,1,0:T(8,128)(2,1)} %get-tuple-element.30.out_x) | copy-start | bytes 2359300
  117.4 38.4 %collective-permute-start.9 = (bf16[768,256]{1,0:T(8,128)(2,1)}, bf16[768,256]{1,0:T(8,128)(2,1)S(1)}, u32[]{:S(2)}, u32[]{:S(2)}) collective-permute-start(bf16[768,256]{1,0:T(8,128)(2,1)} %get-tuple-element.32), channel_id=1, source_target_pairs={{0,96},{32,0},{64,32},{96,64},{1,97},{33,1},{65,33},{97,65},{2,98}... | collective-permute-start | bytes 1179656 | tf_op jit(solution)/shard_map/ppermute | solution.py:249
  117.6 38.2 %collective-permute-start.8 = (bf16[768,256]{1,0:T(8,128)(2,1)}, bf16[768,256]{1,0:T(8,128)(2,1)S(1)}, u32[]{:S(2)}, u32[]{:S(2)}) collective-permute-start(bf16[768,256]{1,0:T(8,128)(2,1)} %get-tuple-element.32), channel_id=1, source_target_pairs={{0,32},{32,64},{64,96},{96,0},{1,33},{33,65},{65,97},{97,1},{2,34}... | collective-permute-start | bytes 1179656 | tf_op jit(solution)/shard_map/ppermute | solution.py:249
  120.7 35.1 %collective-permute-start.7 = (bf16[768,256]{1,0:T(8,128)(2,1)}, bf16[768,256]{1,0:T(8,128)(2,1)S(1)}, u32[]{:S(2)}, u32[]{:S(2)}) collective-permute-start(bf16[768,256]{1,0:T(8,128)(2,1)} %get-tuple-element.32), channel_id=1, source_target_pairs={{1,2},{3,4},{5,6},{7,8},{9,10},{11,12},{13,14},{15,16},{17,18},{19... | collective-permute-start | bytes 1179656 | tf_op jit(solution)/shard_map/ppermute | solution.py:245
  121.4 34.5 %collective-permute-start.6 = (bf16[768,256]{1,0:T(8,128)(2,1)}, bf16[768,256]{1,0:T(8,128)(2,1)S(1)}, u32[]{:S(2)}, u32[]{:S(2)}) collective-permute-start(bf16[768,256]{1,0:T(8,128)(2,1)} %get-tuple-element.32), channel_id=1, source_target_pairs={{0,1},{1,0},{2,3},{3,2},{4,5},{5,4},{6,7},{7,6},{8,9},{9,8},{10,11... | collective-permute-start | bytes 1179656 | tf_op jit(solution)/shard_map/ppermute | solution.py:240
  126.3 1.6 collective-permute-start.10
  128.6 3.6 %collective-permute-start.11 = (f32[2,128]{1,0:T(2,128)S(1)}, f32[2,128]{1,0:T(2,128)S(1)}, u32[]{:S(2)}, u32[]{:S(2)}) collective-permute-start(f32[2,128]{1,0:T(2,128)S(1)} %add.125), channel_id=1, source_target_pairs={{0,2},{1,3},{2,0},{3,1},{4,6},{5,7},{6,4},{7,5},{8,10},{9,11},{10,... | collective-permute-start | bytes 3080 | tf_op jit(solution)/shard_map/ppermute | solution.py:326
  132.2 5.1 %collective-permute-start.12 = (f32[2,128]{1,0:T(2,128)S(1)}, f32[2,128]{1,0:T(2,128)S(1)}, u32[]{:S(2)}, u32[]{:S(2)}) collective-permute-start(f32[2,128]{1,0:T(2,128)S(1)} %add.126), channel_id=1, source_target_pairs={{0,4},{1,5},{2,6},{3,7},{4,0},{5,1},{6,2},{7,3},{8,12},{9,13},{10,... | collective-permute-start | bytes 3080 | tf_op jit(solution)/shard_map/ppermute | solution.py:326
  137.2 3.6 %collective-permute-start.13 = (f32[2,128]{1,0:T(2,128)S(1)}, f32[2,128]{1,0:T(2,128)S(1)}, u32[]{:S(2)}, u32[]{:S(2)}) collective-permute-start(f32[2,128]{1,0:T(2,128)S(1)} %add.127), channel_id=1, source_target_pairs={{0,8},{1,9},{2,10},{3,11},{4,12},{5,13},{6,14},{7,15},{8,0},{9,1},... | collective-permute-start | bytes 3080 | tf_op jit(solution)/shard_map/ppermute | solution.py:326
  140.8 5.8 %collective-permute-start.14 = (f32[2,128]{1,0:T(2,128)S(1)}, f32[2,128]{1,0:T(2,128)S(1)}, u32[]{:S(2)}, u32[]{:S(2)}) collective-permute-start(f32[2,128]{1,0:T(2,128)S(1)} %add.128), channel_id=1, source_target_pairs={{0,16},{1,17},{2,18},{3,19},{4,20},{5,21},{6,22},{7,23},{8,24},{9,... | collective-permute-start | bytes 3080 | tf_op jit(solution)/shard_map/ppermute | solution.py:326
  146.6 3.6 %collective-permute-start.15 = (f32[2,128]{1,0:T(2,128)S(1)}, f32[2,128]{1,0:T(2,128)S(1)}, u32[]{:S(2)}, u32[]{:S(2)}) collective-permute-start(f32[2,128]{1,0:T(2,128)S(1)} %add.129), channel_id=1, source_target_pairs={{0,32},{32,0},{64,96},{96,64},{1,33},{33,1},{65,97},{97,65},{2,34}... | collective-permute-start | bytes 3080 | tf_op jit(solution)/shard_map/ppermute | solution.py:330
  150.2 5.1 %collective-permute-start.16 = (f32[2,128]{1,0:T(2,128)S(1)}, f32[2,128]{1,0:T(2,128)S(1)}, u32[]{:S(2)}, u32[]{:S(2)}) collective-permute-start(f32[2,128]{1,0:T(2,128)S(1)} %add.130), channel_id=1, source_target_pairs={{0,64},{32,96},{64,0},{96,32},{1,65},{33,97},{65,1},{97,33},{2,66}... | collective-permute-start | bytes 3080 | tf_op jit(solution)/shard_map/ppermute | solution.py:330
  (4 other events, 12.9 us)

commit v2 on v1

v2 whole, which is shorter than its diff:
```python
import jax
import jax.numpy as jnp
from jax import lax
from jax.experimental import pallas as pl
from jax.experimental.pallas import tpu as pltpu
from jax.sharding import PartitionSpec as P

HEADS = 12
HEAD = 64
STEP = 0.1
LOG2E = 1.4426950408889634
F32 = jnp.float32
BF16 = jnp.bfloat16


def matmul(a, b, left=1, right=0):
    return lax.dot_general(a, b, (((left,), (right,)), ((), ())), preferred_element_type=F32)


def ramp_of(start, rows, width, total):
    row = lax.broadcasted_iota(jnp.int32, (rows, width), 0) + start
    col = lax.broadcasted_iota(jnp.int32, (rows, width), 1)
    return 2.0 * ((row * width + col).astype(F32) + 0.5) / total - 1.0


def params():
    return pltpu.CompilerParams(vmem_limit_bytes=24 << 20)


VMEM = pl.BlockSpec(memory_space=pltpu.VMEM)
SMEM = pl.BlockSpec(memory_space=pltpu.SMEM)
HBM = pl.BlockSpec(memory_space=pl.ANY)


def neighbours():
    group_count, img_count = lax.axis_size("group"), lax.axis_size("img")
    group, img = lax.axis_index("group"), lax.axis_index("img")
    base = group * img_count
    inner = base + img + 1 - 2 * (img % 2)
    outer = base + jnp.clip(img - 1 + 2 * (img % 2), 0, img_count - 1)
    back = (group + group_count - 1) % group_count * img_count + img
    ahead = (group + 1) % group_count * img_count + img
    return base + img, inner, outer, back, ahead


def normed(value, gain):
    value = value.astype(F32)
    center = value - jnp.mean(value, axis=-1, keepdims=True)
    spread = jnp.mean(center * center, axis=-1, keepdims=True)
    return (center * lax.rsqrt(spread + 1e-05) * gain).astype(BF16)


def embed_kernel(enc, weight, bias, memory_gain, depth, embed, packed):
    width = embed.shape[1]
    value = (matmul(enc[...], weight[...]) + bias[...][None, :]).astype(BF16)
    embed[...] = value
    packed[:, :width] = normed(value, memory_gain[...][None, :])
    packed[:, width:] = depth[...].astype(BF16)


def embed_stage(enc, weight, bias, memory_gain, depth):
    tokens, width = enc.shape[0], weight.shape[1]
    patch = depth.shape[1]
    rows = 256
    whole = lambda array: pl.BlockSpec(array.shape, lambda i: (0,) * array.ndim)
    strip = lambda cols: pl.BlockSpec((rows, cols), lambda i: (i, 0))
    return pl.pallas_call(
        embed_kernel,
        grid=(tokens // rows,),
        in_specs=[strip(enc.shape[1]), whole(weight), whole(bias), whole(memory_gain), strip(patch)],
        out_specs=(strip(width), strip(width + patch)),
        out_shape=(
            jax.ShapeDtypeStruct((tokens, width), BF16),
            jax.ShapeDtypeStruct((tokens, width + patch), BF16),
        ),
        compiler_params=params(),
        name="embed_stage",
    )(enc, weight, bias, memory_gain, depth)


def query_kernel(embed, gain, query_w, value_w, query_t, value_wt):
    scaled = HEAD**-0.5 * LOG2E
    value_wt[...] = value_w[...].T
    rows = 256
    for start in range(0, embed.shape[0], rows):
        part = pl.ds(start, rows)
        value = normed(embed[part, :], gain[...][None, :])
        query_t[:, part] = (matmul(query_w[...], value, 0, 1) * scaled).astype(BF16)


def query_stage(embed, gain, query_w, value_w):
    return pl.pallas_call(
        query_kernel,
        in_specs=[VMEM] * 4,
        out_specs=(VMEM, VMEM),
        out_shape=(
            jax.ShapeDtypeStruct(embed.shape[::-1], BF16),
            jax.ShapeDtypeStruct(value_w.shape[::-1], BF16),
        ),
        compiler_params=params(),
        name="query_stage",
    )(embed, gain, query_w, value_w)


def attention(query_t, keys, values_t, mixed_t, first, count, group):
    def scores(base, half):
        offset = pl.multiple_of(base + half * HEAD, HEAD)
        query = query_t[pl.ds(offset, HEAD), pl.ds(first, count)]
        blank = jnp.zeros_like(query)
        both = jnp.concatenate([query, blank] if half == 0 else [blank, query], axis=0)
        return matmul(keys[:, pl.ds(base, 2 * HEAD)], both), offset

    def finish(score, offset):
        probs = jnp.exp2(score - jnp.max(score, axis=0, keepdims=True)).astype(BF16)
        ones = jnp.ones((16, keys.shape[0]), BF16)
        stacked = jnp.concatenate([values_t[pl.ds(offset, HEAD), :], ones], axis=0)
        mixed = matmul(stacked, probs)
        mixed_t[pl.ds(offset, HEAD), :] = (mixed[:HEAD] * (1.0 / mixed[HEAD : HEAD + 1])).astype(BF16)

    def step(index, carry):
        pending = None
        for pair in range(group):
            base = pl.multiple_of((index * group + pair) * 2 * HEAD, 2 * HEAD)
            for half in range(2):
                current = scores(base, half)
                if pending is not None:
                    finish(*pending)
                pending = current
        finish(*pending)
        return carry

    lax.fori_loop(0, HEADS // 2 // group, step, 0)


def pair_kernel(which, first, count, make, chained, *refs):
    refs = list(refs)

    def take(number):
        return [refs.pop(0) for _ in range(number)]

    dst, live, scale, focal, query_t, embed, out_w, head_w, depth, packed = take(10)
    keys, values_t, key_w, value_wt, total_in = None, None, None, None, None
    if make:
        key_w, value_wt = take(2)
    else:
        keys, values_t = take(2)
    if chained:
        total_in = take(2)[0]
    pair_tokens, sent, total_out = take(3)
    if make:
        keys, values_t = take(2)
    mixed_t, rows_out, sems = take(3)
    zeros = None if chained else take(1)[0]
    tokens, width = embed.shape
    patch = depth.shape[1]
    slots = pair_tokens.shape[0]
    ids = neighbours()
    own, target = ids[0], ids[which]
    hits = [(dst[slot] == target) & (slot < live[0]) for slot in range(slots)]
    dead = [slot >= live[0] for slot in range(slots)]

    def clear(slot):
        return pltpu.make_async_copy(zeros, pair_tokens.at[slot], sems.at[slots + slot])

    def write(slot):
        place = pair_tokens.at[slot, pl.ds(first, count)]
        return pltpu.make_async_copy(rows_out, place, sems.at[slot])

    if not chained:
        zeros[...] = jnp.zeros_like(zeros)
        for slot in range(slots):
            pl.when(dead[slot])(lambda slot=slot: clear(slot).start())
    if make:
        memory = packed[:, :width]
        keys[...] = matmul(memory, key_w[...]).astype(BF16)
        values_t[...] = matmul(value_wt[...], memory, 1, 1).astype(BF16)
    attention(query_t, keys, values_t, mixed_t, first, count, 3)
    rows = 256 if count % 256 == 0 else 128
    weight = jnp.float32(0.0)
    for slot in range(slots):
        weight = weight + jnp.where(hits[slot], 1.0, 0.0)
    shift = scale[own] - scale[target]
    tilt = focal[own] - focal[target]
    for start in range(0, count, rows):
        part = pl.ds(start, rows)
        whole = pl.ds(first + start, rows)
        attended = matmul(mixed_t[:, part], out_w[...], 0, 0)
        value = (embed[whole, :].astype(F32) + attended).astype(BF16)
        rows_out[part, :] = value
        head = matmul(value, head_w[...])
        logit = head[:, patch:]
        soft = jnp.maximum(logit, 0.0) + jnp.log1p(jnp.exp(-jnp.abs(logit)))
        confidence = weight * (0.1 + soft)
        ramp = ramp_of(first + start, rows, patch, tokens * patch)
        other = packed[whole, width:].astype(F32)
        resid = depth[whole, :] - other + shift + tilt * ramp - head[:, :patch]
        moved = confidence * resid
        sent[0, part, :] = moved.astype(BF16)
        sent[1, part, :] = confidence.astype(BF16)
        total_out[part, :] = total_in[whole, :] + moved if chained else moved
    for slot in range(slots):
        pl.when(hits[slot])(lambda slot=slot: write(slot).start())
    for slot in range(slots):
        pl.when(hits[slot])(lambda slot=slot: write(slot).wait())
    if not chained:
        for slot in range(slots):
            pl.when(dead[slot])(lambda slot=slot: clear(slot).wait())


def pair_stage(which, first, count, common, packed, weights, chain, made=None, keep=False):
    tokens, width = common[5].shape
    patch = common[8].shape[1]
    slots = common[0].shape[0]
    make, chained = made is None, chain is not None
    operands = [*common, packed, *(weights if make else made)]
    specs = [SMEM] * 4 + [VMEM] * 8
    if chained:
        operands += [chain[1], chain[0]]
        specs += [VMEM, HBM]
    kept = [jax.ShapeDtypeStruct((tokens, width), BF16), jax.ShapeDtypeStruct((width, tokens), BF16)]
    scratch = [] if keep or not make else [pltpu.VMEM((tokens, width), BF16), pltpu.VMEM((width, tokens), BF16)]
    scratch += [
        pltpu.VMEM((width, count), BF16),
        pltpu.VMEM((count, width), BF16),
        pltpu.SemaphoreType.DMA((2 * slots,)),
    ]
    if not chained:
        scratch.append(pltpu.VMEM((tokens, width), BF16))

    def body(*refs):
        pair_kernel(which, first, count, make, chained, *refs)

    return pl.pallas_call(
        body,
        in_specs=specs,
        out_specs=(HBM, VMEM, VMEM) + ((VMEM, VMEM) if keep else ()),
        out_shape=(
            jax.ShapeDtypeStruct((slots, tokens, width), BF16),
            jax.ShapeDtypeStruct((2, count, patch), BF16),
            jax.ShapeDtypeStruct((count, patch), F32),
        )
        + (tuple(kept) if keep else ()),
        scratch_shapes=scratch,
        input_output_aliases={len(operands) - 1: 0} if chained else {},
        compiler_params=params(),
    )(*operands)


def align_kernel(scale, focal, depth, *refs):
    totals, out_x, in_x = refs[0:2], refs[2:4], refs[4:6]
    out_p, out_o, in_p, in_o = refs[6:10]
    base, change, poses, grads = refs[10:]
    tokens, patch = depth.shape
    pixels = tokens * patch
    rows = 64
    half = tokens // 2

    def wide(ref, index, start):
        return ref[index, pl.ds(start, rows), :].astype(F32)

    def fold(value):
        return jnp.sum(value.reshape(rows // 8, 8, patch), axis=0)

    plain = jnp.zeros((8, patch), F32)
    slope = jnp.zeros((8, patch), F32)
    for start in range(0, tokens, rows):
        piece, local_start = start // half, start % half
        grad = totals[piece][pl.ds(local_start, rows), :] - wide(in_x[piece], 0, local_start)
        grad = grad - wide(in_p, 0, start) - wide(in_o, 0, start)
        grads[pl.ds(start, rows), :] = grad
        plain = plain + fold(grad)
        slope = slope + fold(grad * ramp_of(start, rows, patch, pixels))
    plain = jnp.sum(plain) / pixels
    slope = jnp.sum(slope) / pixels
    sums = [jnp.zeros((8, patch), F32) for _ in range(8)]
    for start in range(0, tokens, rows):
        part = pl.ds(start, rows)
        piece, local_start = start // half, start % half
        grad = grads[part, :]
        ramp = ramp_of(start, rows, patch, pixels)
        delta = -STEP * (grad + plain + slope * ramp)
        change[part, :] = delta.astype(BF16)
        links = [
            wide(out_p, 1, start) + wide(in_p, 1, start),
            wide(out_o, 1, start) + wide(in_o, 1, start),
            wide(out_x[piece], 1, local_start),
            wide(in_x[piece], 1, local_start),
        ]
        shares = [link * delta for link in links]
        base[part, :] = depth[part, :] - STEP * (
            2.0 * grad + (shares[0] + shares[1] + shares[2] + shares[3])
        )
        for index in range(4):
            sums[index] = sums[index] + fold(shares[index])
            sums[index + 4] = sums[index + 4] + fold(shares[index] * ramp)
    sums = [jnp.sum(value) / pixels for value in sums]
    ids = neighbours()
    lane = lax.broadcasted_iota(jnp.int32, (1, poses.shape[1]), 1)

    def spread(start, first, parts):
        own = start - STEP * (2.0 * first + (parts[0] + parts[1] + parts[2] + parts[3]))
        row = jnp.where(lane == ids[0], own, 0.0)
        for index in range(4):
            row = row + jnp.where(lane == ids[index + 1], STEP * parts[index], 0.0)
        return row

    poses[0:1, :] = spread(scale[ids[0]], plain, sums[:4])
    poses[1:2, :] = spread(focal[ids[0]], slope, sums[4:])


def align_stage(scale, focal, depth, totals, out_x, in_x, outs, ins):
    tokens, patch = depth.shape
    return pl.pallas_call(
        align_kernel,
        in_specs=[SMEM, SMEM] + [VMEM] * 11,
        out_specs=(VMEM, VMEM, VMEM),
        out_shape=(
            jax.ShapeDtypeStruct((tokens, patch), F32),
            jax.ShapeDtypeStruct((tokens, patch), BF16),
            jax.ShapeDtypeStruct((2, scale.shape[0]), F32),
        ),
        scratch_shapes=[pltpu.VMEM((tokens, patch), F32)],
        compiler_params=params(),
        name="align_stage",
    )(scale, focal, depth, *totals, *out_x, *in_x, *outs, *ins)


def final_kernel(base, *refs):
    out_x, in_x = refs[0:2], refs[2:4]
    out_p, out_o, in_p, in_o, change_p, change_o, change_b, change_n, result = refs[4:]
    tokens, _ = base.shape
    rows = 64
    half = tokens // 2

    def wide(ref, index, start):
        return ref[index, pl.ds(start, rows), :].astype(F32)

    for start in range(0, tokens, rows):
        part = pl.ds(start, rows)
        piece, local_start = start // half, start % half
        step = (wide(out_p, 1, start) + wide(in_p, 1, start)) * change_p[part, :].astype(F32)
        step += (wide(out_o, 1, start) + wide(in_o, 1, start)) * change_o[part, :].astype(F32)
        step += wide(out_x[piece], 1, local_start) * change_b[part, :].astype(F32)
        step += wide(in_x[piece], 1, local_start) * change_n[part, :].astype(F32)
        result[part, :] = base[part, :] + STEP * step


def final_stage(base, out_x, in_x, outs, ins, changes):
    return pl.pallas_call(
        final_kernel,
        in_specs=[VMEM] * 13,
        out_specs=VMEM,
        out_shape=jax.ShapeDtypeStruct(base.shape, F32),
        compiler_params=params(),
        name="final_stage",
    )(base, *out_x, *in_x, *outs, *ins, *changes)


def swap_inner(value):
    return lax.ppermute(value, "img", [(i, i ^ 1) for i in range(lax.axis_size("img"))])


def swap_outer(value):
    pairs = [(i, i + 1) for i in range(1, lax.axis_size("img") - 1, 2)]
    return lax.ppermute(value, "img", pairs + [(b, a) for a, b in pairs])


def along(value, by):
    count = lax.axis_size("group")
    return lax.ppermute(value, "group", [(i, (i + by) % count) for i in range(count)])


def local(
    enc_tokens,
    embed_weight,
    embed_bias,
    query_gain,
    memory_gain,
    query_weight,
    key_weight,
    value_weight,
    out_weight,
    head_weight,
    pair_dst,
    pair_count,
    depth,
    scale,
    focal,
):
    tokens = enc_tokens.shape[1]
    half = tokens // 2
    depth_now = depth[0]
    embed, packed = embed_stage(enc_tokens[0], embed_weight, embed_bias, memory_gain, depth_now)
    packed_x = along(packed, 1)
    packed_o = swap_outer(packed)
    packed_p = swap_inner(packed)
    query_t, value_wt = query_stage(embed, query_gain, query_weight, value_weight)
    common = (pair_dst, pair_count, scale, focal, query_t, embed, out_weight, head_weight, depth_now)
    weights = (key_weight, value_wt)
    tokens_p, sent_p, total_p = pair_stage(1, 0, tokens, common, packed_p, weights, None)
    in_p = swap_inner(sent_p)
    tokens_o, sent_o, total_o = pair_stage(
        2, 0, tokens, common, packed_o, weights, (tokens_p, total_p)
    )
    in_o = swap_outer(sent_o)
    tokens_a, sent_a, total_a, *made = pair_stage(
        3, 0, half, common, packed_x, weights, (tokens_o, total_o), keep=True
    )
    in_a = along(sent_a, -1)
    tokens_b, sent_b, total_b = pair_stage(
        3, half, half, common, packed_x, weights, (tokens_a, total_o), made=made
    )
    in_b = along(sent_b, -1)
    out_x, in_x, outs, ins = (sent_a, sent_b), (in_a, in_b), (sent_p, sent_o), (in_p, in_o)
    base, change, poses = align_stage(scale, focal, depth_now, (total_a, total_b), out_x, in_x, outs, ins)
    changes = (swap_inner(change), swap_outer(change), along(change, 1), along(change, -1))
    for axis, masks in (("img", (1, 2, 6, 8, 24)), ("group", (1, 3))):
        for mask in masks:
            pairs = [(i, i ^ mask) for i in range(lax.axis_size(axis))]
            poses = poses + lax.ppermute(poses, axis, pairs)
    depth_out = final_stage(base, out_x, in_x, outs, ins, changes)
    return (tokens_b, depth_out[None], poses[0], poses[1])


def solution(mesh):
    whole = P(("group", "img"), None, None)
    line = P(("group", "img"))
    return jax.shard_map(
        local,
        mesh=mesh,
        in_specs=(whole, *[P()] * 9, line, line, whole, P(), P()),
        out_specs=(whole, whole, P(), P()),
        check_vma=False,
    )
```

time: 159 us -> 129 us (0.81); the launches traced: 159 us -> 127 us
  Pallas kernels: 67.7 us -> 53 us
  other arithmetic: 10.4 us -> 0.02 us
  between operations: 8.97 us -> 1.58 us
  starting transfers between devices: 27.8 us -> 33.2 us
  local copies, waits for them, and re-layouts: 10.3 us -> 5.89 us
  matrix products: 3.48 us -> 0 us
  waiting for transfers between devices: 30.2 us -> 33 us
    pallas_call x5 -> x8, Pallas kernels: 67.7 us -> 53 us  [the longest x4 44.2 us: pair_stage(): pl.pallas_call(body, in_specs=specs, out_specs=(HBM, VMEM, VMEM) + ((VMEM...]
    ppermute x10, starting transfers between devices: 18.4 us -> 25.5 us  [the longest x7 19 us: local(): poses = poses + lax.ppermute(poses, axis, pairs)]
    ppermute x4 -> x5, waiting for transfers between devices: 12.4 us -> 19.3 us  [along(): lax.ppermute(value, 'group', [(i, (i + by) % count) for i in range(count)])]
    another operation x4 -> x0, other arithmetic: 5.53 us -> none  [the longest x3 3.69 us: stage(): terms = jnp.stack([jnp.sum(hits.astype(F32)), shift, tilt])]
    ppermute x10, waiting for transfers between devices: 17.8 us -> 13.6 us  [the longest x7 13.6 us: local(): poses = poses + lax.ppermute(poses, axis, pairs)]
    broadcast_in_dim x3 -> x0, local copies, waits for them, and re-layouts: 3.91 us -> none  [the longest x1 1.36 us: local(): embed_bias[None, :]]
    dot_general x1 -> x0, matrix products: 3.48 us -> none  [matmul(): lax.dot_general(a, b, (((left,), (right,)), ((), ())), preferred_element_...]
    broadcast_in_dim x1 -> x0, other arithmetic: 2.94 us -> none  [local(): return (tokens_x, depth_out[None], poses[0], poses[1])]
  transfers between devices with their start and end apart: 17 -> 18, of which waited for: 8 -> 9; matrix products, arithmetic and copies ran while one was open for 10% -> 0% of each run, Pallas kernels for 23% -> 37%
where the time goes in v2:
time: 129 us; the launch traced here: 127 us
  Pallas kernels  53 us (41%)
  starting transfers between devices  33.2 us (26%)
  waiting for transfers between devices  33 us (26%)
  local copies, waits for them, and re-layouts  5.89 us (5%)
  between operations  1.58 us (1%)
    pallas_call x4, Pallas kernels, pair_stage(): pl.pallas_call(body, in_specs=specs, out_specs=(HBM, VMEM, VMEM) + ((VMEM...  44.2 us
    ppermute x5, waiting for transfers between devices, along(): lax.ppermute(value, 'group', [(i, (i + by) % count) for i in range(count)])  19.3 us
    ppermute x7, starting transfers between devices, local(): poses = poses + lax.ppermute(poses, axis, pairs)  19 us
    ppermute x7, waiting for transfers between devices, local(): poses = poses + lax.ppermute(poses, axis, pairs)  13.6 us
    ppermute x3, starting transfers between devices, swap_inner(): lax.ppermute(value, 'img', [(i, i ^ 1) for i in range(lax.axis_size('img'...  6.45 us
    ppermute x5, starting transfers between devices, along(): lax.ppermute(value, 'group', [(i, (i + by) % count) for i in range(count)])  5.52 us
    unnamed x30, local copies, waits for them, and re-layouts  5.37 us
  transfers between devices with their start and end apart: 18, of which 9 were waited for; matrix products, arithmetic and copies ran while one was open for 0% of the time, Pallas kernels for 37%

profile of v2, /device:TPU:6, one launch (start us, length us, event | category | flops | bytes accessed | tf_op | source)
XLA Modules:
  0.0 126.6 jit_solution(15034666157919826412)
XLA Ops:
  6.0 2.5 %embed_stage.1 = (bf16[768,768]{1,0:T(8,128)(2,1)S(1)}, bf16[768,1024]{1,0:T(8,128)(2,1)S(1)}) custom-call(bf16[768,1024]{1,0:T(8,128)(2,1)S(1)} %bitcast.13, bf16[1024,768]{1,0:T(8,128)(2,1)S(1)} %copy-done.6, f32[768]{0:T(1024)S(1)} %copy-done.12, f32[768]{0:T(1024)S(1)} %copy-done.13, f32[768,256]{1,0:T(8,128)S(1)} %bitcast.7), custom_call_target="tpu_custom_call" | custom-call | tf_op jit(solution)/shard_map/embed_stage/pallas_call | solution.py:67
  10.5 2.5 %query_stage.1 = (bf16[768,768]{1,0:T(8,128)(2,1)S(1)}, bf16[768,768]{1,0:T(8,128)(2,1)S(1)}) custom-call(bf16[768,768]{1,0:T(8,128)(2,1)S(1)} %get-tuple-element.25.embed.refs_5_, f32[768]{0:T(1024)S(1)} %copy-done.14, bf16[768,768]{1,0:T(8,128)(2,1)S(1)} %copy-done.7, bf16[768,768]{1,0:T(8,128)(2,1)S(1)} %copy-done.8), custom_call_target="tpu_custom_call" | custom-call | tf_op jit(solution)/shard_map/query_stage/pallas_call | solution.py:92
  13.1 14.6 %shard_map.174 = (bf16[4,768,768]{2,1,0:T(8,128)(2,1)}, bf16[2,768,256]{2,1,0:T(8,128)(2,1)S(1)}, f32[768,256]{1,0:T(8,128)S(1)}) custom-call(s32[4]{0:T(128)S(1)} %copy-done.11, s32[1]{0:T(128)S(6)} %copy.25.refs_1_, f32[128]{0:T(128)S(1)} %copy-done.9, f32[128]{0:T(128)S(1)} %copy-done.10, bf16[768,768]{1,0:T(8,128)(2,1)S(1)} %get-tuple-element.26.refs_4_, ...), custom_call_target="tpu_custom_call" | custom-call | tf_op jit(solution)/shard_map/pallas_call | solution.py:233
  27.6 13.6 %shard_map.175 = (bf16[4,768,768]{2,1,0:T(8,128)(2,1)}, bf16[2,768,256]{2,1,0:T(8,128)(2,1)S(1)}, f32[768,256]{1,0:T(8,128)S(1)}) custom-call(s32[4]{0:T(128)S(1)} %copy-done.11, s32[1]{0:T(128)S(6)} %copy.25.refs_1_, f32[128]{0:T(128)S(1)} %copy-done.9, f32[128]{0:T(128)S(1)} %copy-done.10, ...), custom_call_target="tpu_custom_call", output_to_operand_aliasing={{0}: (13, {})} | custom-call | tf_op jit(solution)/shard_map/pallas_call | solution.py:233
  41.9 6.3 %collective-permute-start.5 = (bf16[2,768,256]{2,1,0:T(8,128)(2,1)S(1)}, bf16[2,768,256]{2,1,0:T(8,128)(2,1)S(1)}, u32[]{:S(2)}, u32[]{:S(2)}) collective-permute-start(bf16[2,768,256]{2,1,0:T(8,128)(2,1)S(1)} %get-tuple-element.41.refs_6_.refs_4_), channel_id=1, source_target_pairs={{0,1},{1,0},{2,3},{3,2},{4,5},{5,4},{6,7},{7,6},{8,9},{9,8},{10,11... | collective-permute-start | bytes 2359304 | tf_op jit(solution)/shard_map/ppermute | solution.py:360
  48.2 9.0 %shard_map.176 = (bf16[4,768,768]{2,1,0:T(8,128)(2,1)}, bf16[2,384,256]{2,1,0:T(8,128)(2,1)S(1)}, f32[384,256]{1,0:T(8,128)S(1)}, bf16[768,768]{1,0:T(8,128)(2,1)S(1)}, bf16[768,768]{1,0:T(8,128)(2,1)S(1)}) custom-call(s32[4]{0:T(128)S(1)} %copy-done.11, s32[1]{0:T(128)S(6)} %copy.25.refs_1_, f32[128]{0:T(128)S(1)} %copy-done.9, ...), custom_call_target="tpu_custom_call", output_to_operand_aliasing={{0}: (13, {})} | custom-call | tf_op jit(solution)/shard_map/pallas_call | solution.py:233
  57.2 7.0 %shard_map.177 = (bf16[4,768,768]{2,1,0:T(8,128)(2,1)}, bf16[2,384,256]{2,1,0:T(8,128)(2,1)S(1)}, f32[384,256]{1,0:T(8,128)S(1)}) custom-call(s32[4]{0:T(128)S(1)} %copy-done.11, s32[1]{0:T(128)S(6)} %copy.25.refs_1_, f32[128]{0:T(128)S(1)} %copy-done.9, f32[128]{0:T(128)S(1)} %copy-done.10, ...), custom_call_target="tpu_custom_call", output_to_operand_aliasing={{0}: (13, {})} | custom-call | tf_op jit(solution)/shard_map/pallas_call | solution.py:233
  66.1 11.4 %collective-permute-done.4.refs_5_.refs_3_ = bf16[2,384,256]{2,1,0:T(8,128)(2,1)S(1)} collective-permute-done((bf16[2,384,256]{2,1,0:T(8,128)(2,1)S(1)}, bf16[2,384,256]{2,1,0:T(8,128)(2,1)S(1)}, u32[]{:S(2)}, u32[]{:S(2)}) %collective-permute-start.4) | collective-permute-done | bytes 393248 | tf_op jit(solution)/shard_map/ppermute | solution.py:370
  77.5 7.9 %collective-permute-done.3.refs_4_.refs_2_ = bf16[2,384,256]{2,1,0:T(8,128)(2,1)S(1)} collective-permute-done((bf16[2,384,256]{2,1,0:T(8,128)(2,1)S(1)}, bf16[2,384,256]{2,1,0:T(8,128)(2,1)S(1)}, u32[]{:S(2)}, u32[]{:S(2)}) %collective-permute-start.3) | collective-permute-done | bytes 393248 | tf_op jit(solution)/shard_map/ppermute | solution.py:370
  85.4 2.4 %align_stage.1 = (f32[768,256]{1,0:T(8,128)S(1)}, bf16[768,256]{1,0:T(8,128)(2,1)S(1)}, f32[2,128]{1,0:T(2,128)S(1)}) custom-call(f32[128]{0:T(128)S(1)} %copy-done.9, f32[128]{0:T(128)S(1)} %copy-done.10, f32[768,256]{1,0:T(8,128)S(1)} %bitcast.12, f32[384,256]{1,0:T(8,128)S(1)} %get-tuple-element.37.refs_0_, f32[384,256]{1,0:T(8,128)S(1)} %get-tuple-element.38.refs_1_, ...), custom_call_target="tpu_custom_call" | custom-call | tf_op jit(solution)/shard_map/align_stage/pallas_call | solution.py:313
  88.7 3.2 %collective-permute-start.9 = (bf16[768,256]{1,0:T(8,128)(2,1)S(1)}, bf16[768,256]{1,0:T(8,128)(2,1)S(1)}, u32[]{:S(2)}, u32[]{:S(2)}) collective-permute-start(bf16[768,256]{1,0:T(8,128)(2,1)S(1)} %get-tuple-element.44), channel_id=1, source_target_pairs={{0,32},{32,64},{64,96},{96,0},{1,33},{33,65},{65,97},{97,1},{2,34}... | collective-permute-start | bytes 1179656 | tf_op jit(solution)/shard_map/ppermute | solution.py:370
  91.9 2.3 %collective-permute-start.11 = (f32[2,128]{1,0:T(2,128)S(1)}, f32[2,128]{1,0:T(2,128)S(1)}, u32[]{:S(2)}, u32[]{:S(2)}) collective-permute-start(f32[2,128]{1,0:T(2,128)S(1)} %get-tuple-element.45), channel_id=1, source_target_pairs={{0,1},{1,0},{2,3},{3,2},{4,5},{5,4},{6,7},{7,6},{8,9},{9,8},{10,11... | collective-permute-start | bytes 3080 | tf_op jit(solution)/shard_map/ppermute | solution.py:420
  95.0 1.6 %collective-permute-start.12 = (f32[2,128]{1,0:T(2,128)S(1)}, f32[2,128]{1,0:T(2,128)S(1)}, u32[]{:S(2)}, u32[]{:S(2)}) collective-permute-start(f32[2,128]{1,0:T(2,128)S(1)} %add.21), channel_id=1, source_target_pairs={{0,2},{1,3},{2,0},{3,1},{4,6},{5,7},{6,4},{7,5},{8,10},{9,11},{10,... | collective-permute-start | bytes 3080 | tf_op jit(solution)/shard_map/ppermute | solution.py:420
  96.7 1.9 %collective-permute-done.12 = f32[2,128]{1,0:T(2,128)S(1)} collective-permute-done((f32[2,128]{1,0:T(2,128)S(1)}, f32[2,128]{1,0:T(2,128)S(1)}, u32[]{:S(2)}, u32[]{:S(2)}) %collective-permute-start.12) | collective-permute-done | bytes 1056 | tf_op jit(solution)/shard_map/ppermute | solution.py:420
  98.6 6.5 %collective-permute-start.13 = (f32[2,128]{1,0:T(2,128)S(1)}, f32[2,128]{1,0:T(2,128)S(1)}, u32[]{:S(2)}, u32[]{:S(2)}) collective-permute-start(f32[2,128]{1,0:T(2,128)S(1)} %add.22), channel_id=1, source_target_pairs={{0,6},{1,7},{2,4},{3,5},{4,2},{5,3},{6,0},{7,1},{8,14},{9,15},{10,... | collective-permute-start | bytes 3080 | tf_op jit(solution)/shard_map/ppermute | solution.py:420
  105.1 1.6 %collective-permute-done.13 = f32[2,128]{1,0:T(2,128)S(1)} collective-permute-done((f32[2,128]{1,0:T(2,128)S(1)}, f32[2,128]{1,0:T(2,128)S(1)}, u32[]{:S(2)}, u32[]{:S(2)}) %collective-permute-start.13) | collective-permute-done | bytes 1056 | tf_op jit(solution)/shard_map/ppermute | solution.py:420
  106.7 2.3 %collective-permute-start.14 = (f32[2,128]{1,0:T(2,128)S(1)}, f32[2,128]{1,0:T(2,128)S(1)}, u32[]{:S(2)}, u32[]{:S(2)}) collective-permute-start(f32[2,128]{1,0:T(2,128)S(1)} %add.23), channel_id=1, source_target_pairs={{0,8},{1,9},{2,10},{3,11},{4,12},{5,13},{6,14},{7,15},{8,0},{9,1},... | collective-permute-start | bytes 3080 | tf_op jit(solution)/shard_map/ppermute | solution.py:420
  109.0 1.6 %collective-permute-done.14 = f32[2,128]{1,0:T(2,128)S(1)} collective-permute-done((f32[2,128]{1,0:T(2,128)S(1)}, f32[2,128]{1,0:T(2,128)S(1)}, u32[]{:S(2)}, u32[]{:S(2)}) %collective-permute-start.14) | collective-permute-done | bytes 1056 | tf_op jit(solution)/shard_map/ppermute | solution.py:420
  110.5 4.2 %collective-permute-start.15 = (f32[2,128]{1,0:T(2,128)S(1)}, f32[2,128]{1,0:T(2,128)S(1)}, u32[]{:S(2)}, u32[]{:S(2)}) collective-permute-start(f32[2,128]{1,0:T(2,128)S(1)} %add.24), channel_id=1, source_target_pairs={{0,24},{1,25},{2,26},{3,27},{4,28},{5,29},{6,30},{7,31},{8,16},{9,... | collective-permute-start | bytes 3080 | tf_op jit(solution)/shard_map/ppermute | solution.py:420
  114.7 1.6 %collective-permute-done.15 = f32[2,128]{1,0:T(2,128)S(1)} collective-permute-done((f32[2,128]{1,0:T(2,128)S(1)}, f32[2,128]{1,0:T(2,128)S(1)}, u32[]{:S(2)}, u32[]{:S(2)}) %collective-permute-start.15) | collective-permute-done | bytes 1056 | tf_op jit(solution)/shard_map/ppermute | solution.py:420
  116.2 3.6 %collective-permute-done.16 = f32[2,128]{1,0:T(2,128)S(1)} collective-permute-done((f32[2,128]{1,0:T(2,128)S(1)}, f32[2,128]{1,0:T(2,128)S(1)}, u32[]{:S(2)}, u32[]{:S(2)}) %collective-permute-start.16) | collective-permute-done | bytes 1056 | tf_op jit(solution)/shard_map/ppermute | solution.py:420
  119.8 2.1 %collective-permute-start.17 = (f32[2,128]{1,0:T(2,128)S(1)}, f32[2,128]{1,0:T(2,128)S(1)}, u32[]{:S(2)}, u32[]{:S(2)}) collective-permute-start(f32[2,128]{1,0:T(2,128)S(1)} %add.26), channel_id=1, source_target_pairs={{0,96},{32,64},{64,32},{96,0},{1,97},{33,65},{65,33},{97,1},{2,98}... | collective-permute-start | bytes 3080 | tf_op jit(solution)/shard_map/ppermute | solution.py:420
  121.9 2.6 %collective-permute-done.17 = f32[2,128]{1,0:T(2,128)S(1)} collective-permute-done((f32[2,128]{1,0:T(2,128)S(1)}, f32[2,128]{1,0:T(2,128)S(1)}, u32[]{:S(2)}, u32[]{:S(2)}) %collective-permute-start.17) | collective-permute-done | bytes 1056 | tf_op jit(solution)/shard_map/ppermute | solution.py:420
  125.1 1.5 %final_stage.1 = f32[768,256]{1,0:T(8,128)} custom-call(f32[768,256]{1,0:T(8,128)S(1)} %get-tuple-element.43.base, bf16[2,384,256]{2,1,0:T(8,128)(2,1)S(1)} %get-tuple-element.39.refs_2_.refs_0_, bf16[2,384,256]{2,1,0:T(8,128)(2,1)S(1)} %get-tuple-element.40.refs_3_.refs_1_, bf16[2,384,256]{2,1,0:T(8,128)(2,1)S(1)} %collective-permute-done.3.refs_4_.refs_2_, ...), custom_call_target="tpu_custom_call" | custom-call | tf_op jit(solution)/shard_map/final_stage/pallas_call | solution.py:349
  (58 shorter events, 11.4 us)
Async XLA Ops:
  6.0 4.5 %copy-start.7 = (bf16[768,768]{1,0:T(8,128)(2,1)S(1)}, bf16[768,768]{1,0:T(8,128)(2,1)}, u32[]{:S(2)}) copy-start(bf16[768,768]{1,0:T(8,128)(2,1)} %query_w.1) | copy-start | bytes 3538948
  6.0 4.5 %copy-start.8 = (bf16[768,768]{1,0:T(8,128)(2,1)S(1)}, bf16[768,768]{1,0:T(8,128)(2,1)}, u32[]{:S(2)}) copy-start(bf16[768,768]{1,0:T(8,128)(2,1)} %value_w.1) | copy-start | bytes 3538948
  6.0 4.5 %copy-start.14 = (f32[768]{0:T(1024)S(1)}, f32[768]{0:T(1024)}, u32[]{:S(2)}) copy-start(f32[768]{0:T(1024)} %gain.1) | copy-start | bytes 9220
  6.0 7.0 %copy-start.4 = (bf16[768,768]{1,0:T(8,128)(2,1)S(1)}, bf16[768,768]{1,0:T(8,128)(2,1)}, u32[]{:S(2)}) copy-start(bf16[768,768]{1,0:T(8,128)(2,1)} %refs_10_.5) | copy-start | bytes 3538948
  8.5 4.5 %collective-permute-start.2 = (bf16[768,1024]{1,0:T(8,128)(2,1)S(1)}, bf16[768,1024]{1,0:T(8,128)(2,1)S(1)}, u32[]{:S(2)}, u32[]{:S(2)}) collective-permute-start(bf16[768,1024]{1,0:T(8,128)(2,1)S(1)} %get-tuple-element.27), channel_id=1, source_target_pairs={{0,1},{1,0},{2,3},{3,2},{4,5},{5,4},{6,7},{7,6},{8,9},{9,8},{10,11... | collective-permute-start | bytes 4718600 | tf_op jit(solution)/shard_map/ppermute | solution.py:360
  8.6 19.1 %collective-permute-start.1 = (bf16[768,1024]{1,0:T(8,128)(2,1)S(1)}, bf16[768,1024]{1,0:T(8,128)(2,1)S(1)}, u32[]{:S(2)}, u32[]{:S(2)}) collective-permute-start(bf16[768,1024]{1,0:T(8,128)(2,1)S(1)} %get-tuple-element.27), channel_id=1, source_target_pairs={{1,2},{3,4},{5,6},{7,8},{9,10},{11,12},{13,14},{15,16},{17,18},{19... | collective-permute-start | bytes 4718600 | tf_op jit(solution)/shard_map/ppermute | solution.py:365
  9.3 38.9 %collective-permute-start = (bf16[768,1024]{1,0:T(8,128)(2,1)S(1)}, bf16[768,1024]{1,0:T(8,128)(2,1)S(1)}, u32[]{:S(2)}, u32[]{:S(2)}) collective-permute-start(bf16[768,1024]{1,0:T(8,128)(2,1)S(1)} %get-tuple-element.27), channel_id=1, source_target_pairs={{0,32},{32,64},{64,96},{96,0},{1,33},{33,65},{65,97},{97,1},{2,34}... | collective-permute-start | bytes 4718600 | tf_op jit(solution)/shard_map/ppermute | solution.py:370
  10.4 2.6 %copy-start.1 = (f32[1,768,256]{2,1,0:T(8,128)S(1)}, f32[1,768,256]{2,1,0:T(8,128)}, u32[]{:S(2)}) copy-start(f32[1,768,256]{2,1,0:T(8,128)} %param.27) | copy-start | bytes 2359300
  10.5 2.6 %copy-start.2 = (bf16[768,768]{1,0:T(8,128)(2,1)S(1)}, bf16[768,768]{1,0:T(8,128)(2,1)}, u32[]{:S(2)}) copy-start(bf16[768,768]{1,0:T(8,128)(2,1)} %refs_6_.7) | copy-start | bytes 3538948
  41.2 44.2 %collective-permute-start.6 = (bf16[2,768,256]{2,1,0:T(8,128)(2,1)S(1)}, bf16[2,768,256]{2,1,0:T(8,128)(2,1)S(1)}, u32[]{:S(2)}, u32[]{:S(2)}) collective-permute-start(bf16[2,768,256]{2,1,0:T(8,128)(2,1)S(1)} %get-tuple-element.42.refs_7_.refs_5_), channel_id=1, source_target_pairs={{1,2},{3,4},{5,6},{7,8},{9,10},{11,12},{13,14},{15,16},{17,18},{19... | collective-permute-start | bytes 2359304 | tf_op jit(solution)/shard_map/ppermute | solution.py:365
  41.9 43.5 %collective-permute-start.5 = (bf16[2,768,256]{2,1,0:T(8,128)(2,1)S(1)}, bf16[2,768,256]{2,1,0:T(8,128)(2,1)S(1)}, u32[]{:S(2)}, u32[]{:S(2)}) collective-permute-start(bf16[2,768,256]{2,1,0:T(8,128)(2,1)S(1)} %get-tuple-element.41.refs_6_.refs_4_), channel_id=1, source_target_pairs={{0,1},{1,0},{2,3},{3,2},{4,5},{5,4},{6,7},{7,6},{8,9},{9,8},{10,11... | collective-permute-start | bytes 2359304 | tf_op jit(solution)/shard_map/ppermute | solution.py:360
  64.3 13.3 %collective-permute-start.4 = (bf16[2,384,256]{2,1,0:T(8,128)(2,1)S(1)}, bf16[2,384,256]{2,1,0:T(8,128)(2,1)S(1)}, u32[]{:S(2)}, u32[]{:S(2)}) collective-permute-start(bf16[2,384,256]{2,1,0:T(8,128)(2,1)S(1)} %get-tuple-element.40.refs_3_.refs_1_), channel_id=1, source_target_pairs={{0,96},{32,0},{64,32},{96,64},{1,97},{33,1},{65,33},{97,65},{2,98}... | collective-permute-start | bytes 1179656 | tf_op jit(solution)/shard_map/ppermute | solution.py:370
  65.2 20.2 %collective-permute-start.3 = (bf16[2,384,256]{2,1,0:T(8,128)(2,1)S(1)}, bf16[2,384,256]{2,1,0:T(8,128)(2,1)S(1)}, u32[]{:S(2)}, u32[]{:S(2)}) collective-permute-start(bf16[2,384,256]{2,1,0:T(8,128)(2,1)S(1)} %get-tuple-element.39.refs_2_.refs_0_), channel_id=1, source_target_pairs={{0,96},{32,0},{64,32},{96,64},{1,97},{33,1},{65,33},{97,65},{2,98}... | collective-permute-start | bytes 1179656 | tf_op jit(solution)/shard_map/ppermute | solution.py:370
  87.9 37.3 %collective-permute-start.10 = (bf16[768,256]{1,0:T(8,128)(2,1)S(1)}, bf16[768,256]{1,0:T(8,128)(2,1)S(1)}, u32[]{:S(2)}, u32[]{:S(2)}) collective-permute-start(bf16[768,256]{1,0:T(8,128)(2,1)S(1)} %get-tuple-element.44), channel_id=1, source_target_pairs={{0,96},{32,0},{64,32},{96,64},{1,97},{33,1},{65,33},{97,65},{2,98}... | collective-permute-start | bytes 1179656 | tf_op jit(solution)/shard_map/ppermute | solution.py:370
  87.9 37.2 %collective-permute-start.7 = (bf16[768,256]{1,0:T(8,128)(2,1)S(1)}, bf16[768,256]{1,0:T(8,128)(2,1)S(1)}, u32[]{:S(2)}, u32[]{:S(2)}) collective-permute-start(bf16[768,256]{1,0:T(8,128)(2,1)S(1)} %get-tuple-element.44), channel_id=1, source_target_pairs={{0,1},{1,0},{2,3},{3,2},{4,5},{5,4},{6,7},{7,6},{8,9},{9,8},{10,11... | collective-permute-start | bytes 1179656 | tf_op jit(solution)/shard_map/ppermute | solution.py:360
  88.0 37.1 %collective-permute-start.8 = (bf16[768,256]{1,0:T(8,128)(2,1)S(1)}, bf16[768,256]{1,0:T(8,128)(2,1)S(1)}, u32[]{:S(2)}, u32[]{:S(2)}) collective-permute-start(bf16[768,256]{1,0:T(8,128)(2,1)S(1)} %get-tuple-element.44), channel_id=1, source_target_pairs={{1,2},{3,4},{5,6},{7,8},{9,10},{11,12},{13,14},{15,16},{17,18},{19... | collective-permute-start | bytes 1179656 | tf_op jit(solution)/shard_map/ppermute | solution.py:365
  88.7 36.4 %collective-permute-start.9 = (bf16[768,256]{1,0:T(8,128)(2,1)S(1)}, bf16[768,256]{1,0:T(8,128)(2,1)S(1)}, u32[]{:S(2)}, u32[]{:S(2)}) collective-permute-start(bf16[768,256]{1,0:T(8,128)(2,1)S(1)} %get-tuple-element.44), channel_id=1, source_target_pairs={{0,32},{32,64},{64,96},{96,0},{1,33},{33,65},{65,97},{97,1},{2,34}... | collective-permute-start | bytes 1179656 | tf_op jit(solution)/shard_map/ppermute | solution.py:370
  91.9 3.1 %collective-permute-start.11 = (f32[2,128]{1,0:T(2,128)S(1)}, f32[2,128]{1,0:T(2,128)S(1)}, u32[]{:S(2)}, u32[]{:S(2)}) collective-permute-start(f32[2,128]{1,0:T(2,128)S(1)} %get-tuple-element.45), channel_id=1, source_target_pairs={{0,1},{1,0},{2,3},{3,2},{4,5},{5,4},{6,7},{7,6},{8,9},{9,8},{10,11... | collective-permute-start | bytes 3080 | tf_op jit(solution)/shard_map/ppermute | solution.py:420
  95.0 3.6 %collective-permute-start.12 = (f32[2,128]{1,0:T(2,128)S(1)}, f32[2,128]{1,0:T(2,128)S(1)}, u32[]{:S(2)}, u32[]{:S(2)}) collective-permute-start(f32[2,128]{1,0:T(2,128)S(1)} %add.21), channel_id=1, source_target_pairs={{0,2},{1,3},{2,0},{3,1},{4,6},{5,7},{6,4},{7,5},{8,10},{9,11},{10,... | collective-permute-start | bytes 3080 | tf_op jit(solution)/shard_map/ppermute | solution.py:420
  98.6 8.1 %collective-permute-start.13 = (f32[2,128]{1,0:T(2,128)S(1)}, f32[2,128]{1,0:T(2,128)S(1)}, u32[]{:S(2)}, u32[]{:S(2)}) collective-permute-start(f32[2,128]{1,0:T(2,128)S(1)} %add.22), channel_id=1, source_target_pairs={{0,6},{1,7},{2,4},{3,5},{4,2},{5,3},{6,0},{7,1},{8,14},{9,15},{10,... | collective-permute-start | bytes 3080 | tf_op jit(solution)/shard_map/ppermute | solution.py:420
  106.7 3.8 %collective-permute-start.14 = (f32[2,128]{1,0:T(2,128)S(1)}, f32[2,128]{1,0:T(2,128)S(1)}, u32[]{:S(2)}, u32[]{:S(2)}) collective-permute-start(f32[2,128]{1,0:T(2,128)S(1)} %add.23), channel_id=1, source_target_pairs={{0,8},{1,9},{2,10},{3,11},{4,12},{5,13},{6,14},{7,15},{8,0},{9,1},... | collective-permute-start | bytes 3080 | tf_op jit(solution)/shard_map/ppermute | solution.py:420
  110.5 5.7 %collective-permute-start.15 = (f32[2,128]{1,0:T(2,128)S(1)}, f32[2,128]{1,0:T(2,128)S(1)}, u32[]{:S(2)}, u32[]{:S(2)}) collective-permute-start(f32[2,128]{1,0:T(2,128)S(1)} %add.24), channel_id=1, source_target_pairs={{0,24},{1,25},{2,26},{3,27},{4,28},{5,29},{6,30},{7,31},{8,16},{9,... | collective-permute-start | bytes 3080 | tf_op jit(solution)/shard_map/ppermute | solution.py:420
  116.2 3.6 %collective-permute-start.16 = (f32[2,128]{1,0:T(2,128)S(1)}, f32[2,128]{1,0:T(2,128)S(1)}, u32[]{:S(2)}, u32[]{:S(2)}) collective-permute-start(f32[2,128]{1,0:T(2,128)S(1)} %add.25), channel_id=1, source_target_pairs={{0,32},{32,0},{64,96},{96,64},{1,33},{33,1},{65,97},{97,65},{2,34}... | collective-permute-start | bytes 3080 | tf_op jit(solution)/shard_map/ppermute | solution.py:420
  119.8 4.8 %collective-permute-start.17 = (f32[2,128]{1,0:T(2,128)S(1)}, f32[2,128]{1,0:T(2,128)S(1)}, u32[]{:S(2)}, u32[]{:S(2)}) collective-permute-start(f32[2,128]{1,0:T(2,128)S(1)} %add.26), channel_id=1, source_target_pairs={{0,96},{32,64},{64,32},{96,0},{1,97},{33,65},{65,33},{97,1},{2,98}... | collective-permute-start | bytes 3080 | tf_op jit(solution)/shard_map/ppermute | solution.py:420
  (9 other events, 15.5 us)

commit v3 on v2

v3 whole, which is shorter than its diff:
```python
import jax
import jax.numpy as jnp
from jax import lax
from jax.experimental import pallas as pl
from jax.experimental.pallas import tpu as pltpu
from jax.sharding import PartitionSpec as P

HEADS = 12
HEAD = 64
STEP = 0.1
FAST = 3
LOG2E = 1.4426950408889634
F32 = jnp.float32
BF16 = jnp.bfloat16


def matmul(a, b, left=1, right=0):
    return lax.dot_general(a, b, (((left,), (right,)), ((), ())), preferred_element_type=F32)


def ramp_of(start, rows, width, total):
    row = lax.broadcasted_iota(jnp.int32, (rows, width), 0) + start
    col = lax.broadcasted_iota(jnp.int32, (rows, width), 1)
    return 2.0 * ((row * width + col).astype(F32) + 0.5) / total - 1.0


def params(mebi=24):
    return pltpu.CompilerParams(vmem_limit_bytes=mebi << 20)


VMEM = pl.BlockSpec(memory_space=pltpu.VMEM)
SMEM = pl.BlockSpec(memory_space=pltpu.SMEM)
HBM = pl.BlockSpec(memory_space=pl.ANY)


def neighbours():
    group_count, img_count = lax.axis_size("group"), lax.axis_size("img")
    group, img = lax.axis_index("group"), lax.axis_index("img")
    base = group * img_count
    inner = base + img + 1 - 2 * (img % 2)
    outer = base + jnp.clip(img - 1 + 2 * (img % 2), 0, img_count - 1)
    back = (group + group_count - 1) % group_count * img_count + img
    ahead = (group + 1) % group_count * img_count + img
    return base + img, inner, outer, back, ahead


def normed(value, gain):
    value = value.astype(F32)
    center = value - jnp.mean(value, axis=-1, keepdims=True)
    spread = jnp.mean(center * center, axis=-1, keepdims=True)
    return (center * lax.rsqrt(spread + 1e-05) * gain).astype(BF16)


def embed_kernel(enc, weight, bias, memory_gain, depth, embed, rows_out, late, *scratch):
    enc_v, weight_v, depth_v, embed_v, rows_v, late_v, arrive, leave = scratch
    tokens = embed.shape[0]
    count = 3
    rows = tokens // count
    moves = [pltpu.make_async_copy(weight, weight_v, arrive.at[0])]
    for index in range(count):
        part = pl.ds(index * rows, rows)
        moves.append(pltpu.make_async_copy(enc.at[part], enc_v.at[part], arrive.at[index + 1]))
    moves.append(pltpu.make_async_copy(depth, depth_v, arrive.at[count + 1]))
    for move in moves:
        move.start()
    moves[0].wait()
    out = []
    for index in range(count):
        part = pl.ds(index * rows, rows)
        moves[index + 1].wait()
        value = (matmul(enc_v[part, :], weight_v[...]) + bias[...][None, :]).astype(BF16)
        embed_v[part, :] = value
        rows_v[part, :] = normed(value, memory_gain[...][None, :])
        for place, (source, target) in enumerate(((rows_v, rows_out), (embed_v, embed))):
            out.append(pltpu.make_async_copy(source.at[part], target.at[part], leave.at[index * 2 + place]))
            out[-1].start()
    moves[-1].wait()
    late_v[...] = depth_v[...].astype(BF16)
    out.append(pltpu.make_async_copy(late_v, late, leave.at[count * 2]))
    out[-1].start()
    for move in out:
        move.wait()


def embed_stage(enc, weight, bias, memory_gain, depth):
    tokens, width = enc.shape[0], weight.shape[1]
    patch = depth.shape[1]
    shapes = [(tokens, width), (tokens, width), (tokens, patch)]
    return pl.pallas_call(
        embed_kernel,
        in_specs=[HBM, HBM, VMEM, VMEM, HBM],
        out_specs=(HBM,) * 3,
        out_shape=tuple(jax.ShapeDtypeStruct(shape, BF16) for shape in shapes),
        scratch_shapes=[
            pltpu.VMEM(enc.shape, BF16),
            pltpu.VMEM(weight.shape, BF16),
            pltpu.VMEM(depth.shape, F32),
            *[pltpu.VMEM(shape, BF16) for shape in shapes],
            pltpu.SemaphoreType.DMA((5,)),
            pltpu.SemaphoreType.DMA((7,)),
        ],
        compiler_params=params(60),
        name="embed_stage",
    )(enc, weight, bias, memory_gain, depth)


def query_kernel(embed, gain, query_w, value_w, query_t, value_wt, peak):
    scaled = HEAD**-0.5 * LOG2E
    value_wt[...] = value_w[...].T
    rows = 256
    largest = jnp.float32(0.0)
    for start in range(0, embed.shape[0], rows):
        part = pl.ds(start, rows)
        value = normed(embed[part, :], gain[...][None, :])
        query = (matmul(query_w[...], value, 0, 1) * scaled).astype(BF16)
        query_t[:, part] = query
        query = query.astype(F32)
        norm = jnp.sum((query * query).reshape(HEADS, HEAD, rows), axis=1)
        largest = jnp.maximum(largest, jnp.max(norm))
    peak[...] = jnp.full(peak.shape, largest, F32)


def query_stage(embed, gain, query_w, value_w):
    return pl.pallas_call(
        query_kernel,
        in_specs=[VMEM] * 4,
        out_specs=(VMEM,) * 3,
        out_shape=(
            jax.ShapeDtypeStruct(embed.shape[::-1], BF16),
            jax.ShapeDtypeStruct(value_w.shape[::-1], BF16),
            jax.ShapeDtypeStruct((8, 128), F32),
        ),
        compiler_params=params(),
        name="query_stage",
    )(embed, gain, query_w, value_w)


def attention(query_t, keys, values_t, mixed_t, first, count, group, shifted):
    def scores(base, half):
        offset = pl.multiple_of(base + half * HEAD, HEAD)
        query = query_t[pl.ds(offset, HEAD), pl.ds(first, count)]
        blank = jnp.zeros_like(query)
        both = jnp.concatenate([query, blank] if half == 0 else [blank, query], axis=0)
        return matmul(keys[:, pl.ds(base, 2 * HEAD)], both), offset

    def finish(score, offset):
        if shifted:
            score = score - jnp.max(score, axis=0, keepdims=True)
        probs = jnp.exp2(score).astype(BF16)
        ones = jnp.ones((16, keys.shape[0]), BF16)
        stacked = jnp.concatenate([values_t[pl.ds(offset, HEAD), :], ones], axis=0)
        mixed = matmul(stacked, probs)
        mixed_t[pl.ds(offset, HEAD), :] = (mixed[:HEAD] * (1.0 / mixed[HEAD : HEAD + 1])).astype(BF16)

    def single(head, carry):
        base = pl.multiple_of(head // 2 * 2 * HEAD, 2 * HEAD)
        both = query_t[pl.ds(base, 2 * HEAD), pl.ds(first, count)]
        row = lax.broadcasted_iota(jnp.int32, both.shape, 0) // HEAD
        both = jnp.where(row == head % 2, both, jnp.zeros_like(both))
        finish(matmul(keys[:, pl.ds(base, 2 * HEAD)], both), pl.multiple_of(head * HEAD, HEAD))
        return carry

    def step(index, carry):
        pending = None
        for pair in range(group):
            base = pl.multiple_of((index * group + pair) * 2 * HEAD, 2 * HEAD)
            for half in range(2):
                current = scores(base, half)
                if pending is not None:
                    finish(*pending)
                pending = current
        finish(*pending)
        return carry

    if shifted:
        lax.fori_loop(0, HEADS, single, 0)
    else:
        lax.fori_loop(0, HEADS // 2 // group, step, 0)


def key_peak(keys):
    width = keys.shape[1]
    square = keys[...].astype(F32)
    square = (square * square).astype(BF16)
    row = lax.broadcasted_iota(jnp.int32, (width, 128), 0) // HEAD
    col = lax.broadcasted_iota(jnp.int32, (width, 128), 1)
    return jnp.max(matmul(square, jnp.where(row == col, 1.0, 0.0).astype(BF16)))


def pair_kernel(which, first, count, make, keep, chained, *refs):
    refs = list(refs)

    def take(number):
        return [refs.pop(0) for _ in range(number)]

    dst, live, scale, focal, query_t, peak, embed, out_w, head_w, depth = take(10)
    if make:
        packed, key_w, value_wt = take(3)
    else:
        keys, values_t, reach = take(3)
    if chained:
        take(1)
    pair_tokens, sent, moved_out = take(3)
    if make:
        keys, values_t = take(2)
        reach = take(1)[0] if keep else None
    mixed_t, rows_out, sems = take(3)
    zeros = None if chained else take(1)[0]
    tokens, _ = embed.shape
    patch = depth.shape[1]
    slots = pair_tokens.shape[0]
    ids = neighbours()
    own, target = ids[0], ids[which]
    hits = [(dst[slot] == target) & (slot < live[0]) for slot in range(slots)]
    dead = [slot >= live[0] for slot in range(slots)]

    def clear(slot):
        return pltpu.make_async_copy(zeros, pair_tokens.at[slot], sems.at[slots + slot])

    def write(slot):
        place = pair_tokens.at[slot, pl.ds(first, count)]
        return pltpu.make_async_copy(rows_out, place, sems.at[slot])

    if not chained:
        zeros[...] = jnp.zeros_like(zeros)
        for slot in range(slots):
            pl.when(dead[slot])(lambda slot=slot: clear(slot).start())
    if make:
        memory = packed[...]
        keys[...] = matmul(memory, key_w[...]).astype(BF16)
        values_t[...] = matmul(value_wt[...], memory, 1, 1).astype(BF16)
        largest = key_peak(keys)
        if keep:
            reach[...] = jnp.full(reach.shape, largest, F32)
    else:
        largest = jnp.max(reach[...])
    small = jnp.max(peak[...]) * largest <= 8000.0

    @pl.when(small)
    def _():
        attention(query_t, keys, values_t, mixed_t, first, count, FAST, False)

    @pl.when(jnp.logical_not(small))
    def _():
        attention(query_t, keys, values_t, mixed_t, first, count, 1, True)

    rows = 256 if count % 256 == 0 else 128
    weight = jnp.float32(0.0)
    for slot in range(slots):
        weight = weight + jnp.where(hits[slot], 1.0, 0.0)
    shift = scale[own] - scale[target]
    tilt = focal[own] - focal[target]
    for start in range(0, count, rows):
        part = pl.ds(start, rows)
        whole = pl.ds(first + start, rows)
        attended = matmul(mixed_t[:, part], out_w[...], 0, 0)
        value = (embed[whole, :].astype(F32) + attended).astype(BF16)
        rows_out[part, :] = value
        head = matmul(value, head_w[...])
        logit = head[:, patch:]
        soft = jnp.maximum(logit, 0.0) + jnp.log1p(jnp.exp(-jnp.abs(logit)))
        confidence = weight * (0.1 + soft)
        ramp = ramp_of(first + start, rows, patch, tokens * patch)
        moved = confidence * (depth[whole, :] + shift + tilt * ramp - head[:, :patch])
        sent[0, part, :] = moved.astype(BF16)
        sent[1, part, :] = confidence.astype(BF16)
        moved_out[part, :] = moved
        if sent.shape[0] == 3:
            sent[2, part, :] = depth[whole, :].astype(BF16)
    for slot in range(slots):
        pl.when(hits[slot])(lambda slot=slot: write(slot).start())
    for slot in range(slots):
        pl.when(hits[slot])(lambda slot=slot: write(slot).wait())
    if not chained:
        for slot in range(slots):
            pl.when(dead[slot])(lambda slot=slot: clear(slot).wait())


def pair_stage(which, first, count, common, source, chain=None, keep=False):
    tokens, width = common[6].shape
    patch = common[9].shape[1]
    slots = common[0].shape[0]
    chained = chain is not None
    make = source[0].shape[0] == tokens and source[2].shape == (width, width)
    operands = [*common, *source]
    specs = [SMEM] * 4 + [VMEM] * (len(operands) - 4)
    if chained:
        operands.append(chain)
        specs.append(HBM)
    kept = ((tokens, width), (width, tokens))
    scratch = [] if keep or not make else [pltpu.VMEM(shape, BF16) for shape in kept]
    scratch += [
        pltpu.VMEM((width, count), BF16),
        pltpu.VMEM((count, width), BF16),
        pltpu.SemaphoreType.DMA((2 * slots,)),
    ]
    if not chained:
        scratch.append(pltpu.VMEM((tokens, width), BF16))
    results = [
        jax.ShapeDtypeStruct((slots, tokens, width), BF16),
        jax.ShapeDtypeStruct((2 if which == 3 else 3, count, patch), BF16),
        jax.ShapeDtypeStruct((count, patch), F32),
    ]
    if keep:
        results += [jax.ShapeDtypeStruct(shape, BF16) for shape in kept]
        results.append(jax.ShapeDtypeStruct((8, 128), F32))

    def body(*refs):
        pair_kernel(which, first, count, make, keep, chained, *refs)

    return pl.pallas_call(
        body,
        in_specs=specs,
        out_specs=(HBM,) + (VMEM,) * (len(results) - 1),
        out_shape=tuple(results),
        scratch_shapes=scratch,
        input_output_aliases={len(operands) - 1: 0} if chained else {},
        compiler_params=params(),
    )(*operands)


def strip(pieces, start, rows, *index):
    for piece in pieces:
        height = piece.shape[-2]
        if start < height:
            return piece[(*index, pl.ds(start, rows), slice(None))].astype(F32)
        start -= height


def wide(pieces, index, start, rows):
    return strip(pieces, start, rows, index)


def align_kernel(scale, focal, depth, *refs):
    moved_x, (moved_o, moved_p), out_x, in_x = [refs[2 * index : 2 * index + 2] for index in range(4)]
    moved_o, moved_p = (moved_o,), (moved_p,)
    out_o, in_o, out_p, in_p, late = [refs[index : index + 1] for index in range(8, 13)]
    base, change, poses, grads = refs[13:]
    tokens, patch = depth.shape
    pixels = tokens * patch
    rows = 64

    def fold(value):
        return jnp.sum(value.reshape(rows // 8, 8, patch), axis=0)

    plain = jnp.zeros((8, patch), F32)
    slope = jnp.zeros((8, patch), F32)
    for start in range(0, tokens, rows):
        own = depth[pl.ds(start, rows), :]
        grad = jnp.zeros_like(own)
        for pieces in (moved_x, moved_o, moved_p):
            grad = grad + strip(pieces, start, rows)
        for pieces in (in_x, in_o, in_p):
            grad = grad - wide(pieces, 0, start, rows) + wide(pieces, 1, start, rows) * own
        others = (strip(late, start, rows), wide(in_o, 2, start, rows), wide(in_p, 2, start, rows))
        for pieces, other in zip((out_x, out_o, out_p), others):
            grad = grad - wide(pieces, 1, start, rows) * other
        grads[pl.ds(start, rows), :] = grad
        plain = plain + fold(grad)
        slope = slope + fold(grad * ramp_of(start, rows, patch, pixels))
    plain = jnp.sum(plain) / pixels
    slope = jnp.sum(slope) / pixels
    sums = [jnp.zeros((8, patch), F32) for _ in range(8)]
    for start in range(0, tokens, rows):
        part = pl.ds(start, rows)
        grad = grads[part, :]
        ramp = ramp_of(start, rows, patch, pixels)
        delta = -STEP * (grad + plain + slope * ramp)
        change[part, :] = delta.astype(BF16)
        links = [
            wide(out_p, 1, start, rows) + wide(in_p, 1, start, rows),
            wide(out_o, 1, start, rows) + wide(in_o, 1, start, rows),
            wide(out_x, 1, start, rows),
            wide(in_x, 1, start, rows),
        ]
        shares = [link * delta for link in links]
        base[part, :] = depth[part, :] - STEP * (
            2.0 * grad + (shares[0] + shares[1] + shares[2] + shares[3])
        )
        for index in range(4):
            sums[index] = sums[index] + fold(shares[index])
            sums[index + 4] = sums[index + 4] + fold(shares[index] * ramp)
    sums = [jnp.sum(value) / pixels for value in sums]
    ids = neighbours()
    lane = lax.broadcasted_iota(jnp.int32, (1, poses.shape[0]), 1)

    def spread(start, first, parts):
        own = start - STEP * (2.0 * first + (parts[0] + parts[1] + parts[2] + parts[3]))
        row = jnp.where(lane == ids[0], own, 0.0)
        for index in range(4):
            row = row + jnp.where(lane == ids[index + 1], STEP * parts[index], 0.0)
        return row

    images = lane.shape[1]
    for half, row in enumerate((spread(scale[ids[0]], plain, sums[:4]), spread(focal[ids[0]], slope, sums[4:]))):
        place = slice(half * images, (half + 1) * images)
        poses[:, :, place] = jnp.broadcast_to(row[None], (images, 1, images))


def align_stage(scale, focal, depth, *arrays):
    tokens, patch = depth.shape
    return pl.pallas_call(
        align_kernel,
        in_specs=[SMEM, SMEM] + [VMEM] * (len(arrays) + 1),
        out_specs=(VMEM, VMEM, VMEM),
        out_shape=(
            jax.ShapeDtypeStruct((tokens, patch), F32),
            jax.ShapeDtypeStruct((tokens, patch), BF16),
            jax.ShapeDtypeStruct((scale.shape[0], 1, 2 * scale.shape[0]), F32),
        ),
        scratch_shapes=[pltpu.VMEM((tokens, patch), F32)],
        compiler_params=params(),
        name="align_stage",
    )(scale, focal, depth, *arrays)


def final_kernel(base, *refs):
    out_x, in_x = refs[0:2], refs[2:4]
    out_o, in_o, out_p, in_p = [refs[index : index + 1] for index in range(4, 8)]
    change_p, change_o, change_b, change_n, poses, result, pose = refs[8:]
    images = poses.shape[0]
    pose[0:1, :] = jnp.sum(poses[:, :, :images], axis=0)
    pose[1:2, :] = jnp.sum(poses[:, :, images:], axis=0)
    tokens, _ = base.shape
    rows = 64
    for start in range(0, tokens, rows):
        part = pl.ds(start, rows)
        step = (wide(out_p, 1, start, rows) + wide(in_p, 1, start, rows)) * change_p[part, :].astype(F32)
        step += (wide(out_o, 1, start, rows) + wide(in_o, 1, start, rows)) * change_o[part, :].astype(F32)
        step += wide(out_x, 1, start, rows) * change_b[part, :].astype(F32)
        step += wide(in_x, 1, start, rows) * change_n[part, :].astype(F32)
        result[part, :] = base[part, :] + STEP * step


def final_stage(base, sums, changes, poses):
    return pl.pallas_call(
        final_kernel,
        in_specs=[VMEM] * 14,
        out_specs=(VMEM, VMEM),
        out_shape=(
            jax.ShapeDtypeStruct(base.shape, F32),
            jax.ShapeDtypeStruct((2, poses.shape[0]), F32),
        ),
        compiler_params=params(),
        name="final_stage",
    )(base, *sums, *changes, poses)


def swap_inner(value):
    return lax.ppermute(value, "img", [(i, i ^ 1) for i in range(lax.axis_size("img"))])


def swap_outer(value):
    count = lax.axis_size("img")
    pairs = [(i, (i + 1) % count) for i in range(1, count, 2)]
    return lax.ppermute(value, "img", pairs + [(b, a) for a, b in pairs])


def along(value, by):
    count = lax.axis_size("group")
    return lax.ppermute(value, "group", [(i, (i + by) % count) for i in range(count)])


def local(
    enc_tokens,
    embed_weight,
    embed_bias,
    query_gain,
    memory_gain,
    query_weight,
    key_weight,
    value_weight,
    out_weight,
    head_weight,
    pair_dst,
    pair_count,
    depth,
    scale,
    focal,
):
    tokens = enc_tokens.shape[1]
    half = tokens // 2
    depth_now = depth[0]
    embed, rows, short = embed_stage(
        enc_tokens[0], embed_weight, embed_bias, memory_gain, depth_now
    )
    rows_x = along(rows, 1)
    rows_o = swap_outer(rows)
    rows_p = swap_inner(rows)
    late_x = along(short, 1)
    query_t, value_wt, peak = query_stage(embed, query_gain, query_weight, value_weight)
    common = (pair_dst, pair_count, scale, focal, query_t, peak, embed, out_weight, head_weight, depth_now)
    weights = (key_weight, value_wt)
    kept, sent_p, moved_p = pair_stage(1, 0, tokens, common, (rows_p, *weights))
    in_p = swap_inner(sent_p)
    kept, sent_o, moved_o = pair_stage(2, 0, tokens, common, (rows_o, *weights), kept)
    in_o = swap_outer(sent_o)
    kept, sent_a, moved_a, *made_x = pair_stage(3, 0, half, common, (rows_x, *weights), kept, True)
    in_a = along(sent_a, -1)
    kept, sent_b, moved_b = pair_stage(3, half, tokens - half, common, made_x, kept)
    in_b = along(sent_b, -1)
    sums = (sent_a, sent_b, in_a, in_b, sent_o, in_o, sent_p, in_p)
    moved = (moved_a, moved_b, moved_o, moved_p)
    base, change, poses = align_stage(scale, focal, depth_now, *moved, *sums, late_x)
    changes = (swap_inner(change), swap_outer(change), along(change, 1), along(change, -1))
    poses = lax.all_to_all(poses, ("group", "img"), 0, 0, tiled=True)
    depth_out, pose = final_stage(base, sums, changes, poses)
    return (kept, depth_out[None], pose[0], pose[1])


def solution(mesh):
    whole = P(("group", "img"), None, None)
    line = P(("group", "img"))
    return jax.shard_map(
        local,
        mesh=mesh,
        in_specs=(whole, *[P()] * 9, line, line, whole, P(), P()),
        out_specs=(whole, whole, P(), P()),
        check_vma=False,
    )
```

time: 129 us -> 111 us (0.86)
  the two profiles are of different devices: /device:TPU:6 before, /device:TPU:1 now
where the time goes in v3:
time: 111 us
  Pallas kernels  52.6 us (47%)
  starting transfers between devices  20 us (18%)
  waiting for transfers between devices  16.9 us (15%)
  blocking collectives  16.8 us (15%)
  local copies, waits for them, and re-layouts  3.1 us (3%)
  between operations  1.53 us (1%)
    pallas_call x4, Pallas kernels, pair_stage(): pl.pallas_call(body, in_specs=specs, out_specs=(HBM,) + (VMEM,) * (len(re...  39.2 us
    ppermute x6, waiting for transfers between devices, along(): lax.ppermute(value, 'group', [(i, (i + by) % count) for i in range(count)])  16.8 us
    all_to_all x1, blocking collectives, local(): poses = lax.all_to_all(poses, ('group', 'img'), 0, 0, tiled=True)  16.8 us
    ppermute x3, starting transfers between devices, swap_inner(): lax.ppermute(value, 'img', [(i, i ^ 1) for i in range(lax.axis_size('img'...  10.3 us
    ppermute x6, starting transfers between devices, along(): lax.ppermute(value, 'group', [(i, (i + by) % count) for i in range(count)])  7.9 us
    pallas_call x1, Pallas kernels, embed_stage(): pl.pallas_call(embed_kernel, in_specs=[HBM, HBM, VMEM, VMEM, HBM], out_sp...  6.24 us
    pallas_call x1, Pallas kernels, align_stage(): pl.pallas_call(align_kernel, in_specs=[SMEM, SMEM] + [VMEM] * (len(arrays...  3.14 us
    unnamed x26, local copies, waits for them, and re-layouts  2.59 us
  transfers between devices with their start and end apart: 12, of which 2 were waited for; matrix products, arithmetic and copies ran while one was open for 0% of the time, Pallas kernels for 38%

profile of v3, /device:TPU:1, one launch (start us, length us, event | category | flops | bytes accessed | tf_op | source)
XLA Modules:
  0.0 110.9 jit_solution(8862413628165181522)
XLA Ops:
  0.7 6.2 %embed_stage.1 = (bf16[768,768]{1,0:T(8,128)(2,1)}, bf16[768,768]{1,0:T(8,128)(2,1)}, bf16[768,256]{1,0:T(8,128)(2,1)}) custom-call(bf16[768,1024]{1,0:T(8,128)(2,1)} %bitcast.13, bf16[1024,768]{1,0:T(8,128)(2,1)} %weight.1, f32[768]{0:T(1024)} %bias.1, f32[768]{0:T(1024)} %memory_gain.1, f32[768,256]{1,0:T(8,128)} %bitcast.7), custom_call_target="tpu_custom_call" | custom-call | tf_op jit(solution)/shard_map/embed_stage/pallas_call | solution.py:89
  6.9 1.5 %collective-permute-start.2 = (bf16[768,768]{1,0:T(8,128)(2,1)}, bf16[768,768]{1,0:T(8,128)(2,1)S(1)}, u32[]{:S(2)}, u32[]{:S(2)}) collective-permute-start(bf16[768,768]{1,0:T(8,128)(2,1)} %get-tuple-element.33), channel_id=1, source_target_pairs={{0,1},{1,0},{2,3},{3,2},{4,5},{5,4},{6,7},{7,6},{8,9},{9,8},{10,11... | collective-permute-start | bytes 3538952 | tf_op jit(solution)/shard_map/ppermute | solution.py:450
  8.4 1.4 %collective-permute-start.1 = (bf16[768,768]{1,0:T(8,128)(2,1)}, bf16[768,768]{1,0:T(8,128)(2,1)S(1)}, u32[]{:S(2)}, u32[]{:S(2)}) collective-permute-start(bf16[768,768]{1,0:T(8,128)(2,1)} %get-tuple-element.33), channel_id=1, source_target_pairs={{1,2},{3,4},{5,6},{7,8},{9,10},{11,12},{13,14},{15,16},{17,18},{19... | collective-permute-start | bytes 3538952 | tf_op jit(solution)/shard_map/ppermute | solution.py:456
  9.8 1.2 %collective-permute-start = (bf16[768,768]{1,0:T(8,128)(2,1)}, bf16[768,768]{1,0:T(8,128)(2,1)S(1)}, u32[]{:S(2)}, u32[]{:S(2)}) collective-permute-start(bf16[768,768]{1,0:T(8,128)(2,1)} %get-tuple-element.33), channel_id=1, source_target_pairs={{0,32},{32,64},{64,96},{96,0},{1,33},{33,65},{65,97},{97,1},{2,34}... | collective-permute-start | bytes 3538952 | tf_op jit(solution)/shard_map/ppermute | solution.py:461
  11.7 1.3 %copy-done = bf16[768,768]{1,0:T(8,128)(2,1)S(1)} copy-done((bf16[768,768]{1,0:T(8,128)(2,1)S(1)}, bf16[768,768]{1,0:T(8,128)(2,1)}, u32[]{:S(2)}) %copy-start) | copy-done | bytes 1179672
  12.9 1.3 %copy-done.7 = bf16[768,768]{1,0:T(8,128)(2,1)S(1)} copy-done((bf16[768,768]{1,0:T(8,128)(2,1)S(1)}, bf16[768,768]{1,0:T(8,128)(2,1)}, u32[]{:S(2)}) %copy-start.7) | copy-done | bytes 1179672
  14.2 2.6 %query_stage.1 = (bf16[768,768]{1,0:T(8,128)(2,1)S(1)}, bf16[768,768]{1,0:T(8,128)(2,1)S(1)}, f32[8,128]{1,0:T(8,128)S(1)}) custom-call(bf16[768,768]{1,0:T(8,128)(2,1)S(1)} %copy-done, f32[768]{0:T(1024)S(1)} %copy-done.11, bf16[768,768]{1,0:T(8,128)(2,1)S(1)} %copy-done.6, bf16[768,768]{1,0:T(8,128)(2,1)S(1)} %copy-done.7), custom_call_target="tpu_custom_call" | custom-call | tf_op jit(solution)/shard_map/query_stage/pallas_call | solution.py:124
  16.9 12.3 %shard_map.174 = (bf16[4,768,768]{2,1,0:T(8,128)(2,1)}, bf16[3,768,256]{2,1,0:T(8,128)(2,1)S(1)}, f32[768,256]{1,0:T(8,128)S(1)}) custom-call(s32[4]{0:T(128)S(1)} %copy-done.10, s32[1]{0:T(128)S(6)} %copy.25.refs_1_, f32[128]{0:T(128)S(1)} %copy-done.8, f32[128]{0:T(128)S(1)} %copy-done.9, bf16[768,768]{1,0:T(8,128)(2,1)S(1)} %get-tuple-element.31.refs_4_, ...), custom_call_target="tpu_custom_call" | custom-call | tf_op jit(solution)/shard_map/pallas_call | solution.py:311
  29.2 12.5 %shard_map.175 = (bf16[4,768,768]{2,1,0:T(8,128)(2,1)}, bf16[3,768,256]{2,1,0:T(8,128)(2,1)S(1)}, f32[768,256]{1,0:T(8,128)S(1)}) custom-call(s32[4]{0:T(128)S(1)} %copy-done.10, s32[1]{0:T(128)S(6)} %copy.25.refs_1_, f32[128]{0:T(128)S(1)} %copy-done.8, f32[128]{0:T(128)S(1)} %copy-done.9, ...), custom_call_target="tpu_custom_call", output_to_operand_aliasing={{0}: (13, {})} | custom-call | tf_op jit(solution)/shard_map/pallas_call | solution.py:311
  41.7 0.4 collective-permute-start.5
  42.1 5.0 %collective-permute-start.6 = (bf16[3,768,256]{2,1,0:T(8,128)(2,1)S(1)}, bf16[3,768,256]{2,1,0:T(8,128)(2,1)S(1)}, u32[]{:S(2)}, u32[]{:S(2)}) collective-permute-start(bf16[3,768,256]{2,1,0:T(8,128)(2,1)S(1)} %get-tuple-element.49.refs_10_.refs_6_), channel_id=1, source_target_pairs={{0,1},{1,0},{2,3},{3,2},{4,5},{5,4},{6,7},{7,6},{8,9},{9,8},{10,11... | collective-permute-start | bytes 3538952 | tf_op jit(solution)/shard_map/ppermute | solution.py:450
  47.2 0.8 collective-permute-start.7
  48.0 8.5 %shard_map.176 = (bf16[4,768,768]{2,1,0:T(8,128)(2,1)}, bf16[2,384,256]{2,1,0:T(8,128)(2,1)S(1)}, f32[384,256]{1,0:T(8,128)S(1)}, bf16[768,768]{1,0:T(8,128)(2,1...) custom-call(s32[4]{0:T(128)S(1)} %copy-done.10, ...), custom_call_target="tpu_custom_call", output_to_operand_aliasing={{0}: (13, {})} | custom-call | tf_op jit(solution)/shard_map/pallas_call | solution.py:311
  56.5 5.9 %shard_map.177 = (bf16[4,768,768]{2,1,0:T(8,128)(2,1)}, bf16[2,384,256]{2,1,0:T(8,128)(2,1)S(1)}, f32[384,256]{1,0:T(8,128)S(1)}) custom-call(s32[4]{0:T(128)S(1)} %copy-done.10, s32[1]{0:T(128)S(6)} %copy.25.refs_1_, f32[128]{0:T(128)S(1)} %copy-done.8, f32[128]{0:T(128)S(1)} %copy-done.9, ...), custom_call_target="tpu_custom_call", output_to_operand_aliasing={{0}: (13, {})} | custom-call | tf_op jit(solution)/shard_map/pallas_call | solution.py:311
  62.5 2.3 %collective-permute-start.4 = (bf16[2,384,256]{2,1,0:T(8,128)(2,1)S(1)}, bf16[2,384,256]{2,1,0:T(8,128)(2,1)S(1)}, u32[]{:S(2)}, u32[]{:S(2)}) collective-permute-start(bf16[2,384,256]{2,1,0:T(8,128)(2,1)S(1)} %get-tuple-element.47.refs_5_.refs_1_), channel_id=1, source_target_pairs={{0,96},{32,0},{64,32},{96,64},{1,97},{33,1},{65,33},{97,65},{2,98}... | collective-permute-start | bytes 1179656 | tf_op jit(solution)/shard_map/ppermute | solution.py:461
  64.8 0.1 collective-permute-start.3
  64.8 8.4 %collective-permute-done.4.refs_7_.refs_3_ = bf16[2,384,256]{2,1,0:T(8,128)(2,1)S(1)} collective-permute-done((bf16[2,384,256]{2,1,0:T(8,128)(2,1)S(1)}, bf16[2,384,256]{2,1,0:T(8,128)(2,1)S(1)}, u32[]{:S(2)}, u32[]{:S(2)}) %collective-permute-start.4) | collective-permute-done | bytes 393248 | tf_op jit(solution)/shard_map/ppermute | solution.py:461
  73.2 8.4 %collective-permute-done.3.refs_6_.refs_2_ = bf16[2,384,256]{2,1,0:T(8,128)(2,1)S(1)} collective-permute-done((bf16[2,384,256]{2,1,0:T(8,128)(2,1)S(1)}, bf16[2,384,256]{2,1,0:T(8,128)(2,1)S(1)}, u32[]{:S(2)}, u32[]{:S(2)}) %collective-permute-start.3) | collective-permute-done | bytes 393248 | tf_op jit(solution)/shard_map/ppermute | solution.py:461
  81.7 3.1 %align_stage.1 = (f32[768,256]{1,0:T(8,128)S(1)}, bf16[768,256]{1,0:T(8,128)(2,1)S(1)}, f32[128,1,256]{2,1,0:T(1,128)S(1)}) custom-call(f32[128]{0:T(128)S(1)} %copy-done.8, f32[128]{0:T(128)S(1)} %copy-done.9, f32[768,256]{1,0:T(8,128)S(1)} %bitcast.12, f32[384,256]{1,0:T(8,128)S(1)} %get-tuple-element.42.refs_0_, ...), custom_call_target="tpu_custom_call" | custom-call | tf_op jit(solution)/shard_map/align_stage/pallas_call | solution.py:402
  84.8 3.5 %collective-permute-start.11 = (bf16[768,256]{1,0:T(8,128)(2,1)S(1)}, bf16[768,256]{1,0:T(8,128)(2,1)S(1)}, u32[]{:S(2)}, u32[]{:S(2)}) collective-permute-start(bf16[768,256]{1,0:T(8,128)(2,1)S(1)} %get-tuple-element.52), channel_id=1, source_target_pairs={{0,96},{32,0},{64,32},{96,64},{1,97},{33,1},{65,33},{97,65},{2,98}... | collective-permute-start | bytes 1179656 | tf_op jit(solution)/shard_map/ppermute | solution.py:461
  88.3 3.8 %collective-permute-start.8 = (bf16[768,256]{1,0:T(8,128)(2,1)S(1)}, bf16[768,256]{1,0:T(8,128)(2,1)S(1)}, u32[]{:S(2)}, u32[]{:S(2)}) collective-permute-start(bf16[768,256]{1,0:T(8,128)(2,1)S(1)} %get-tuple-element.52), channel_id=1, source_target_pairs={{0,1},{1,0},{2,3},{3,2},{4,5},{5,4},{6,7},{7,6},{8,9},{9,8},{10,11... | collective-permute-start | bytes 1179656 | tf_op jit(solution)/shard_map/ppermute | solution.py:450
  92.1 16.8 %all_to_all.5.refs_12_ = f32[128,1,256]{2,1,0:T(1,128)S(1)} all-to-all(f32[128,1,256]{2,1,0:T(1,128)S(1)} %get-tuple-element.53), channel_id=1, replica_groups=mesh['group'=4,'img'=32] {'group','img'}, dimensions={0} | all-to-all | bytes 262144 | tf_op jit(solution)/shard_map/all_to_all | solution.py:506
  108.9 1.5 %final_stage.1 = (f32[768,256]{1,0:T(8,128)}, f32[2,128]{1,0:T(2,128)S(1)}) custom-call(f32[768,256]{1,0:T(8,128)S(1)} %get-tuple-element.51.base, bf16[2,384,256]{2,1,0:T(8,128)(2,1)S(1)} %get-tuple-element.46.refs_4_.refs_0_, bf16[2,384,256]{2,1,0:T(8,128)(2,1)S(1)} %get-tuple-element.47.refs_5_.refs_1_, ...), custom_call_target="tpu_custom_call" | custom-call | tf_op jit(solution)/shard_map/final_stage/pallas_call | solution.py:436
  110.4 0.5 slice_bitcast_fusion
  (36 shorter events, 0.1 us)
Async XLA Ops:
  0.6 11.0 %copy-start.6 = (bf16[768,768]{1,0:T(8,128)(2,1)S(1)}, bf16[768,768]{1,0:T(8,128)(2,1)}, u32[]{:S(2)}) copy-start(bf16[768,768]{1,0:T(8,128)(2,1)} %query_w.1) | copy-start | bytes 3538948
  0.6 11.0 %copy-start.11 = (f32[768]{0:T(1024)S(1)}, f32[768]{0:T(1024)}, u32[]{:S(2)}) copy-start(f32[768]{0:T(1024)} %gain.1) | copy-start | bytes 9220
  0.7 16.2 %copy-start.4 = (bf16[768,512]{1,0:T(8,128)(2,1)S(1)}, bf16[768,512]{1,0:T(8,128)(2,1)}, u32[]{:S(2)}) copy-start(bf16[768,512]{1,0:T(8,128)(2,1)} %refs_8_.7) | copy-start | bytes 2359300
  0.7 16.2 %copy-start.5 = (bf16[768,768]{1,0:T(8,128)(2,1)S(1)}, bf16[768,768]{1,0:T(8,128)(2,1)}, u32[]{:S(2)}) copy-start(bf16[768,768]{1,0:T(8,128)(2,1)} %refs_11_.5) | copy-start | bytes 3538948
  6.9 9.9 %collective-permute-start.2 = (bf16[768,768]{1,0:T(8,128)(2,1)}, bf16[768,768]{1,0:T(8,128)(2,1)S(1)}, u32[]{:S(2)}, u32[]{:S(2)}) collective-permute-start(bf16[768,768]{1,0:T(8,128)(2,1)} %get-tuple-element.33), channel_id=1, source_target_pairs={{0,1},{1,0},{2,3},{3,2},{4,5},{5,4},{6,7},{7,6},{8,9},{9,8},{10,11... | collective-permute-start | bytes 3538952 | tf_op jit(solution)/shard_map/ppermute | solution.py:450
  8.4 20.8 %collective-permute-start.1 = (bf16[768,768]{1,0:T(8,128)(2,1)}, bf16[768,768]{1,0:T(8,128)(2,1)S(1)}, u32[]{:S(2)}, u32[]{:S(2)}) collective-permute-start(bf16[768,768]{1,0:T(8,128)(2,1)} %get-tuple-element.33), channel_id=1, source_target_pairs={{1,2},{3,4},{5,6},{7,8},{9,10},{11,12},{13,14},{15,16},{17,18},{19... | collective-permute-start | bytes 3538952 | tf_op jit(solution)/shard_map/ppermute | solution.py:456
  9.8 38.2 %collective-permute-start = (bf16[768,768]{1,0:T(8,128)(2,1)}, bf16[768,768]{1,0:T(8,128)(2,1)S(1)}, u32[]{:S(2)}, u32[]{:S(2)}) collective-permute-start(bf16[768,768]{1,0:T(8,128)(2,1)} %get-tuple-element.33), channel_id=1, source_target_pairs={{0,32},{32,64},{64,96},{96,0},{1,33},{33,65},{65,97},{97,1},{2,34}... | collective-permute-start | bytes 3538952 | tf_op jit(solution)/shard_map/ppermute | solution.py:461
  11.7 1.3 %copy-start = (bf16[768,768]{1,0:T(8,128)(2,1)S(1)}, bf16[768,768]{1,0:T(8,128)(2,1)}, u32[]{:S(2)}) copy-start(bf16[768,768]{1,0:T(8,128)(2,1)} %get-tuple-element.30.embed.refs_6_) | copy-start | bytes 3538948
  14.2 2.6 %copy-start.1 = (bf16[768,768]{1,0:T(8,128)(2,1)S(1)}, bf16[768,768]{1,0:T(8,128)(2,1)}, u32[]{:S(2)}) copy-start(bf16[768,768]{1,0:T(8,128)(2,1)} %get-tuple-element.30.embed.refs_6_) | copy-start | bytes 3538948
  14.2 2.6 %copy-start.2 = (f32[1,768,256]{2,1,0:T(8,128)S(1)}, f32[1,768,256]{2,1,0:T(8,128)}, u32[]{:S(2)}) copy-start(f32[1,768,256]{2,1,0:T(8,128)} %param.27) | copy-start | bytes 2359300
  14.2 2.6 %copy-start.3 = (bf16[768,768]{1,0:T(8,128)(2,1)S(1)}, bf16[768,768]{1,0:T(8,128)(2,1)}, u32[]{:S(2)}) copy-start(bf16[768,768]{1,0:T(8,128)(2,1)} %refs_7_.7) | copy-start | bytes 3538948
  14.2 2.7 %copy-start.8 = (f32[128]{0:T(128)S(1)}, f32[128]{0:T(128)}, u32[]{:S(2)}) copy-start(f32[128]{0:T(128)} %scale.1) | copy-start | bytes 1540
  14.2 2.7 %copy-start.9 = (f32[128]{0:T(128)S(1)}, f32[128]{0:T(128)}, u32[]{:S(2)}) copy-start(f32[128]{0:T(128)} %focal.1) | copy-start | bytes 1540
  14.2 2.7 %copy-start.10 = (s32[4]{0:T(128)S(1)}, s32[4]{0:T(128)}, u32[]{:S(2)}) copy-start(s32[4]{0:T(128)} %refs_0_.7) | copy-start | bytes 52
  29.2 18.0 %copy-start.12 = (bf16[768,256]{1,0:T(8,128)(2,1)S(1)}, bf16[768,256]{1,0:T(8,128)(2,1)}, u32[]{:S(2)}) copy-start(bf16[768,256]{1,0:T(8,128)(2,1)} %get-tuple-element.50) | copy-start | bytes 1179652
  41.7 40.0 %collective-permute-start.5 = (bf16[3,768,256]{2,1,0:T(8,128)(2,1)S(1)}, bf16[3,768,256]{2,1,0:T(8,128)(2,1)S(1)}, u32[]{:S(2)}, u32[]{:S(2)}) collective-permute-start(bf16[3,768,256]{2,1,0:T(8,128)(2,1)S(1)} %get-tuple-element.48.refs_8_.refs_4_), channel_id=1, source_target_pairs={{1,2},{3,4},{5,6},{7,8},{9,10},{11,12},{13,14},{15,16},{17,18},{19... | collective-permute-start | bytes 3538952 | tf_op jit(solution)/shard_map/ppermute | solution.py:456
  42.1 39.5 %collective-permute-start.6 = (bf16[3,768,256]{2,1,0:T(8,128)(2,1)S(1)}, bf16[3,768,256]{2,1,0:T(8,128)(2,1)S(1)}, u32[]{:S(2)}, u32[]{:S(2)}) collective-permute-start(bf16[3,768,256]{2,1,0:T(8,128)(2,1)S(1)} %get-tuple-element.49.refs_10_.refs_6_), channel_id=1, source_target_pairs={{0,1},{1,0},{2,3},{3,2},{4,5},{5,4},{6,7},{7,6},{8,9},{9,8},{10,11... | collective-permute-start | bytes 3538952 | tf_op jit(solution)/shard_map/ppermute | solution.py:450
  47.2 17.7 %collective-permute-start.7 = (bf16[768,256]{1,0:T(8,128)(2,1)S(1)}, bf16[768,256]{1,0:T(8,128)(2,1)S(1)}, u32[]{:S(2)}, u32[]{:S(2)}) collective-permute-start(bf16[768,256]{1,0:T(8,128)(2,1)S(1)} %copy-done.12), channel_id=1, source_target_pairs={{0,32},{32,64},{64,96},{96,0},{1,33},{33,65},{65,97},{97,1},{2,34}... | collective-permute-start | bytes 1179656 | tf_op jit(solution)/shard_map/ppermute | solution.py:461
  62.5 10.8 %collective-permute-start.4 = (bf16[2,384,256]{2,1,0:T(8,128)(2,1)S(1)}, bf16[2,384,256]{2,1,0:T(8,128)(2,1)S(1)}, u32[]{:S(2)}, u32[]{:S(2)}) collective-permute-start(bf16[2,384,256]{2,1,0:T(8,128)(2,1)S(1)} %get-tuple-element.47.refs_5_.refs_1_), channel_id=1, source_target_pairs={{0,96},{32,0},{64,32},{96,64},{1,97},{33,1},{65,33},{97,65},{2,98}... | collective-permute-start | bytes 1179656 | tf_op jit(solution)/shard_map/ppermute | solution.py:461
  64.8 16.9 %collective-permute-start.3 = (bf16[2,384,256]{2,1,0:T(8,128)(2,1)S(1)}, bf16[2,384,256]{2,1,0:T(8,128)(2,1)S(1)}, u32[]{:S(2)}, u32[]{:S(2)}) collective-permute-start(bf16[2,384,256]{2,1,0:T(8,128)(2,1)S(1)} %get-tuple-element.46.refs_4_.refs_0_), channel_id=1, source_target_pairs={{0,96},{32,0},{64,32},{96,64},{1,97},{33,1},{65,33},{97,65},{2,98}... | collective-permute-start | bytes 1179656 | tf_op jit(solution)/shard_map/ppermute | solution.py:461
  84.8 24.0 %collective-permute-start.11 = (bf16[768,256]{1,0:T(8,128)(2,1)S(1)}, bf16[768,256]{1,0:T(8,128)(2,1)S(1)}, u32[]{:S(2)}, u32[]{:S(2)}) collective-permute-start(bf16[768,256]{1,0:T(8,128)(2,1)S(1)} %get-tuple-element.52), channel_id=1, source_target_pairs={{0,96},{32,0},{64,32},{96,64},{1,97},{33,1},{65,33},{97,65},{2,98}... | collective-permute-start | bytes 1179656 | tf_op jit(solution)/shard_map/ppermute | solution.py:461
  88.3 20.6 %collective-permute-start.10 = (bf16[768,256]{1,0:T(8,128)(2,1)S(1)}, bf16[768,256]{1,0:T(8,128)(2,1)S(1)}, u32[]{:S(2)}, u32[]{:S(2)}) collective-permute-start(bf16[768,256]{1,0:T(8,128)(2,1)S(1)} %get-tuple-element.52), channel_id=1, source_target_pairs={{0,32},{32,64},{64,96},{96,0},{1,33},{33,65},{65,97},{97,1},{2,34}... | collective-permute-start | bytes 1179656 | tf_op jit(solution)/shard_map/ppermute | solution.py:461
  88.3 20.6 %collective-permute-start.9 = (bf16[768,256]{1,0:T(8,128)(2,1)S(1)}, bf16[768,256]{1,0:T(8,128)(2,1)S(1)}, u32[]{:S(2)}, u32[]{:S(2)}) collective-permute-start(bf16[768,256]{1,0:T(8,128)(2,1)S(1)} %get-tuple-element.52), channel_id=1, source_target_pairs={{1,2},{3,4},{5,6},{7,8},{9,10},{11,12},{13,14},{15,16},{17,18},{19... | collective-permute-start | bytes 1179656 | tf_op jit(solution)/shard_map/ppermute | solution.py:456
  88.3 20.6 %collective-permute-start.8 = (bf16[768,256]{1,0:T(8,128)(2,1)S(1)}, bf16[768,256]{1,0:T(8,128)(2,1)S(1)}, u32[]{:S(2)}, u32[]{:S(2)}) collective-permute-start(bf16[768,256]{1,0:T(8,128)(2,1)S(1)} %get-tuple-element.52), channel_id=1, source_target_pairs={{0,1},{1,0},{2,3},{3,2},{4,5},{5,4},{6,7},{7,6},{8,9},{9,8},{10,11... | collective-permute-start | bytes 1179656 | tf_op jit(solution)/shard_map/ppermute | solution.py:450
  (1 other events, 1.3 us)

commit v4 on v3

--- a/solution.py
+++ b/solution.py
@@ -52,7 +52,7 @@
 
 
 def embed_kernel(enc, weight, bias, memory_gain, depth, embed, rows_out, late, *scratch):
-    enc_v, weight_v, depth_v, embed_v, rows_v, late_v, arrive, leave = scratch
+    enc_v, weight_v, depth_v, bias_v, gain_v, embed_v, rows_v, late_v, arrive, leave = scratch
     tokens = embed.shape[0]
     count = 3
     rows = tokens // count
@@ -60,17 +60,19 @@
     for index in range(count):
         part = pl.ds(index * rows, rows)
         moves.append(pltpu.make_async_copy(enc.at[part], enc_v.at[part], arrive.at[index + 1]))
-    moves.append(pltpu.make_async_copy(depth, depth_v, arrive.at[count + 1]))
+    for place, pair in enumerate(((bias, bias_v), (memory_gain, gain_v), (depth, depth_v))):
+        moves.append(pltpu.make_async_copy(*pair, arrive.at[count + 1 + place]))
     for move in moves:
         move.start()
-    moves[0].wait()
+    for move in (moves[0], moves[count + 1], moves[count + 2]):
+        move.wait()
     out = []
     for index in range(count):
         part = pl.ds(index * rows, rows)
         moves[index + 1].wait()
-        value = (matmul(enc_v[part, :], weight_v[...]) + bias[...][None, :]).astype(BF16)
+        value = (matmul(enc_v[part, :], weight_v[...]) + bias_v[...][None, :]).astype(BF16)
         embed_v[part, :] = value
-        rows_v[part, :] = normed(value, memory_gain[...][None, :])
+        rows_v[part, :] = normed(value, gain_v[...][None, :])
         for place, (source, target) in enumerate(((rows_v, rows_out), (embed_v, embed))):
             out.append(pltpu.make_async_copy(source.at[part], target.at[part], leave.at[index * 2 + place]))
             out[-1].start()
@@ -88,20 +90,22 @@
     shapes = [(tokens, width), (tokens, width), (tokens, patch)]
     return pl.pallas_call(
         embed_kernel,
-        in_specs=[HBM, HBM, VMEM, VMEM, HBM],
+        in_specs=[HBM] * 5,
         out_specs=(HBM,) * 3,
         out_shape=tuple(jax.ShapeDtypeStruct(shape, BF16) for shape in shapes),
         scratch_shapes=[
             pltpu.VMEM(enc.shape, BF16),
             pltpu.VMEM(weight.shape, BF16),
             pltpu.VMEM(depth.shape, F32),
+            pltpu.VMEM(bias.shape, F32),
+            pltpu.VMEM(bias.shape, F32),
             *[pltpu.VMEM(shape, BF16) for shape in shapes],
-            pltpu.SemaphoreType.DMA((5,)),
+            pltpu.SemaphoreType.DMA((7,)),
             pltpu.SemaphoreType.DMA((7,)),
         ],
-        compiler_params=params(60),
+        compiler_params=params(),
         name="embed_stage",
-    )(enc, weight, bias, memory_gain, depth)
+    )(*[pltpu.with_memory_space_constraint(array, pltpu.HBM) for array in (enc, weight, bias, memory_gain, depth)])
 
 
 def query_kernel(embed, gain, query_w, value_w, query_t, value_wt, peak):
@@ -215,11 +219,14 @@
     dead = [slot >= live[0] for slot in range(slots)]
 
     def clear(slot):
-        return pltpu.make_async_copy(zeros, pair_tokens.at[slot], sems.at[slots + slot])
-
-    def write(slot):
-        place = pair_tokens.at[slot, pl.ds(first, count)]
-        return pltpu.make_async_copy(rows_out, place, sems.at[slot])
+        return pltpu.make_async_copy(zeros, pair_tokens.at[slot], sems.at[slot])
+
+    rows = 256 if count % 256 == 0 else 128
+
+    def write(slot, start):
+        place = pair_tokens.at[slot, pl.ds(first + start, rows)]
+        source = rows_out.at[pl.ds(start, rows)]
+        return pltpu.make_async_copy(source, place, sems.at[slots * (1 + start // rows) + slot])
 
     if not chained:
         zeros[...] = jnp.zeros_like(zeros)
@@ -244,7 +251,6 @@
     def _():
         attention(query_t, keys, values_t, mixed_t, first, count, 1, True)
 
-    rows = 256 if count % 256 == 0 else 128
     weight = jnp.float32(0.0)
     for slot in range(slots):
         weight = weight + jnp.where(hits[slot], 1.0, 0.0)
@@ -256,6 +262,8 @@
         attended = matmul(mixed_t[:, part], out_w[...], 0, 0)
         value = (embed[whole, :].astype(F32) + attended).astype(BF16)
         rows_out[part, :] = value
+        for slot in range(slots):
+            pl.when(hits[slot])(lambda slot=slot: write(slot, start).start())
         head = matmul(value, head_w[...])
         logit = head[:, patch:]
         soft = jnp.maximum(logit, 0.0) + jnp.log1p(jnp.exp(-jnp.abs(logit)))
@@ -267,10 +275,9 @@
         moved_out[part, :] = moved
         if sent.shape[0] == 3:
             sent[2, part, :] = depth[whole, :].astype(BF16)
-    for slot in range(slots):
-        pl.when(hits[slot])(lambda slot=slot: write(slot).start())
-    for slot in range(slots):
-        pl.when(hits[slot])(lambda slot=slot: write(slot).wait())
+    for start in range(0, count, rows):
+        for slot in range(slots):
+            pl.when(hits[slot])(lambda slot=slot: write(slot, start).wait())
     if not chained:
         for slot in range(slots):
             pl.when(dead[slot])(lambda slot=slot: clear(slot).wait())
@@ -292,7 +299,7 @@
     scratch += [
         pltpu.VMEM((width, count), BF16),
         pltpu.VMEM((count, width), BF16),
-        pltpu.SemaphoreType.DMA((2 * slots,)),
+        pltpu.SemaphoreType.DMA((4 * slots,)),
     ]
     if not chained:
         scratch.append(pltpu.VMEM((tokens, width), BF16))
@@ -331,11 +338,39 @@
     return strip(pieces, start, rows, index)
 
 
-def align_kernel(scale, focal, depth, *refs):
-    moved_x, (moved_o, moved_p), out_x, in_x = [refs[2 * index : 2 * index + 2] for index in range(4)]
+def gather_kernel(depth, *refs):
+    moved_x, (moved_o, moved_p), out_x = [refs[2 * index : 2 * index + 2] for index in range(3)]
     moved_o, moved_p = (moved_o,), (moved_p,)
-    out_o, in_o, out_p, in_p, late = [refs[index : index + 1] for index in range(8, 13)]
-    base, change, poses, grads = refs[13:]
+    out_o, in_o, out_p, in_p, late = [refs[index : index + 1] for index in range(6, 11)]
+    total, link_o, link_p = refs[11:]
+    rows = 64
+    for start in range(0, depth.shape[0], rows):
+        part = pl.ds(start, rows)
+        own = depth[part, :]
+        grad = strip(moved_x, start, rows) + strip(moved_o, start, rows) + strip(moved_p, start, rows)
+        grad = grad - wide(out_x, 1, start, rows) * strip(late, start, rows)
+        for outs, ins, link in ((out_o, in_o, link_o), (out_p, in_p, link_p)):
+            back = wide(ins, 1, start, rows)
+            ahead = wide(outs, 1, start, rows)
+            grad = grad - wide(ins, 0, start, rows) + back * own - ahead * wide(ins, 2, start, rows)
+            link[part, :] = back + ahead
+        total[part, :] = grad
+
+
+def gather_stage(depth, *arrays):
+    return pl.pallas_call(
+        gather_kernel,
+        in_specs=[VMEM] * (len(arrays) + 1),
+        out_specs=(VMEM,) * 3,
+        out_shape=(jax.ShapeDtypeStruct(depth.shape, F32),) * 3,
+        compiler_params=params(),
+        name="gather_stage",
+    )(depth, *arrays)
+
+
+def align_kernel(scale, focal, depth, total, link_o, link_p, *refs):
+    out_x, in_x = refs[0:2], refs[2:4]
+    base, change, poses, grads = refs[4:]
     tokens, patch = depth.shape
     pixels = tokens * patch
     rows = 64
@@ -346,15 +381,8 @@
     plain = jnp.zeros((8, patch), F32)
     slope = jnp.zeros((8, patch), F32)
     for start in range(0, tokens, rows):
-        own = depth[pl.ds(start, rows), :]
-        grad = jnp.zeros_like(own)
-        for pieces in (moved_x, moved_o, moved_p):
-            grad = grad + strip(pieces, start, rows)
-        for pieces in (in_x, in_o, in_p):
-            grad = grad - wide(pieces, 0, start, rows) + wide(pieces, 1, start, rows) * own
-        others = (strip(late, start, rows), wide(in_o, 2, start, rows), wide(in_p, 2, start, rows))
-        for pieces, other in zip((out_x, out_o, out_p), others):
-            grad = grad - wide(pieces, 1, start, rows) * other
+        part = pl.ds(start, rows)
+        grad = total[part, :] - wide(in_x, 0, start, rows) + wide(in_x, 1, start, rows) * depth[part, :]
         grads[pl.ds(start, rows), :] = grad
         plain = plain + fold(grad)
         slope = slope + fold(grad * ramp_of(start, rows, patch, pixels))
@@ -368,8 +396,8 @@
         delta = -STEP * (grad + plain + slope * ramp)
         change[part, :] = delta.astype(BF16)
         links = [
-            wide(out_p, 1, start, rows) + wide(in_p, 1, start, rows),
-            wide(out_o, 1, start, rows) + wide(in_o, 1, start, rows),
+            link_p[part, :],
+            link_o[part, :],
             wide(out_x, 1, start, rows),
             wide(in_x, 1, start, rows),
         ]
@@ -415,18 +443,18 @@
 
 
 def final_kernel(base, *refs):
-    out_x, in_x = refs[0:2], refs[2:4]
-    out_o, in_o, out_p, in_p = [refs[index : index + 1] for index in range(4, 8)]
-    change_p, change_o, change_b, change_n, poses, result, pose = refs[8:]
+    link_o, link_p = refs[:2]
+    out_x, in_x = refs[2:4], refs[4:6]
+    change_p, change_o, change_b, change_n, poses, result, pose_a, pose_f = refs[6:]
     images = poses.shape[0]
-    pose[0:1, :] = jnp.sum(poses[:, :, :images], axis=0)
-    pose[1:2, :] = jnp.sum(poses[:, :, images:], axis=0)
+    pose_a[...] = jnp.sum(poses[:, :, :images], axis=0)[0]
+    pose_f[...] = jnp.sum(poses[:, :, images:], axis=0)[0]
     tokens, _ = base.shape
     rows = 64
     for start in range(0, tokens, rows):
         part = pl.ds(start, rows)
-        step = (wide(out_p, 1, start, rows) + wide(in_p, 1, start, rows)) * change_p[part, :].astype(F32)
-        step += (wide(out_o, 1, start, rows) + wide(in_o, 1, start, rows)) * change_o[part, :].astype(F32)
+        step = link_p[part, :] * change_p[part, :].astype(F32)
+        step += link_o[part, :] * change_o[part, :].astype(F32)
         step += wide(out_x, 1, start, rows) * change_b[part, :].astype(F32)
         step += wide(in_x, 1, start, rows) * change_n[part, :].astype(F32)
         result[part, :] = base[part, :] + STEP * step
@@ -435,11 +463,12 @@
 def final_stage(base, sums, changes, poses):
     return pl.pallas_call(
         final_kernel,
-        in_specs=[VMEM] * 14,
-        out_specs=(VMEM, VMEM),
+        in_specs=[VMEM] * 12,
+        out_specs=(VMEM,) * 3,
         out_shape=(
             jax.ShapeDtypeStruct(base.shape, F32),
-            jax.ShapeDtypeStruct((2, poses.shape[0]), F32),
+            jax.ShapeDtypeStruct((poses.shape[0],), F32),
+            jax.ShapeDtypeStruct((poses.shape[0],), F32),
         ),
         compiler_params=params(),
         name="final_stage",
@@ -499,13 +528,14 @@
     in_a = along(sent_a, -1)
     kept, sent_b, moved_b = pair_stage(3, half, tokens - half, common, made_x, kept)
     in_b = along(sent_b, -1)
-    sums = (sent_a, sent_b, in_a, in_b, sent_o, in_o, sent_p, in_p)
     moved = (moved_a, moved_b, moved_o, moved_p)
-    base, change, poses = align_stage(scale, focal, depth_now, *moved, *sums, late_x)
+    total, *links = gather_stage(depth_now, *moved, sent_a, sent_b, sent_o, in_o, sent_p, in_p, late_x)
+    sums = (*links, sent_a, sent_b, in_a, in_b)
+    base, change, poses = align_stage(scale, focal, depth_now, total, *sums)
     changes = (swap_inner(change), swap_outer(change), along(change, 1), along(change, -1))
     poses = lax.all_to_all(poses, ("group", "img"), 0, 0, tiled=True)
-    depth_out, pose = final_stage(base, sums, changes, poses)
-    return (kept, depth_out[None], pose[0], pose[1])
+    depth_out, pose_a, pose_f = final_stage(base, sums, changes, poses)
+    return (kept, depth_out[None], pose_a, pose_f)
 
 
 def solution(mesh):

time: 111 us -> 107 us (0.964)
  local copies, waits for them, and re-layouts: 3.1 us -> 0.05 us
  waiting for transfers between devices: 16.9 us -> 15.3 us
    unnamed x26 -> x20, local copies, waits for them, and re-layouts: 2.59 us -> 0.05 us
    ppermute x6, waiting for transfers between devices: 16.8 us -> 15.2 us  [along(): lax.ppermute(value, 'group', [(i, (i + by) % count) for i in range(count)])]
    pallas_call x2 -> x3, Pallas kernels: 7.7 us -> 8.23 us  [the longest x1 5.95 us: embed_stage(): pl.pallas_call(embed_kernel, in_specs=[HBM] * 5, out_specs=(HBM,) * 3, ou...]
  transfers between devices with their start and end apart: 12 -> 12, of which waited for: 2 -> 2; matrix products, arithmetic and copies ran while one was open for 0% -> 0% of each run, Pallas kernels for 38% -> 39%
where the time goes in v4:
time: 107 us
  Pallas kernels  51.5 us (48%)
  starting transfers between devices  20.8 us (19%)
  blocking collectives  17.5 us (16%)
  waiting for transfers between devices  15.3 us (14%)
  between operations  1.54 us (1%)
    pallas_call x4, Pallas kernels, pair_stage(): pl.pallas_call(body, in_specs=specs, out_specs=(HBM,) + (VMEM,) * (len(re...  38.4 us
    all_to_all x1, blocking collectives, local(): poses = lax.all_to_all(poses, ('group', 'img'), 0, 0, tiled=True)  17.5 us
    ppermute x6, waiting for transfers between devices, along(): lax.ppermute(value, 'group', [(i, (i + by) % count) for i in range(count)])  15.2 us
    ppermute x3, starting transfers between devices, swap_inner(): lax.ppermute(value, 'img', [(i, i ^ 1) for i in range(lax.axis_size('img'...  10.5 us
    ppermute x6, starting transfers between devices, along(): lax.ppermute(value, 'group', [(i, (i + by) % count) for i in range(count)])  8.2 us
    pallas_call x1, Pallas kernels, embed_stage(): pl.pallas_call(embed_kernel, in_specs=[HBM] * 5, out_specs=(HBM,) * 3, ou...  5.95 us
    pallas_call x1, Pallas kernels, query_stage(): pl.pallas_call(query_kernel, in_specs=[VMEM] * 4, out_specs=(VMEM,) * 3,...  2.6 us
    pallas_call x1, Pallas kernels, align_stage(): pl.pallas_call(align_kernel, in_specs=[SMEM, SMEM] + [VMEM] * (len(arrays...  2.32 us
  transfers between devices with their start and end apart: 12, of which 2 were waited for; matrix products, arithmetic and copies ran while one was open for 0% of the time, Pallas kernels for 39%

profile of v4, /device:TPU:1, one launch (start us, length us, event | category | flops | bytes accessed | tf_op | source)
XLA Modules:
  0.0 106.6 jit_solution(503064150089151397)
XLA Ops:
  0.7 5.9 %embed_stage.1 = (bf16[768,768]{1,0:T(8,128)(2,1)S(1)}, bf16[768,768]{1,0:T(8,128)(2,1)S(1)}, bf16[768,256]{1,0:T(8,128)(2,1)S(1)}) custom-call(bf16[768,1024]{1,0:T(8,128)(2,1)} %bitcast.10, bf16[1024,768]{1,0:T(8,128)(2,1)} %weight.1, f32[768]{0:T(1024)} %bias.1, f32[768]{0:T(1024)} %memory_gain.1, f32[768,256]{1,0:T(8,128)} %bitcast.3), custom_call_target="tpu_custom_call" | custom-call | tf_op jit(solution)/shard_map/embed_stage/pallas_call | solution.py:91
  6.6 1.5 %collective-permute-start.2 = (bf16[768,768]{1,0:T(8,128)(2,1)S(1)}, bf16[768,768]{1,0:T(8,128)(2,1)S(1)}, u32[]{:S(2)}, u32[]{:S(2)}) collective-permute-start(bf16[768,768]{1,0:T(8,128)(2,1)S(1)} %get-tuple-element.37), channel_id=1, source_target_pairs={{0,1},{1,0},{2,3},{3,2},{4,5},{5,4},{6,7},{7,6},{8,9},{9,8},{10,11... | collective-permute-start | bytes 3538952 | tf_op jit(solution)/shard_map/ppermute | solution.py:479
  8.1 1.4 %collective-permute-start.1 = (bf16[768,768]{1,0:T(8,128)(2,1)S(1)}, bf16[768,768]{1,0:T(8,128)(2,1)S(1)}, u32[]{:S(2)}, u32[]{:S(2)}) collective-permute-start(bf16[768,768]{1,0:T(8,128)(2,1)S(1)} %get-tuple-element.37), channel_id=1, source_target_pairs={{1,2},{3,4},{5,6},{7,8},{9,10},{11,12},{13,14},{15,16},{17,18},{19... | collective-permute-start | bytes 3538952 | tf_op jit(solution)/shard_map/ppermute | solution.py:485
  9.5 1.2 %collective-permute-start = (bf16[768,768]{1,0:T(8,128)(2,1)S(1)}, bf16[768,768]{1,0:T(8,128)(2,1)S(1)}, u32[]{:S(2)}, u32[]{:S(2)}) collective-permute-start(bf16[768,768]{1,0:T(8,128)(2,1)S(1)} %get-tuple-element.37), channel_id=1, source_target_pairs={{0,32},{32,64},{64,96},{96,0},{1,33},{33,65},{65,97},{97,1},{2,34}... | collective-permute-start | bytes 3538952 | tf_op jit(solution)/shard_map/ppermute | solution.py:490
  11.4 0.0 copy-start.1
  11.4 0.0 copy-start.2
  11.4 2.6 %query_stage.1 = (bf16[768,768]{1,0:T(8,128)(2,1)S(1)}, bf16[768,768]{1,0:T(8,128)(2,1)S(1)}, f32[8,128]{1,0:T(8,128)S(1)}) custom-call(bf16[768,768]{1,0:T(8,128)(2,1)S(1)} %get-tuple-element.34.embed.refs_6_, f32[768]{0:T(1024)S(1)} %copy-done.9, bf16[768,768]{1,0:T(8,128)(2,1)S(1)} %copy-done.4, bf16[768,768]{1,0:T(8,128)(2,1)S(1)} %copy-done.5), custom_call_target="tpu_custom_call" | custom-call | tf_op jit(solution)/shard_map/query_stage/pallas_call | solution.py:128
  14.1 12.1 %shard_map.174 = (bf16[4,768,768]{2,1,0:T(8,128)(2,1)}, bf16[3,768,256]{2,1,0:T(8,128)(2,1)S(1)}, f32[768,256]{1,0:T(8,128)S(1)}) custom-call(s32[4]{0:T(128)S(1)} %copy-done.8, s32[1]{0:T(128)S(6)} %copy.25.refs_1_, f32[128]{0:T(128)S(1)} %copy-done.6, f32[128]{0:T(128)S(1)} %copy-done.7, bf16[768,768]{1,0:T(8,128)(2,1)S(1)} %get-tuple-element.35.refs_4_, ...), custom_call_target="tpu_custom_call" | custom-call | tf_op jit(solution)/shard_map/pallas_call | solution.py:318
  26.2 12.0 %shard_map.175 = (bf16[4,768,768]{2,1,0:T(8,128)(2,1)}, bf16[3,768,256]{2,1,0:T(8,128)(2,1)S(1)}, f32[768,256]{1,0:T(8,128)S(1)}) custom-call(s32[4]{0:T(128)S(1)} %copy-done.8, s32[1]{0:T(128)S(6)} %copy.25.refs_1_, f32[128]{0:T(128)S(1)} %copy-done.6, f32[128]{0:T(128)S(1)} %copy-done.7, ...), custom_call_target="tpu_custom_call", output_to_operand_aliasing={{0}: (13, {})} | custom-call | tf_op jit(solution)/shard_map/pallas_call | solution.py:318
  38.3 0.7 collective-permute-start.3
  39.0 6.3 %collective-permute-start.4 = (bf16[3,768,256]{2,1,0:T(8,128)(2,1)S(1)}, bf16[3,768,256]{2,1,0:T(8,128)(2,1)S(1)}, u32[]{:S(2)}, u32[]{:S(2)}) collective-permute-start(bf16[3,768,256]{2,1,0:T(8,128)(2,1)S(1)} %get-tuple-element.53.refs_8_), channel_id=1, source_target_pairs={{0,1},{1,0},{2,3},{3,2},{4,5},{5,4},{6,7},{7,6},{8,9},{9,8},{10,11... | collective-permute-start | bytes 3538952 | tf_op jit(solution)/shard_map/ppermute | solution.py:479
  45.3 1.2 %collective-permute-start.5 = (bf16[768,256]{1,0:T(8,128)(2,1)S(1)}, bf16[768,256]{1,0:T(8,128)(2,1)S(1)}, u32[]{:S(2)}, u32[]{:S(2)}) collective-permute-start(bf16[768,256]{1,0:T(8,128)(2,1)S(1)} %get-tuple-element.54), channel_id=1, source_target_pairs={{0,32},{32,64},{64,96},{96,0},{1,33},{33,65},{65,97},{97,1},{2,34}... | collective-permute-start | bytes 1179656 | tf_op jit(solution)/shard_map/ppermute | solution.py:490
  46.5 8.4 %shard_map.176 = (bf16[4,768,768]{2,1,0:T(8,128)(2,1)}, bf16[2,384,256]{2,1,0:T(8,128)(2,1)S(1)}, f32[384,256]{1,0:T(8,128)S(1)}, bf16[768,768]{1,0:T(8,128)(2,1...) custom-call(s32[4]{0:T(128)S(1)} %copy-done.8, s32[1]{0:T(128)S(6)} %copy.25.refs_1_, ...), custom_call_target="tpu_custom_call", output_to_operand_aliasing={{0}: (13, {})} | custom-call | tf_op jit(solution)/shard_map/pallas_call | solution.py:318
  54.9 5.9 %shard_map.177 = (bf16[4,768,768]{2,1,0:T(8,128)(2,1)}, bf16[2,384,256]{2,1,0:T(8,128)(2,1)S(1)}, f32[384,256]{1,0:T(8,128)S(1)}) custom-call(s32[4]{0:T(128)S(1)} %copy-done.8, s32[1]{0:T(128)S(6)} %copy.25.refs_1_, f32[128]{0:T(128)S(1)} %copy-done.6, f32[128]{0:T(128)S(1)} %copy-done.7, ...), custom_call_target="tpu_custom_call", output_to_operand_aliasing={{0}: (13, {})} | custom-call | tf_op jit(solution)/shard_map/pallas_call | solution.py:318
  60.8 1.6 %collective-permute-start.7 = (bf16[2,384,256]{2,1,0:T(8,128)(2,1)S(1)}, bf16[2,384,256]{2,1,0:T(8,128)(2,1)S(1)}, u32[]{:S(2)}, u32[]{:S(2)}) collective-permute-start(bf16[2,384,256]{2,1,0:T(8,128)(2,1)S(1)} %get-tuple-element.51.refs_5_.refs_1_.refs_3_), channel_id=1, source_target_pairs={{0,96},{32,0},{64,32},{96,64},{1,97},{33,1},{65,33},{97,65},{2,98}... | collective-permute-start | bytes 1179656 | tf_op jit(solution)/shard_map/ppermute | solution.py:490
  62.5 1.1 %collective-permute-start.6 = (bf16[2,384,256]{2,1,0:T(8,128)(2,1)S(1)}, bf16[2,384,256]{2,1,0:T(8,128)(2,1)S(1)}, u32[]{:S(2)}, u32[]{:S(2)}) collective-permute-start(bf16[2,384,256]{2,1,0:T(8,128)(2,1)S(1)} %get-tuple-element.50.refs_4_.refs_0_.refs_2_), channel_id=1, source_target_pairs={{0,96},{32,0},{64,32},{96,64},{1,97},{33,1},{65,33},{97,65},{2,98}... | collective-permute-start | bytes 1179656 | tf_op jit(solution)/shard_map/ppermute | solution.py:490
  63.6 0.8 gather_stage.1
  64.5 6.8 %collective-permute-done.7.refs_3_.refs_5_ = bf16[2,384,256]{2,1,0:T(8,128)(2,1)S(1)} collective-permute-done((bf16[2,384,256]{2,1,0:T(8,128)(2,1)S(1)}, bf16[2,384,256]{2,1,0:T(8,128)(2,1)S(1)}, u32[]{:S(2)}, u32[]{:S(2)}) %collective-permute-start.7) | collective-permute-done | bytes 393248 | tf_op jit(solution)/shard_map/ppermute | solution.py:490
  71.3 8.4 %collective-permute-done.6.refs_2_.refs_4_ = bf16[2,384,256]{2,1,0:T(8,128)(2,1)S(1)} collective-permute-done((bf16[2,384,256]{2,1,0:T(8,128)(2,1)S(1)}, bf16[2,384,256]{2,1,0:T(8,128)(2,1)S(1)}, u32[]{:S(2)}, u32[]{:S(2)}) %collective-permute-start.6) | collective-permute-done | bytes 393248 | tf_op jit(solution)/shard_map/ppermute | solution.py:490
  79.7 2.3 %align_stage.1 = (f32[768,256]{1,0:T(8,128)S(1)}, bf16[768,256]{1,0:T(8,128)(2,1)S(1)}, f32[128,1,256]{2,1,0:T(1,128)S(1)}) custom-call(f32[128]{0:T(128)S(1)} %copy-done.6, f32[128]{0:T(128)S(1)} %copy-done.7, f32[768,256]{1,0:T(8,128)S(1)} %bitcast.9, f32[768,256]{1,0:T(8,128)S(1)} %get-tuple-element.55.total, ...), custom_call_target="tpu_custom_call" | custom-call | tf_op jit(solution)/shard_map/align_stage/pallas_call | solution.py:430
  82.0 3.0 %collective-permute-start.11 = (bf16[768,256]{1,0:T(8,128)(2,1)S(1)}, bf16[768,256]{1,0:T(8,128)(2,1)S(1)}, u32[]{:S(2)}, u32[]{:S(2)}) collective-permute-start(bf16[768,256]{1,0:T(8,128)(2,1)S(1)} %get-tuple-element.59), channel_id=1, source_target_pairs={{0,96},{32,0},{64,32},{96,64},{1,97},{33,1},{65,33},{97,65},{2,98}... | collective-permute-start | bytes 1179656 | tf_op jit(solution)/shard_map/ppermute | solution.py:490
  85.0 2.7 %collective-permute-start.8 = (bf16[768,256]{1,0:T(8,128)(2,1)S(1)}, bf16[768,256]{1,0:T(8,128)(2,1)S(1)}, u32[]{:S(2)}, u32[]{:S(2)}) collective-permute-start(bf16[768,256]{1,0:T(8,128)(2,1)S(1)} %get-tuple-element.59), channel_id=1, source_target_pairs={{0,1},{1,0},{2,3},{3,2},{4,5},{5,4},{6,7},{7,6},{8,9},{9,8},{10,11... | collective-permute-start | bytes 1179656 | tf_op jit(solution)/shard_map/ppermute | solution.py:479
  87.7 17.5 %all_to_all.5.refs_10_ = f32[128,1,256]{2,1,0:T(1,128)S(1)} all-to-all(f32[128,1,256]{2,1,0:T(1,128)S(1)} %get-tuple-element.60), channel_id=1, replica_groups=mesh['group'=4,'img'=32] {'group','img'}, dimensions={0} | all-to-all | bytes 262144 | tf_op jit(solution)/shard_map/all_to_all | solution.py:536
  105.2 1.4 %final_stage.1 = (f32[768,256]{1,0:T(8,128)}, f32[128]{0:T(128)}, f32[128]{0:T(128)}) custom-call(f32[768,256]{1,0:T(8,128)S(1)} %get-tuple-element.58.base, f32[768,256]{1,0:T(8,128)S(1)} %get-tuple-element.56.link_o.refs_0_, f32[768,256]{1,0:T(8,128)S(1)} %get-tuple-element.57.link_p.refs_1_, ...), custom_call_target="tpu_custom_call" | custom-call | tf_op jit(solution)/shard_map/final_stage/pallas_call | solution.py:464
  (30 shorter events, 0.1 us)
Async XLA Ops:
  0.6 10.7 %copy-start.4 = (bf16[768,768]{1,0:T(8,128)(2,1)S(1)}, bf16[768,768]{1,0:T(8,128)(2,1)}, u32[]{:S(2)}) copy-start(bf16[768,768]{1,0:T(8,128)(2,1)} %query_w.1) | copy-start | bytes 3538948
  0.6 10.7 %copy-start.5 = (bf16[768,768]{1,0:T(8,128)(2,1)S(1)}, bf16[768,768]{1,0:T(8,128)(2,1)}, u32[]{:S(2)}) copy-start(bf16[768,768]{1,0:T(8,128)(2,1)} %value_w.1) | copy-start | bytes 3538948
  0.7 10.7 %copy-start.9 = (f32[768]{0:T(1024)S(1)}, f32[768]{0:T(1024)}, u32[]{:S(2)}) copy-start(f32[768]{0:T(1024)} %gain.1) | copy-start | bytes 9220
  0.7 13.4 %copy-start.3 = (bf16[768,768]{1,0:T(8,128)(2,1)S(1)}, bf16[768,768]{1,0:T(8,128)(2,1)}, u32[]{:S(2)}) copy-start(bf16[768,768]{1,0:T(8,128)(2,1)} %refs_11_.5) | copy-start | bytes 3538948
  6.6 7.4 %collective-permute-start.2 = (bf16[768,768]{1,0:T(8,128)(2,1)S(1)}, bf16[768,768]{1,0:T(8,128)(2,1)S(1)}, u32[]{:S(2)}, u32[]{:S(2)}) collective-permute-start(bf16[768,768]{1,0:T(8,128)(2,1)S(1)} %get-tuple-element.37), channel_id=1, source_target_pairs={{0,1},{1,0},{2,3},{3,2},{4,5},{5,4},{6,7},{7,6},{8,9},{9,8},{10,11... | collective-permute-start | bytes 3538952 | tf_op jit(solution)/shard_map/ppermute | solution.py:479
  8.1 18.1 %collective-permute-start.1 = (bf16[768,768]{1,0:T(8,128)(2,1)S(1)}, bf16[768,768]{1,0:T(8,128)(2,1)S(1)}, u32[]{:S(2)}, u32[]{:S(2)}) collective-permute-start(bf16[768,768]{1,0:T(8,128)(2,1)S(1)} %get-tuple-element.37), channel_id=1, source_target_pairs={{1,2},{3,4},{5,6},{7,8},{9,10},{11,12},{13,14},{15,16},{17,18},{19... | collective-permute-start | bytes 3538952 | tf_op jit(solution)/shard_map/ppermute | solution.py:485
  9.5 37.1 %collective-permute-start = (bf16[768,768]{1,0:T(8,128)(2,1)S(1)}, bf16[768,768]{1,0:T(8,128)(2,1)S(1)}, u32[]{:S(2)}, u32[]{:S(2)}) collective-permute-start(bf16[768,768]{1,0:T(8,128)(2,1)S(1)} %get-tuple-element.37), channel_id=1, source_target_pairs={{0,32},{32,64},{64,96},{96,0},{1,33},{33,65},{65,97},{97,1},{2,34}... | collective-permute-start | bytes 3538952 | tf_op jit(solution)/shard_map/ppermute | solution.py:490
  11.4 2.7 %copy-start = (f32[1,768,256]{2,1,0:T(8,128)S(1)}, f32[1,768,256]{2,1,0:T(8,128)}, u32[]{:S(2)}) copy-start(f32[1,768,256]{2,1,0:T(8,128)} %param.27) | copy-start | bytes 2359300
  11.4 2.7 %copy-start.1 = (bf16[768,768]{1,0:T(8,128)(2,1)S(1)}, bf16[768,768]{1,0:T(8,128)(2,1)}, u32[]{:S(2)}) copy-start(bf16[768,768]{1,0:T(8,128)(2,1)} %refs_7_.7) | copy-start | bytes 3538948
  11.4 2.7 %copy-start.2 = (bf16[768,512]{1,0:T(8,128)(2,1)S(1)}, bf16[768,512]{1,0:T(8,128)(2,1)}, u32[]{:S(2)}) copy-start(bf16[768,512]{1,0:T(8,128)(2,1)} %refs_8_.7) | copy-start | bytes 2359300
  11.4 2.7 %copy-start.6 = (f32[128]{0:T(128)S(1)}, f32[128]{0:T(128)}, u32[]{:S(2)}) copy-start(f32[128]{0:T(128)} %scale.1) | copy-start | bytes 1540
  11.4 2.7 %copy-start.7 = (f32[128]{0:T(128)S(1)}, f32[128]{0:T(128)}, u32[]{:S(2)}) copy-start(f32[128]{0:T(128)} %focal.1) | copy-start | bytes 1540
  11.4 2.7 %copy-start.8 = (s32[4]{0:T(128)S(1)}, s32[4]{0:T(128)}, u32[]{:S(2)}) copy-start(s32[4]{0:T(128)} %refs_0_.7) | copy-start | bytes 52
  38.3 25.4 %collective-permute-start.3 = (bf16[3,768,256]{2,1,0:T(8,128)(2,1)S(1)}, bf16[3,768,256]{2,1,0:T(8,128)(2,1)S(1)}, u32[]{:S(2)}, u32[]{:S(2)}) collective-permute-start(bf16[3,768,256]{2,1,0:T(8,128)(2,1)S(1)} %get-tuple-element.52.refs_6_), channel_id=1, source_target_pairs={{1,2},{3,4},{5,6},{7,8},{9,10},{11,12},{13,14},{15,16},{17,18},{19... | collective-permute-start | bytes 3538952 | tf_op jit(solution)/shard_map/ppermute | solution.py:485
  39.0 24.7 %collective-permute-start.4 = (bf16[3,768,256]{2,1,0:T(8,128)(2,1)S(1)}, bf16[3,768,256]{2,1,0:T(8,128)(2,1)S(1)}, u32[]{:S(2)}, u32[]{:S(2)}) collective-permute-start(bf16[3,768,256]{2,1,0:T(8,128)(2,1)S(1)} %get-tuple-element.53.refs_8_), channel_id=1, source_target_pairs={{0,1},{1,0},{2,3},{3,2},{4,5},{5,4},{6,7},{7,6},{8,9},{9,8},{10,11... | collective-permute-start | bytes 3538952 | tf_op jit(solution)/shard_map/ppermute | solution.py:479
  45.3 18.3 %collective-permute-start.5 = (bf16[768,256]{1,0:T(8,128)(2,1)S(1)}, bf16[768,256]{1,0:T(8,128)(2,1)S(1)}, u32[]{:S(2)}, u32[]{:S(2)}) collective-permute-start(bf16[768,256]{1,0:T(8,128)(2,1)S(1)} %get-tuple-element.54), channel_id=1, source_target_pairs={{0,32},{32,64},{64,96},{96,0},{1,33},{33,65},{65,97},{97,1},{2,34}... | collective-permute-start | bytes 1179656 | tf_op jit(solution)/shard_map/ppermute | solution.py:490
  60.8 10.5 %collective-permute-start.7 = (bf16[2,384,256]{2,1,0:T(8,128)(2,1)S(1)}, bf16[2,384,256]{2,1,0:T(8,128)(2,1)S(1)}, u32[]{:S(2)}, u32[]{:S(2)}) collective-permute-start(bf16[2,384,256]{2,1,0:T(8,128)(2,1)S(1)} %get-tuple-element.51.refs_5_.refs_1_.refs_3_), channel_id=1, source_target_pairs={{0,96},{32,0},{64,32},{96,64},{1,97},{33,1},{65,33},{97,65},{2,98}... | collective-permute-start | bytes 1179656 | tf_op jit(solution)/shard_map/ppermute | solution.py:490
  62.5 17.2 %collective-permute-start.6 = (bf16[2,384,256]{2,1,0:T(8,128)(2,1)S(1)}, bf16[2,384,256]{2,1,0:T(8,128)(2,1)S(1)}, u32[]{:S(2)}, u32[]{:S(2)}) collective-permute-start(bf16[2,384,256]{2,1,0:T(8,128)(2,1)S(1)} %get-tuple-element.50.refs_4_.refs_0_.refs_2_), channel_id=1, source_target_pairs={{0,96},{32,0},{64,32},{96,64},{1,97},{33,1},{65,33},{97,65},{2,98}... | collective-permute-start | bytes 1179656 | tf_op jit(solution)/shard_map/ppermute | solution.py:490
  82.0 23.1 %collective-permute-start.11 = (bf16[768,256]{1,0:T(8,128)(2,1)S(1)}, bf16[768,256]{1,0:T(8,128)(2,1)S(1)}, u32[]{:S(2)}, u32[]{:S(2)}) collective-permute-start(bf16[768,256]{1,0:T(8,128)(2,1)S(1)} %get-tuple-element.59), channel_id=1, source_target_pairs={{0,96},{32,0},{64,32},{96,64},{1,97},{33,1},{65,33},{97,65},{2,98}... | collective-permute-start | bytes 1179656 | tf_op jit(solution)/shard_map/ppermute | solution.py:490
  85.0 20.2 %collective-permute-start.10 = (bf16[768,256]{1,0:T(8,128)(2,1)S(1)}, bf16[768,256]{1,0:T(8,128)(2,1)S(1)}, u32[]{:S(2)}, u32[]{:S(2)}) collective-permute-start(bf16[768,256]{1,0:T(8,128)(2,1)S(1)} %get-tuple-element.59), channel_id=1, source_target_pairs={{0,32},{32,64},{64,96},{96,0},{1,33},{33,65},{65,97},{97,1},{2,34}... | collective-permute-start | bytes 1179656 | tf_op jit(solution)/shard_map/ppermute | solution.py:490
  85.0 20.2 %collective-permute-start.9 = (bf16[768,256]{1,0:T(8,128)(2,1)S(1)}, bf16[768,256]{1,0:T(8,128)(2,1)S(1)}, u32[]{:S(2)}, u32[]{:S(2)}) collective-permute-start(bf16[768,256]{1,0:T(8,128)(2,1)S(1)} %get-tuple-element.59), channel_id=1, source_target_pairs={{1,2},{3,4},{5,6},{7,8},{9,10},{11,12},{13,14},{15,16},{17,18},{19... | collective-permute-start | bytes 1179656 | tf_op jit(solution)/shard_map/ppermute | solution.py:485
  85.0 20.2 %collective-permute-start.8 = (bf16[768,256]{1,0:T(8,128)(2,1)S(1)}, bf16[768,256]{1,0:T(8,128)(2,1)S(1)}, u32[]{:S(2)}, u32[]{:S(2)}) collective-permute-start(bf16[768,256]{1,0:T(8,128)(2,1)S(1)} %get-tuple-element.59), channel_id=1, source_target_pairs={{0,1},{1,0},{2,3},{3,2},{4,5},{5,4},{6,7},{7,6},{8,9},{9,8},{10,11... | collective-permute-start | bytes 1179656 | tf_op jit(solution)/shard_map/ppermute | solution.py:479

commit v5 on v4

--- a/solution.py
+++ b/solution.py
@@ -52,7 +52,7 @@
 
 
 def embed_kernel(enc, weight, bias, memory_gain, depth, embed, rows_out, late, *scratch):
-    enc_v, weight_v, depth_v, bias_v, gain_v, embed_v, rows_v, late_v, arrive, leave = scratch
+    enc_v, weight_v, depth_v, bias_v, gain_v, arrive = scratch
     tokens = embed.shape[0]
     count = 3
     rows = tokens // count
@@ -62,26 +62,22 @@
         moves.append(pltpu.make_async_copy(enc.at[part], enc_v.at[part], arrive.at[index + 1]))
     for place, pair in enumerate(((bias, bias_v), (memory_gain, gain_v), (depth, depth_v))):
         moves.append(pltpu.make_async_copy(*pair, arrive.at[count + 1 + place]))
-    for move in moves:
+    early = (moves[0], moves[1], moves[count + 1], moves[count + 2])
+    for move in early:
         move.start()
-    for move in (moves[0], moves[count + 1], moves[count + 2]):
+    moves[0].wait()
+    for move in (*moves[2 : count + 1], moves[-1]):
+        move.start()
+    for move in early[2:]:
         move.wait()
-    out = []
     for index in range(count):
         part = pl.ds(index * rows, rows)
         moves[index + 1].wait()
         value = (matmul(enc_v[part, :], weight_v[...]) + bias_v[...][None, :]).astype(BF16)
-        embed_v[part, :] = value
-        rows_v[part, :] = normed(value, gain_v[...][None, :])
-        for place, (source, target) in enumerate(((rows_v, rows_out), (embed_v, embed))):
-            out.append(pltpu.make_async_copy(source.at[part], target.at[part], leave.at[index * 2 + place]))
-            out[-1].start()
+        embed[part, :] = value
+        rows_out[part, :] = normed(value, gain_v[...][None, :])
     moves[-1].wait()
-    late_v[...] = depth_v[...].astype(BF16)
-    out.append(pltpu.make_async_copy(late_v, late, leave.at[count * 2]))
-    out[-1].start()
-    for move in out:
-        move.wait()
+    late[...] = depth_v[...].astype(BF16)
 
 
 def embed_stage(enc, weight, bias, memory_gain, depth):
@@ -91,7 +87,7 @@
     return pl.pallas_call(
         embed_kernel,
         in_specs=[HBM] * 5,
-        out_specs=(HBM,) * 3,
+        out_specs=(VMEM,) * 3,
         out_shape=tuple(jax.ShapeDtypeStruct(shape, BF16) for shape in shapes),
         scratch_shapes=[
             pltpu.VMEM(enc.shape, BF16),
@@ -99,8 +95,6 @@
             pltpu.VMEM(depth.shape, F32),
             pltpu.VMEM(bias.shape, F32),
             pltpu.VMEM(bias.shape, F32),
-            *[pltpu.VMEM(shape, BF16) for shape in shapes],
-            pltpu.SemaphoreType.DMA((7,)),
             pltpu.SemaphoreType.DMA((7,)),
         ],
         compiler_params=params(),
@@ -221,7 +215,7 @@
     def clear(slot):
         return pltpu.make_async_copy(zeros, pair_tokens.at[slot], sems.at[slot])
 
-    rows = 256 if count % 256 == 0 else 128
+    rows = 384
 
     def write(slot, start):
         place = pair_tokens.at[slot, pl.ds(first + start, rows)]

time: 107 us -> 105 us (0.981)
  Pallas kernels: 51.5 us -> 49.9 us
    pallas_call x1, Pallas kernels: 5.95 us -> 4.72 us  [embed_stage(): pl.pallas_call(embed_kernel, in_specs=[HBM] * 5, out_specs=(VMEM,) * 3, o...]
where the time goes in v5:
time: 105 us
  Pallas kernels  49.9 us (48%)
  starting transfers between devices  20.9 us (20%)
  blocking collectives  17.6 us (17%)
  waiting for transfers between devices  15.3 us (15%)
  between operations  1.54 us (1%)
    pallas_call x4, Pallas kernels, pair_stage(): pl.pallas_call(body, in_specs=specs, out_specs=(HBM,) + (VMEM,) * (len(re...  38 us
    all_to_all x1, blocking collectives, local(): poses = lax.all_to_all(poses, ('group', 'img'), 0, 0, tiled=True)  17.6 us
    ppermute x6, waiting for transfers between devices, along(): lax.ppermute(value, 'group', [(i, (i + by) % count) for i in range(count)])  15.3 us
    ppermute x3, starting transfers between devices, swap_inner(): lax.ppermute(value, 'img', [(i, i ^ 1) for i in range(lax.axis_size('img'...  10.2 us
    ppermute x6, starting transfers between devices, along(): lax.ppermute(value, 'group', [(i, (i + by) % count) for i in range(count)])  8.71 us
    pallas_call x1, Pallas kernels, embed_stage(): pl.pallas_call(embed_kernel, in_specs=[HBM] * 5, out_specs=(VMEM,) * 3, o...  4.72 us
    pallas_call x1, Pallas kernels, query_stage(): pl.pallas_call(query_kernel, in_specs=[VMEM] * 4, out_specs=(VMEM,) * 3,...  2.6 us
    pallas_call x1, Pallas kernels, align_stage(): pl.pallas_call(align_kernel, in_specs=[SMEM, SMEM] + [VMEM] * (len(arrays...  2.32 us
  transfers between devices with their start and end apart: 12, of which 2 were waited for; matrix products, arithmetic and copies ran while one was open for 0% of the time, Pallas kernels for 39%

profile of v5, /device:TPU:1, one launch (start us, length us, event | category | flops | bytes accessed | tf_op | source)
XLA Modules:
  0.0 105.3 jit_solution(8090533967825838680)
XLA Ops:
  0.7 4.7 %embed_stage.1 = (bf16[768,768]{1,0:T(8,128)(2,1)S(1)}, bf16[768,768]{1,0:T(8,128)(2,1)S(1)}, bf16[768,256]{1,0:T(8,128)(2,1)S(1)}) custom-call(bf16[768,1024]{1,0:T(8,128)(2,1)} %bitcast.10, bf16[1024,768]{1,0:T(8,128)(2,1)} %weight.1, f32[768]{0:T(1024)} %bias.1, f32[768]{0:T(1024)} %memory_gain.1, f32[768,256]{1,0:T(8,128)} %bitcast.3), custom_call_target="tpu_custom_call" | custom-call | tf_op jit(solution)/shard_map/embed_stage/pallas_call | solution.py:87
  5.4 1.5 %collective-permute-start.2 = (bf16[768,768]{1,0:T(8,128)(2,1)S(1)}, bf16[768,768]{1,0:T(8,128)(2,1)S(1)}, u32[]{:S(2)}, u32[]{:S(2)}) collective-permute-start(bf16[768,768]{1,0:T(8,128)(2,1)S(1)} %get-tuple-element.37), channel_id=1, source_target_pairs={{0,1},{1,0},{2,3},{3,2},{4,5},{5,4},{6,7},{7,6},{8,9},{9,8},{10,11... | collective-permute-start | bytes 3538952 | tf_op jit(solution)/shard_map/ppermute | solution.py:473
  6.9 1.4 %collective-permute-start.1 = (bf16[768,768]{1,0:T(8,128)(2,1)S(1)}, bf16[768,768]{1,0:T(8,128)(2,1)S(1)}, u32[]{:S(2)}, u32[]{:S(2)}) collective-permute-start(bf16[768,768]{1,0:T(8,128)(2,1)S(1)} %get-tuple-element.37), channel_id=1, source_target_pairs={{1,2},{3,4},{5,6},{7,8},{9,10},{11,12},{13,14},{15,16},{17,18},{19... | collective-permute-start | bytes 3538952 | tf_op jit(solution)/shard_map/ppermute | solution.py:479
  8.3 1.2 %collective-permute-start = (bf16[768,768]{1,0:T(8,128)(2,1)S(1)}, bf16[768,768]{1,0:T(8,128)(2,1)S(1)}, u32[]{:S(2)}, u32[]{:S(2)}) collective-permute-start(bf16[768,768]{1,0:T(8,128)(2,1)S(1)} %get-tuple-element.37), channel_id=1, source_target_pairs={{0,32},{32,64},{64,96},{96,0},{1,33},{33,65},{65,97},{97,1},{2,34}... | collective-permute-start | bytes 3538952 | tf_op jit(solution)/shard_map/ppermute | solution.py:484
  10.2 0.0 copy-start
  10.2 0.0 copy-start.6
  10.2 2.6 %query_stage.1 = (bf16[768,768]{1,0:T(8,128)(2,1)S(1)}, bf16[768,768]{1,0:T(8,128)(2,1)S(1)}, f32[8,128]{1,0:T(8,128)S(1)}) custom-call(bf16[768,768]{1,0:T(8,128)(2,1)S(1)} %get-tuple-element.34.embed.refs_6_, f32[768]{0:T(1024)S(1)} %copy-done.9, bf16[768,768]{1,0:T(8,128)(2,1)S(1)} %copy-done.4, bf16[768,768]{1,0:T(8,128)(2,1)S(1)} %copy-done.5), custom_call_target="tpu_custom_call" | custom-call | tf_op jit(solution)/shard_map/query_stage/pallas_call | solution.py:122
  12.9 12.1 %shard_map.174 = (bf16[4,768,768]{2,1,0:T(8,128)(2,1)}, bf16[3,768,256]{2,1,0:T(8,128)(2,1)S(1)}, f32[768,256]{1,0:T(8,128)S(1)}) custom-call(s32[4]{0:T(128)S(1)} %copy-done.8, s32[1]{0:T(128)S(6)} %copy.25.refs_1_, f32[128]{0:T(128)S(1)} %copy-done.6, f32[128]{0:T(128)S(1)} %copy-done.7, bf16[768,768]{1,0:T(8,128)(2,1)S(1)} %get-tuple-element.35.refs_4_, ...), custom_call_target="tpu_custom_call" | custom-call | tf_op jit(solution)/shard_map/pallas_call | solution.py:312
  25.0 12.1 %shard_map.175 = (bf16[4,768,768]{2,1,0:T(8,128)(2,1)}, bf16[3,768,256]{2,1,0:T(8,128)(2,1)S(1)}, f32[768,256]{1,0:T(8,128)S(1)}) custom-call(s32[4]{0:T(128)S(1)} %copy-done.8, s32[1]{0:T(128)S(6)} %copy.25.refs_1_, f32[128]{0:T(128)S(1)} %copy-done.6, f32[128]{0:T(128)S(1)} %copy-done.7, ...), custom_call_target="tpu_custom_call", output_to_operand_aliasing={{0}: (13, {})} | custom-call | tf_op jit(solution)/shard_map/pallas_call | solution.py:312
  37.1 0.6 collective-permute-start.3
  37.7 6.4 %collective-permute-start.4 = (bf16[3,768,256]{2,1,0:T(8,128)(2,1)S(1)}, bf16[3,768,256]{2,1,0:T(8,128)(2,1)S(1)}, u32[]{:S(2)}, u32[]{:S(2)}) collective-permute-start(bf16[3,768,256]{2,1,0:T(8,128)(2,1)S(1)} %get-tuple-element.53.refs_8_), channel_id=1, source_target_pairs={{0,1},{1,0},{2,3},{3,2},{4,5},{5,4},{6,7},{7,6},{8,9},{9,8},{10,11... | collective-permute-start | bytes 3538952 | tf_op jit(solution)/shard_map/ppermute | solution.py:473
  44.2 1.2 %collective-permute-start.5 = (bf16[768,256]{1,0:T(8,128)(2,1)S(1)}, bf16[768,256]{1,0:T(8,128)(2,1)S(1)}, u32[]{:S(2)}, u32[]{:S(2)}) collective-permute-start(bf16[768,256]{1,0:T(8,128)(2,1)S(1)} %get-tuple-element.54), channel_id=1, source_target_pairs={{0,32},{32,64},{64,96},{96,0},{1,33},{33,65},{65,97},{97,1},{2,34}... | collective-permute-start | bytes 1179656 | tf_op jit(solution)/shard_map/ppermute | solution.py:484
  45.4 8.2 %shard_map.176 = (bf16[4,768,768]{2,1,0:T(8,128)(2,1)}, bf16[2,384,256]{2,1,0:T(8,128)(2,1)S(1)}, f32[384,256]{1,0:T(8,128)S(1)}, bf16[768,768]{1,0:T(8,128)(2,1...) custom-call(s32[4]{0:T(128)S(1)} %copy-done.8, s32[1]{0:T(128)S(6)} %copy.25.refs_1_, ...), custom_call_target="tpu_custom_call", output_to_operand_aliasing={{0}: (13, {})} | custom-call | tf_op jit(solution)/shard_map/pallas_call | solution.py:312
  53.6 5.6 %shard_map.177 = (bf16[4,768,768]{2,1,0:T(8,128)(2,1)}, bf16[2,384,256]{2,1,0:T(8,128)(2,1)S(1)}, f32[384,256]{1,0:T(8,128)S(1)}) custom-call(s32[4]{0:T(128)S(1)} %copy-done.8, s32[1]{0:T(128)S(6)} %copy.25.refs_1_, f32[128]{0:T(128)S(1)} %copy-done.6, f32[128]{0:T(128)S(1)} %copy-done.7, ...), custom_call_target="tpu_custom_call", output_to_operand_aliasing={{0}: (13, {})} | custom-call | tf_op jit(solution)/shard_map/pallas_call | solution.py:312
  59.2 1.9 %collective-permute-start.7 = (bf16[2,384,256]{2,1,0:T(8,128)(2,1)S(1)}, bf16[2,384,256]{2,1,0:T(8,128)(2,1)S(1)}, u32[]{:S(2)}, u32[]{:S(2)}) collective-permute-start(bf16[2,384,256]{2,1,0:T(8,128)(2,1)S(1)} %get-tuple-element.51.refs_5_.refs_1_.refs_3_), channel_id=1, source_target_pairs={{0,96},{32,0},{64,32},{96,64},{1,97},{33,1},{65,33},{97,65},{2,98}... | collective-permute-start | bytes 1179656 | tf_op jit(solution)/shard_map/ppermute | solution.py:484
  61.2 0.9 collective-permute-start.6
  62.0 0.8 gather_stage.1
  62.9 6.8 %collective-permute-done.7.refs_3_.refs_5_ = bf16[2,384,256]{2,1,0:T(8,128)(2,1)S(1)} collective-permute-done((bf16[2,384,256]{2,1,0:T(8,128)(2,1)S(1)}, bf16[2,384,256]{2,1,0:T(8,128)(2,1)S(1)}, u32[]{:S(2)}, u32[]{:S(2)}) %collective-permute-start.7) | collective-permute-done | bytes 393248 | tf_op jit(solution)/shard_map/ppermute | solution.py:484
  69.7 8.4 %collective-permute-done.6.refs_2_.refs_4_ = bf16[2,384,256]{2,1,0:T(8,128)(2,1)S(1)} collective-permute-done((bf16[2,384,256]{2,1,0:T(8,128)(2,1)S(1)}, bf16[2,384,256]{2,1,0:T(8,128)(2,1)S(1)}, u32[]{:S(2)}, u32[]{:S(2)}) %collective-permute-start.6) | collective-permute-done | bytes 393248 | tf_op jit(solution)/shard_map/ppermute | solution.py:484
  78.2 2.3 %align_stage.1 = (f32[768,256]{1,0:T(8,128)S(1)}, bf16[768,256]{1,0:T(8,128)(2,1)S(1)}, f32[128,1,256]{2,1,0:T(1,128)S(1)}) custom-call(f32[128]{0:T(128)S(1)} %copy-done.6, f32[128]{0:T(128)S(1)} %copy-done.7, f32[768,256]{1,0:T(8,128)S(1)} %bitcast.9, f32[768,256]{1,0:T(8,128)S(1)} %get-tuple-element.55.total, ...), custom_call_target="tpu_custom_call" | custom-call | tf_op jit(solution)/shard_map/align_stage/pallas_call | solution.py:424
  80.5 3.5 %collective-permute-start.11 = (bf16[768,256]{1,0:T(8,128)(2,1)S(1)}, bf16[768,256]{1,0:T(8,128)(2,1)S(1)}, u32[]{:S(2)}, u32[]{:S(2)}) collective-permute-start(bf16[768,256]{1,0:T(8,128)(2,1)S(1)} %get-tuple-element.59), channel_id=1, source_target_pairs={{0,96},{32,0},{64,32},{96,64},{1,97},{33,1},{65,33},{97,65},{2,98}... | collective-permute-start | bytes 1179656 | tf_op jit(solution)/shard_map/ppermute | solution.py:484
  84.0 2.3 %collective-permute-start.8 = (bf16[768,256]{1,0:T(8,128)(2,1)S(1)}, bf16[768,256]{1,0:T(8,128)(2,1)S(1)}, u32[]{:S(2)}, u32[]{:S(2)}) collective-permute-start(bf16[768,256]{1,0:T(8,128)(2,1)S(1)} %get-tuple-element.59), channel_id=1, source_target_pairs={{0,1},{1,0},{2,3},{3,2},{4,5},{5,4},{6,7},{7,6},{8,9},{9,8},{10,11... | collective-permute-start | bytes 1179656 | tf_op jit(solution)/shard_map/ppermute | solution.py:473
  86.2 17.6 %all_to_all.5.refs_10_ = f32[128,1,256]{2,1,0:T(1,128)S(1)} all-to-all(f32[128,1,256]{2,1,0:T(1,128)S(1)} %get-tuple-element.60), channel_id=1, replica_groups=mesh['group'=4,'img'=32] {'group','img'}, dimensions={0} | all-to-all | bytes 262144 | tf_op jit(solution)/shard_map/all_to_all | solution.py:530
  103.9 1.4 %final_stage.1 = (f32[768,256]{1,0:T(8,128)}, f32[128]{0:T(128)}, f32[128]{0:T(128)}) custom-call(f32[768,256]{1,0:T(8,128)S(1)} %get-tuple-element.58.base, f32[768,256]{1,0:T(8,128)S(1)} %get-tuple-element.56.link_o.refs_0_, f32[768,256]{1,0:T(8,128)S(1)} %get-tuple-element.57.link_p.refs_1_, ...), custom_call_target="tpu_custom_call" | custom-call | tf_op jit(solution)/shard_map/final_stage/pallas_call | solution.py:458
  (30 shorter events, 0.1 us)
Async XLA Ops:
  0.6 9.5 %copy-start.4 = (bf16[768,768]{1,0:T(8,128)(2,1)S(1)}, bf16[768,768]{1,0:T(8,128)(2,1)}, u32[]{:S(2)}) copy-start(bf16[768,768]{1,0:T(8,128)(2,1)} %query_w.1) | copy-start | bytes 3538948
  0.6 9.5 %copy-start.5 = (bf16[768,768]{1,0:T(8,128)(2,1)S(1)}, bf16[768,768]{1,0:T(8,128)(2,1)}, u32[]{:S(2)}) copy-start(bf16[768,768]{1,0:T(8,128)(2,1)} %value_w.1) | copy-start | bytes 3538948
  0.7 9.5 %copy-start.9 = (f32[768]{0:T(1024)S(1)}, f32[768]{0:T(1024)}, u32[]{:S(2)}) copy-start(f32[768]{0:T(1024)} %gain.1) | copy-start | bytes 9220
  0.7 12.2 %copy-start.3 = (bf16[768,768]{1,0:T(8,128)(2,1)S(1)}, bf16[768,768]{1,0:T(8,128)(2,1)}, u32[]{:S(2)}) copy-start(bf16[768,768]{1,0:T(8,128)(2,1)} %refs_11_.5) | copy-start | bytes 3538948
  5.4 7.4 %collective-permute-start.2 = (bf16[768,768]{1,0:T(8,128)(2,1)S(1)}, bf16[768,768]{1,0:T(8,128)(2,1)S(1)}, u32[]{:S(2)}, u32[]{:S(2)}) collective-permute-start(bf16[768,768]{1,0:T(8,128)(2,1)S(1)} %get-tuple-element.37), channel_id=1, source_target_pairs={{0,1},{1,0},{2,3},{3,2},{4,5},{5,4},{6,7},{7,6},{8,9},{9,8},{10,11... | collective-permute-start | bytes 3538952 | tf_op jit(solution)/shard_map/ppermute | solution.py:473
  6.9 18.1 %collective-permute-start.1 = (bf16[768,768]{1,0:T(8,128)(2,1)S(1)}, bf16[768,768]{1,0:T(8,128)(2,1)S(1)}, u32[]{:S(2)}, u32[]{:S(2)}) collective-permute-start(bf16[768,768]{1,0:T(8,128)(2,1)S(1)} %get-tuple-element.37), channel_id=1, source_target_pairs={{1,2},{3,4},{5,6},{7,8},{9,10},{11,12},{13,14},{15,16},{17,18},{19... | collective-permute-start | bytes 3538952 | tf_op jit(solution)/shard_map/ppermute | solution.py:479
  8.3 37.1 %collective-permute-start = (bf16[768,768]{1,0:T(8,128)(2,1)S(1)}, bf16[768,768]{1,0:T(8,128)(2,1)S(1)}, u32[]{:S(2)}, u32[]{:S(2)}) collective-permute-start(bf16[768,768]{1,0:T(8,128)(2,1)S(1)} %get-tuple-element.37), channel_id=1, source_target_pairs={{0,32},{32,64},{64,96},{96,0},{1,33},{33,65},{65,97},{97,1},{2,34}... | collective-permute-start | bytes 3538952 | tf_op jit(solution)/shard_map/ppermute | solution.py:484
  10.2 2.7 %copy-start = (f32[1,768,256]{2,1,0:T(8,128)S(1)}, f32[1,768,256]{2,1,0:T(8,128)}, u32[]{:S(2)}) copy-start(f32[1,768,256]{2,1,0:T(8,128)} %param.27) | copy-start | bytes 2359300
  10.2 2.7 %copy-start.1 = (bf16[768,768]{1,0:T(8,128)(2,1)S(1)}, bf16[768,768]{1,0:T(8,128)(2,1)}, u32[]{:S(2)}) copy-start(bf16[768,768]{1,0:T(8,128)(2,1)} %refs_7_.7) | copy-start | bytes 3538948
  10.2 2.7 %copy-start.2 = (bf16[768,512]{1,0:T(8,128)(2,1)S(1)}, bf16[768,512]{1,0:T(8,128)(2,1)}, u32[]{:S(2)}) copy-start(bf16[768,512]{1,0:T(8,128)(2,1)} %refs_8_.7) | copy-start | bytes 2359300
  10.2 2.7 %copy-start.6 = (f32[128]{0:T(128)S(1)}, f32[128]{0:T(128)}, u32[]{:S(2)}) copy-start(f32[128]{0:T(128)} %scale.1) | copy-start | bytes 1540
  10.2 2.7 %copy-start.7 = (f32[128]{0:T(128)S(1)}, f32[128]{0:T(128)}, u32[]{:S(2)}) copy-start(f32[128]{0:T(128)} %focal.1) | copy-start | bytes 1540
  10.2 2.7 %copy-start.8 = (s32[4]{0:T(128)S(1)}, s32[4]{0:T(128)}, u32[]{:S(2)}) copy-start(s32[4]{0:T(128)} %refs_0_.7) | copy-start | bytes 52
  37.1 24.9 %collective-permute-start.3 = (bf16[3,768,256]{2,1,0:T(8,128)(2,1)S(1)}, bf16[3,768,256]{2,1,0:T(8,128)(2,1)S(1)}, u32[]{:S(2)}, u32[]{:S(2)}) collective-permute-start(bf16[3,768,256]{2,1,0:T(8,128)(2,1)S(1)} %get-tuple-element.52.refs_6_), channel_id=1, source_target_pairs={{1,2},{3,4},{5,6},{7,8},{9,10},{11,12},{13,14},{15,16},{17,18},{19... | collective-permute-start | bytes 3538952 | tf_op jit(solution)/shard_map/ppermute | solution.py:479
  37.7 24.3 %collective-permute-start.4 = (bf16[3,768,256]{2,1,0:T(8,128)(2,1)S(1)}, bf16[3,768,256]{2,1,0:T(8,128)(2,1)S(1)}, u32[]{:S(2)}, u32[]{:S(2)}) collective-permute-start(bf16[3,768,256]{2,1,0:T(8,128)(2,1)S(1)} %get-tuple-element.53.refs_8_), channel_id=1, source_target_pairs={{0,1},{1,0},{2,3},{3,2},{4,5},{5,4},{6,7},{7,6},{8,9},{9,8},{10,11... | collective-permute-start | bytes 3538952 | tf_op jit(solution)/shard_map/ppermute | solution.py:473
  44.2 17.9 %collective-permute-start.5 = (bf16[768,256]{1,0:T(8,128)(2,1)S(1)}, bf16[768,256]{1,0:T(8,128)(2,1)S(1)}, u32[]{:S(2)}, u32[]{:S(2)}) collective-permute-start(bf16[768,256]{1,0:T(8,128)(2,1)S(1)} %get-tuple-element.54), channel_id=1, source_target_pairs={{0,32},{32,64},{64,96},{96,0},{1,33},{33,65},{65,97},{97,1},{2,34}... | collective-permute-start | bytes 1179656 | tf_op jit(solution)/shard_map/ppermute | solution.py:484
  59.2 10.5 %collective-permute-start.7 = (bf16[2,384,256]{2,1,0:T(8,128)(2,1)S(1)}, bf16[2,384,256]{2,1,0:T(8,128)(2,1)S(1)}, u32[]{:S(2)}, u32[]{:S(2)}) collective-permute-start(bf16[2,384,256]{2,1,0:T(8,128)(2,1)S(1)} %get-tuple-element.51.refs_5_.refs_1_.refs_3_), channel_id=1, source_target_pairs={{0,96},{32,0},{64,32},{96,64},{1,97},{33,1},{65,33},{97,65},{2,98}... | collective-permute-start | bytes 1179656 | tf_op jit(solution)/shard_map/ppermute | solution.py:484
  61.2 17.0 %collective-permute-start.6 = (bf16[2,384,256]{2,1,0:T(8,128)(2,1)S(1)}, bf16[2,384,256]{2,1,0:T(8,128)(2,1)S(1)}, u32[]{:S(2)}, u32[]{:S(2)}) collective-permute-start(bf16[2,384,256]{2,1,0:T(8,128)(2,1)S(1)} %get-tuple-element.50.refs_4_.refs_0_.refs_2_), channel_id=1, source_target_pairs={{0,96},{32,0},{64,32},{96,64},{1,97},{33,1},{65,33},{97,65},{2,98}... | collective-permute-start | bytes 1179656 | tf_op jit(solution)/shard_map/ppermute | solution.py:484
  80.5 23.4 %collective-permute-start.11 = (bf16[768,256]{1,0:T(8,128)(2,1)S(1)}, bf16[768,256]{1,0:T(8,128)(2,1)S(1)}, u32[]{:S(2)}, u32[]{:S(2)}) collective-permute-start(bf16[768,256]{1,0:T(8,128)(2,1)S(1)} %get-tuple-element.59), channel_id=1, source_target_pairs={{0,96},{32,0},{64,32},{96,64},{1,97},{33,1},{65,33},{97,65},{2,98}... | collective-permute-start | bytes 1179656 | tf_op jit(solution)/shard_map/ppermute | solution.py:484
  84.0 19.9 %collective-permute-start.10 = (bf16[768,256]{1,0:T(8,128)(2,1)S(1)}, bf16[768,256]{1,0:T(8,128)(2,1)S(1)}, u32[]{:S(2)}, u32[]{:S(2)}) collective-permute-start(bf16[768,256]{1,0:T(8,128)(2,1)S(1)} %get-tuple-element.59), channel_id=1, source_target_pairs={{0,32},{32,64},{64,96},{96,0},{1,33},{33,65},{65,97},{97,1},{2,34}... | collective-permute-start | bytes 1179656 | tf_op jit(solution)/shard_map/ppermute | solution.py:484
  84.0 19.9 %collective-permute-start.9 = (bf16[768,256]{1,0:T(8,128)(2,1)S(1)}, bf16[768,256]{1,0:T(8,128)(2,1)S(1)}, u32[]{:S(2)}, u32[]{:S(2)}) collective-permute-start(bf16[768,256]{1,0:T(8,128)(2,1)S(1)} %get-tuple-element.59), channel_id=1, source_target_pairs={{1,2},{3,4},{5,6},{7,8},{9,10},{11,12},{13,14},{15,16},{17,18},{19... | collective-permute-start | bytes 1179656 | tf_op jit(solution)/shard_map/ppermute | solution.py:479
  84.0 19.9 %collective-permute-start.8 = (bf16[768,256]{1,0:T(8,128)(2,1)S(1)}, bf16[768,256]{1,0:T(8,128)(2,1)S(1)}, u32[]{:S(2)}, u32[]{:S(2)}) collective-permute-start(bf16[768,256]{1,0:T(8,128)(2,1)S(1)} %get-tuple-element.59), channel_id=1, source_target_pairs={{0,1},{1,0},{2,3},{3,2},{4,5},{5,4},{6,7},{7,6},{8,9},{9,8},{10,11... | collective-permute-start | bytes 1179656 | tf_op jit(solution)/shard_map/ppermute | solution.py:473
